TPU v7x, 128 devices: a whole 4x4x4 slice. The times are simulated.
128 devices in a mesh: dp: 16 (over z, x), mp: 8 (over y, core).
Axes of the slice: x: 4, y: 4, z: 4, core: 2. Of those that a mesh axis runs over, the one named last changes fastest.
Arguments:
- tokens: bfloat16 [6144, 8192], P('dp', 'mp'), may hold values from -6 to 6
- cotangent: bfloat16 [6144, 8192], P('dp', 'mp'), may hold values from -6 to 6
- seq_right: bfloat16 [48, 128, 128], P('dp'), may hold values from -0.5 to 0.5
- seq_left: bfloat16 [128, 48, 48], P('dp'), may hold values from -0.875 to 0.875
- seq_gain: float32 [8192], P('mp'), may hold values from 0.5 to 2
- right_one: bfloat16 [64, 512, 128], P('mp'), may hold values from -0.5 to 0.5
- left_one: bfloat16 [512, 64, 64], P('mp'), may hold values from -0.75 to 0.75
- left_two: bfloat16 [512, 64, 64], P('mp'), may hold values from -0.75 to 0.75
- right_two: bfloat16 [64, 128, 512], P('mp'), may hold values from -0.25 to 0.25
Outputs:
- output: bfloat16 [6144, 8192], P('dp', 'mp')
- grad_tokens: bfloat16 [6144, 8192], P('dp', 'mp')
- grad_seq_right: float32 [48, 128, 128], P('dp')
- grad_seq_left: float32 [128, 48, 48], P('dp')
- grad_gain: float32 [8192], P('mp')
- grad_right_one: float32 [64, 512, 128], P('mp')
- grad_left_one: float32 [512, 64, 64], P('mp')
- grad_left_two: float32 [512, 64, 64], P('mp')
- grad_right_two: float32 [64, 128, 512], P('mp')
All inputs are finite; a program needn't handle non-finite values.
Results may differ from a plain program's by a relative error of at most 0.01.
Values may be sent and summed in bfloat16 or wider, within the bound.
No kernel may reach another device: no remote copies, remote signals or barrier semaphores. Data moves between devices by JAX's collectives and lax.ppermute only.
A program may use at most 128 MiB of HBM per device.

v0:
```python
import math

import jax
import jax.numpy as jnp
from jax import lax
from jax.sharding import PartitionSpec as P


def gelu_value(value):
    return value * 0.5 * (1.0 + jax.scipy.special.erf(value / math.sqrt(2.0)))


def gelu_slope(value):
    cdf_part = 0.5 * (1.0 + jax.scipy.special.erf(value / math.sqrt(2.0)))
    return cdf_part + value * jnp.exp(-0.5 * value * value) / math.sqrt(2.0 * math.pi)


def product(form, left_arg, right_arg):
    return jnp.einsum(form, left_arg, right_arg, preferred_element_type=jnp.float32)


def per_device(
    tokens, cotangent, seq_right, seq_left, seq_gain, right_one, left_one, left_two, right_two
):
    rows_here, cols_here = tokens.shape
    block_len = seq_right.shape[1]
    blocks_here = rows_here // block_len
    feat_blocks = right_one.shape[0]
    feat_size = right_one.shape[2]
    seq_view = tokens.reshape(blocks_here, block_len, cols_here)
    first = product("sij,sjc->sic", seq_right, seq_view).astype(jnp.bfloat16)
    first_moved = lax.all_to_all(first, "dp", split_axis=1, concat_axis=0, tiled=True)
    mixed_moved = product("isk,kic->sic", seq_left, first_moved).astype(jnp.bfloat16)
    mixed = lax.all_to_all(mixed_moved, "dp", split_axis=0, concat_axis=1, tiled=True)
    blend = (seq_view.astype(jnp.float32) + seq_gain * mixed.astype(jnp.float32)).astype(
        jnp.bfloat16
    )
    zview = blend.reshape(rows_here, feat_blocks, feat_size)
    scale_rows = float(rows_here * lax.axis_size("dp")) ** (-0.5)
    scale_cols = float(cols_here * lax.axis_size("mp")) ** (-0.5)
    gview = cotangent.reshape(rows_here, feat_blocks, feat_size)
    back_c = product("bij,tbi->bjt", right_two, gview).astype(jnp.bfloat16)
    act_a = product("bij,tbj->bit", right_one, zview).astype(jnp.bfloat16)
    act_a_moved = lax.all_to_all(act_a, "mp", split_axis=1, concat_axis=0, tiled=True)
    pre = product("ibk,kit->bit", left_one, act_a_moved)
    hidden = gelu_value(pre).astype(jnp.bfloat16)
    act_c_moved = product("ibk,kit->bit", left_two, hidden).astype(jnp.bfloat16)
    act_c = lax.all_to_all(act_c_moved, "mp", split_axis=0, concat_axis=1, tiled=True)
    back_c_moved = lax.all_to_all(back_c, "mp", split_axis=1, concat_axis=0, tiled=True)
    back_h = product("ibk,bit->kit", left_two, back_c_moved)
    back_pre = (back_h * gelu_slope(pre)).astype(jnp.bfloat16)
    part_l2 = product("bit,kit->ibk", back_c_moved, hidden)
    back_a_moved = product("ibk,bit->kit", left_one, back_pre).astype(jnp.bfloat16)
    part_l1 = product("bit,kit->ibk", back_pre, act_a_moved)
    sum_l2 = lax.psum(part_l2, "dp")
    sum_l1 = lax.psum(part_l1, "dp")
    back_a = lax.all_to_all(back_a_moved, "mp", split_axis=0, concat_axis=1, tiled=True)
    last = product("bij,bjt->tbi", right_two, act_c)
    output = (zview.astype(jnp.float32) + last).astype(jnp.bfloat16).reshape(rows_here, cols_here)
    part_r2 = product("tbi,bjt->bij", gview, act_c)
    sum_r2 = lax.psum(part_r2, "dp")
    back_zz = product("bij,bit->tbj", right_one, back_a)
    part_r1 = product("bit,tbj->bij", back_a, zview)
    back_z = (gview.astype(jnp.float32) + back_zz).reshape(blocks_here, block_len, cols_here)
    part_gain = jnp.sum(back_z * mixed.astype(jnp.float32), axis=(0, 1))
    sum_r1, sum_gain = lax.psum((part_r1, part_gain), "dp")
    back_mixed = (back_z * seq_gain).astype(jnp.bfloat16)
    back_mixed_moved = lax.all_to_all(back_mixed, "dp", split_axis=1, concat_axis=0, tiled=True)
    back_first_moved = product("isk,sic->kic", seq_left, back_mixed_moved).astype(jnp.bfloat16)
    part_seq_left = product("sic,kic->isk", back_mixed_moved, first_moved)
    back_first = lax.all_to_all(back_first_moved, "dp", split_axis=0, concat_axis=1, tiled=True)
    grad_tokens = (back_z + product("sij,sic->sjc", seq_right, back_first)).astype(jnp.bfloat16)
    part_seq_right = product("sic,sjc->sij", back_first, seq_view)
    sum_seq_right, sum_seq_left = lax.psum((part_seq_right, part_seq_left), "mp")
    return (
        output,
        grad_tokens.reshape(rows_here, cols_here),
        sum_seq_right * scale_cols,
        sum_seq_left * scale_cols,
        sum_gain * scale_rows,
        sum_r1 * scale_rows,
        sum_l1 * scale_rows,
        sum_l2 * scale_rows,
        sum_r2 * scale_rows,
    )


def solution(mesh):
    return jax.shard_map(
        per_device,
        mesh=mesh,
        in_specs=(
            P("dp", "mp"),
            P("dp", "mp"),
            P("dp", None, None),
            P("dp", None, None),
            P("mp"),
            P("mp", None, None),
            P("mp", None, None),
            P("mp", None, None),
            P("mp", None, None),
        ),
        out_specs=(
            P("dp", "mp"),
            P("dp", "mp"),
            P("dp", None, None),
            P("dp", None, None),
            P("mp"),
            P("mp", None, None),
            P("mp", None, None),
            P("mp", None, None),
            P("mp", None, None),
        ),
        check_vma=False,
    )
```

profile of v0, /device:TPU:0, one launch (start us, length us, event | category | flops | bytes accessed | tf_op | source)
XLA Modules:
  0.0 532.5 jit_solution(9947332528177199786)
XLA Ops:
  7.2 1.6 convolution_convert_fusion.3
  9.5 25.0 %all_to_all.135 = bf16[3,128,1024]{2,0,1:T(4,128)(2,1)S(1)} all-to-all(bf16[3,128,1024]{2,0,1:T(4,128)(2,1)S(1)} %copy.143), channel_id=1, replica_groups=mesh['dp'=16,'mp'=8] {'dp'}, dimensions={1} | all-to-all | bytes 1572864 | tf_op jit(solution)/shard_map/all_to_all | solution.py:32
  37.4 3.6 all-to-all-start.1
  41.0 2.6 copy.142
  43.6 10.8 %all-to-all-done.1 = bf16[48,8,1024]{2,1,0:T(8,128)(2,1)S(1)} async-done(((bf16[48,8,1024]{2,1,0:T(8,128)(2,1)}), bf16[48,8,1024]{2,1,0:T(8,128)(2,1)S(1)}, u32[]{:S(2)}, u32[]{:S(2)}) %all-to-all-start.1) | async-done | bytes 786464 | tf_op jit(solution)/shard_map/all_to_all | solution.py:34
  57.0 1.7 copy.149
  58.7 2.2 add_convert_fusion
  61.8 2.7 convert_bitcast_fusion.2
  64.5 5.0 copy.151
  69.5 4.6 all-to-all-start.2
  76.6 3.5 copy.160
  80.1 32.5 %all-to-all-done.2 = bf16[8,512,384]{2,0,1:T(8,128)(2,1)} async-done(((bf16[8,512,384]{2,0,1:T(8,128)(2,1)}), bf16[8,512,384]{2,0,1:T(8,128)(2,1)}, u32[]{:S(2)}, u32[]{:S(2)}) %all-to-all-start.2) | async-done | bytes 3145760 | tf_op jit(solution)/shard_map/all_to_all | solution.py:44
  112.6 4.6 all-to-all-start.4
  117.3 5.8 %fusion.7 = (bf16[64,64,384]{2,0,1:T(8,128)(2,1)}, f32[64,384,64]{1,2,0:T(8,128)}) fusion(bf16[64,64,64]{2,1,0:T(8,128)(2,1)S(1)} %copy-done, bf16[8,8,64,384]{3,1,2,0:T(8,128)(2,1)} %bitcast.12), kind=kOutput, calls=%fused_computation.10 | convolution fusion | flops 209190912 | bytes 13107200 | tf_op jit(solution)/shard_map/ibk,kit->bit/dot_general | solution.py:19
  123.1 32.4 %all-to-all-done.4 = bf16[8,512,384]{2,0,1:T(8,128)(2,1)} async-done(((bf16[8,512,384]{2,0,1:T(8,128)(2,1)}), bf16[8,512,384]{2,0,1:T(8,128)(2,1)}, u32[]{:S(2)}, u32[]{:S(2)}) %all-to-all-start.4) | async-done | bytes 3145760 | tf_op jit(solution)/shard_map/all_to_all | solution.py:49
  155.5 5.6 %fusion.5 = bf16[64,64,384]{2,0,1:T(8,128)(2,1)S(1)} fusion(f32[64,384,64]{1,2,0:T(8,128)} %get-tuple-element.61, bf16[64,64,64]{2,1,0:T(8,128)(2,1)S(1)} %copy-done.20, bf16[8,8,64,384]{3,0,2,1:T(8,128)(2,1)} %bitcast.22), kind=kOutput, calls=%fused_computation.6 | convolution fusion | flops 217055232 | bytes 13107200 | tf_op jit(solution)/shard_map/ibk,bit->kit/dot_general | solution.py:19
  162.8 3.6 copy.164
  166.3 3.6 all-to-all-start.5
  170.0 2.3 copy.157
  172.3 36.1 %all-to-all-done.5 = bf16[64,64,384]{2,1,0:T(8,128)(2,1)S(1)} async-done(((bf16[64,64,384]{2,1,0:T(8,128)(2,1)}), bf16[64,64,384]{2,1,0:T(8,128)(2,1)S(1)}, u32[]{:S(2)}, u32[]{:S(2)}) %all-to-all-start.5) | async-done | bytes 3145760 | tf_op jit(solution)/shard_map/all_to_all | solution.py:57
  208.4 1.7 copy-done.6
  210.1 2.5 copy.165
  214.1 2.1 copy.167
  216.2 2.5 reshape.50
  220.3 1.6 copy.168
  222.0 4.6 all-to-all-start.6
  226.5 3.2 convert_bitcast_fusion.1
  229.7 3.5 copy.154
  233.3 10.8 %all-to-all-done.6 = bf16[3,128,1024]{2,0,1:T(4,128)(2,1)} async-done(((bf16[3,128,1024]{2,0,1:T(4,128)(2,1)}), bf16[3,128,1024]{2,0,1:T(4,128)(2,1)}, u32[]{:S(2)}, u32[]{:S(2)}) %all-to-all-start.6) | async-done | bytes 786464 | tf_op jit(solution)/shard_map/all_to_all | solution.py:68
  244.1 4.5 all-to-all-start.3
  248.5 5.4 %fusion.10 = f32[64,64,64]{2,1,0:T(8,128)} fusion(bf16[64,64,384]{2,0,1:T(8,128)(2,1)} %get-tuple-element.60, bf16[8,8,64,384]{3,0,2,1:T(8,128)(2,1)} %bitcast.22), kind=kOutput, calls=%fused_computation.13 | convolution fusion | flops 201326592 | bytes 7340032 | tf_op jit(solution)/shard_map/bit,kit->ibk/dot_general | solution.py:19
  258.9 28.1 %all-to-all-done.3 = bf16[64,64,384]{2,1,0:T(8,128)(2,1)} async-done(((bf16[64,64,384]{2,1,0:T(8,128)(2,1)}), bf16[64,64,384]{2,1,0:T(8,128)(2,1)}, u32[]{:S(2)}, u32[]{:S(2)}) %all-to-all-start.3) | async-done | bytes 3145760 | tf_op jit(solution)/shard_map/all_to_all | solution.py:48
  287.0 4.3 all-to-all-start.7
  291.3 5.4 %fusion.14 = f32[64,64,64]{2,1,0:T(8,128)} fusion(bf16[64,64,384]{2,0,1:T(8,128)(2,1)} %copy-done.5, bf16[8,8,64,384]{3,1,2,0:T(8,128)(2,1)} %bitcast.12), kind=kOutput, calls=%fused_computation.17 | convolution fusion | flops 201326592 | bytes 7340032 | tf_op jit(solution)/shard_map/bit,kit->ibk/dot_general | solution.py:19
  296.7 4.0 copy.155
  300.7 2.3 fusion.39
  305.8 2.4 fusion.29
  308.3 3.4 convolution_bitcast_fusion
  311.8 3.1 fusion.25
  314.9 2.3 copy.181
  317.2 39.4 %psum.51 = f32[1024]{0:T(1024)S(1)} all-reduce(f32[1024]{0:T(1024)S(1)} %bitcast.152), channel_id=1, replica_groups=mesh['dp'=16,'mp'=8] {'dp'}, use_global_device_ids=true, to_apply=%region_3.0 | all-reduce | flops 1024 | bytes 8192 | tf_op jit(solution)/shard_map/psum | solution.py:66
  357.2 3.0 fusion.24
  360.2 7.1 %all-reduce.7.cloned.1.call-done = (f32[3,128,128]{2,1,0:T(8,128)}, f32[8,48,48]{2,1,0:T(8,128)}) async-done(((f32[3,128,128]{2,1,0:T(8,128)}, f32[8,48,48]{2,1,0:T(8,128)}), (f32[3,128,128]{2,1,0:T(8,128)}, f32[8,48,48]{2,1,0:T(8,128)})) %all-reduce.7.cloned.1.call-update) | async-done | bytes 270352 | tf_op jit(solution)/shard_map/psum | solution.py:74
  367.3 1.6 broadcast_multiply_fusion.5
  370.5 144.6 %all-reduce.5.cloned.1.call-done = (f32[8,512,128]{2,1,0:T(8,128)}, f32[64,64,64]{2,1,0:T(8,128)}, f32[64,64,64]{2,1,0:T(8,128)}, f32[8,128,512]{1,2,0:T(8,128)}) async-done(((f32[8,512,128]{2,1,0:T(8,128)}, f32[64,64,64]{2,1,0:T(8,128)}, f32[64,64,64]{2,1,0:T(8,128)}, f32[8,128,512]{1,2,0:T(8,128)}), (f32[8,512,128]{2,1,0:T(8,128)}, f32[64,64,64]{2,1,0:T(8,128)}, f32[64,64,64]{2,1,0:T(8,128)}, ...) | async-done | bytes 6291472 | tf_op jit(solution)/shard_map/psum | solution.py:66
  515.1 3.2 broadcast_multiply_fusion.3
  518.6 1.8 copy.182
  520.4 5.2 broadcast_multiply_fusion.1
  (73 shorter events, 24.6 us)
Async XLA Ops:
  7.2 110.1 %copy-start = (bf16[64,64,64]{2,1,0:T(8,128)(2,1)S(1)}, bf16[64,64,64]{2,1,0:T(8,128)(2,1)}, u32[]{:S(2)}) copy-start(bf16[64,64,64]{2,1,0:T(8,128)(2,1)} %param.15) | copy-start | bytes 1572868
  9.5 25.4 %copy-start.22 = (bf16[8,48,48]{2,1,0:T(8,128)(2,1)S(1)}, bf16[8,48,48]{2,1,0:T(8,128)(2,1)}, u32[]{:S(2)}) copy-start(bf16[8,48,48]{2,1,0:T(8,128)(2,1)} %param.12) | copy-start | bytes 110596
  34.9 8.6 %copy-start.14 = (bf16[16,3,8,1024]{3,2,1,0:T(8,128)(2,1)}, bf16[16,3,8,1024]{3,2,1,0:T(8,128)(2,1)S(1)}, u32[]{:S(2)}) copy-start(bf16[16,3,8,1024]{3,2,1,0:T(8,128)(2,1)S(1)} %copy.145) | copy-start | bytes 2359300
  37.4 16.9 %all-to-all-start.1 = ((bf16[48,8,1024]{2,1,0:T(8,128)(2,1)}), bf16[48,8,1024]{2,1,0:T(8,128)(2,1)S(1)}, u32[]{:S(2)}, u32[]{:S(2)}) async-start(bf16[48,8,1024]{2,1,0:T(8,128)(2,1)} %copy.147), calls=%async_computation.1 | async-start | bytes 1572864 | tf_op jit(solution)/shard_map/all_to_all | solution.py:34
  54.3 0.9 copy-start.18
  56.6 2.1 copy-start.23
  57.0 3.9 copy-start.3
  58.7 3.1 copy-start.10
  60.9 0.9 copy-start.8
  69.5 6.1 %copy-start.12 = (bf16[8,128,512]{2,1,0:T(8,128)(2,1)S(1)}, bf16[8,128,512]{2,1,0:T(8,128)(2,1)}, u32[]{:S(2)}) copy-start(bf16[8,128,512]{2,1,0:T(8,128)(2,1)} %param.17) | copy-start | bytes 3145732
  69.5 43.1 %all-to-all-start.2 = ((bf16[8,512,384]{2,0,1:T(8,128)(2,1)}), bf16[8,512,384]{2,0,1:T(8,128)(2,1)}, u32[]{:S(2)}, u32[]{:S(2)}) async-start(bf16[8,512,384]{2,0,1:T(8,128)(2,1)} %copy.151), calls=%async_computation.2 | async-start | bytes 6291456 | tf_op jit(solution)/shard_map/all_to_all | solution.py:44
  75.6 4.6 copy-start.7
  112.6 42.9 %all-to-all-start.4 = ((bf16[8,512,384]{2,0,1:T(8,128)(2,1)}), bf16[8,512,384]{2,0,1:T(8,128)(2,1)}, u32[]{:S(2)}, u32[]{:S(2)}) async-start(bf16[8,512,384]{2,0,1:T(8,128)(2,1)} %copy.160), calls=%async_computation.4 | async-start | bytes 6291456 | tf_op jit(solution)/shard_map/all_to_all | solution.py:49
  117.3 38.2 %copy-start.20 = (bf16[64,64,64]{2,1,0:T(8,128)(2,1)S(1)}, bf16[64,64,64]{2,1,0:T(8,128)(2,1)}, u32[]{:S(2)}) copy-start(bf16[64,64,64]{2,1,0:T(8,128)(2,1)} %param.16) | copy-start | bytes 1572868
  161.1 1.6 copy-start.5
  166.3 42.0 %all-to-all-start.5 = ((bf16[64,64,384]{2,1,0:T(8,128)(2,1)}), bf16[64,64,384]{2,1,0:T(8,128)(2,1)S(1)}, u32[]{:S(2)}, u32[]{:S(2)}) async-start(bf16[64,64,384]{2,1,0:T(8,128)(2,1)} %copy.164), calls=%async_computation.5 | async-start | bytes 6291456 | tf_op jit(solution)/shard_map/all_to_all | solution.py:57
  208.4 1.7 copy-start.6
  210.1 2.5 copy-start.4
  210.1 2.6 copy-start.11
  210.1 2.9 copy-start.13
  222.0 22.1 %all-to-all-start.6 = ((bf16[3,128,1024]{2,0,1:T(4,128)(2,1)}), bf16[3,128,1024]{2,0,1:T(4,128)(2,1)}, u32[]{:S(2)}, u32[]{:S(2)}) async-start(bf16[3,128,1024]{2,0,1:T(4,128)(2,1)} %copy.168), calls=%async_computation.6 | async-start | bytes 2097152 | tf_op jit(solution)/shard_map/all_to_all | solution.py:68
  244.1 42.9 %all-to-all-start.3 = ((bf16[64,64,384]{2,1,0:T(8,128)(2,1)}), bf16[64,64,384]{2,1,0:T(8,128)(2,1)}, u32[]{:S(2)}, u32[]{:S(2)}) async-start(bf16[64,64,384]{2,1,0:T(8,128)(2,1)} %copy.154), calls=%async_computation.3 | async-start | bytes 6291456 | tf_op jit(solution)/shard_map/all_to_all | solution.py:48
  255.5 0.9 copy-start.16
  287.0 18.9 %all-to-all-start.7 = ((bf16[48,8,1024]{2,1,0:T(8,128)(2,1)}), bf16[48,8,1024]{2,1,0:T(8,128)(2,1)}, u32[]{:S(2)}, u32[]{:S(2)}) async-start(bf16[48,8,1024]{2,1,0:T(8,128)(2,1)} %copy.173), calls=%async_computation.7 | async-start | bytes 1572864 | tf_op jit(solution)/shard_map/all_to_all | solution.py:71
  291.3 76.0 %all-reduce.7.cloned.1.call-start = ((), (), s32[]{:S(2)}) async-start(), calls=%async_computation.9 | async-start | bytes 786432 | tf_op jit(solution)/shard_map/psum | solution.py:74
  296.7 4.0 copy-start.9
  300.7 2.3 copy-start.15
  300.7 2.3 copy-start.17
  303.0 5.3 copy-start.2
  308.3 206.9 %all-reduce.5.cloned.1.call-start = ((), (), s32[]{:S(2)}) async-start(), calls=%async_computation.8 | async-start | bytes 16777216 | tf_op jit(solution)/shard_map/psum | solution.py:66
  311.8 45.4 %copy-start.21 = (bf16[3,128,128]{2,1,0:T(8,128)(2,1)S(1)}, bf16[3,128,128]{2,1,0:T(8,128)(2,1)}, u32[]{:S(2)}) copy-start(bf16[3,128,128]{2,1,0:T(8,128)(2,1)} %param.11) | copy-start | bytes 294916
  515.1 3.3 copy-start.19
  520.4 5.2 copy-start.1
Sparse Core Ops, SparseCore 0:
  308.4 58.8 all-reduce.6
  373.2 141.9 all-reduce.4
where the time goes:
time: 534 us; the launch traced here: 532 us
  waiting for transfers between devices  304 us (57%)
  blocking collectives  64.5 us (12%)
  local copies, waits for them, and re-layouts  51.5 us (10%)
  matrix products  51.1 us (10%)
  starting transfers between devices  29.9 us (6%)
  other arithmetic  17.6 us (3%)
  between operations  14.4 us (3%)
    psum x1, waiting for transfers between devices, per_device(): sum_r1, sum_gain = lax.psum((part_r1, part_gain), 'dp')  145 us
    dot_general x18, matrix products, product(): jnp.einsum(form, left_arg, right_arg, preferred_element_type=jnp.float32)  51.1 us
    psum x1, blocking collectives, per_device(): sum_r1, sum_gain = lax.psum((part_r1, part_gain), 'dp')  39.4 us
    all_to_all x1, waiting for transfers between devices, per_device(): lax.all_to_all(back_a_moved, 'mp', split_axis=0, concat_axis=1, tiled=True)  36.1 us
    all_to_all x1, waiting for transfers between devices, per_device(): lax.all_to_all(act_a, 'mp', split_axis=1, concat_axis=0, tiled=True)  32.5 us
    all_to_all x1, waiting for transfers between devices, per_device(): lax.all_to_all(back_c, 'mp', split_axis=1, concat_axis=0, tiled=True)  32.4 us
    all_to_all x1, waiting for transfers between devices, per_device(): lax.all_to_all(act_c_moved, 'mp', split_axis=0, concat_axis=1, tiled=True)  28.1 us
    all_to_all x1, blocking collectives, per_device(): lax.all_to_all(first, 'dp', split_axis=1, concat_axis=0, tiled=True)  25 us
  transfers between devices with their start and end apart: 9, of which 9 were waited for; matrix products, arithmetic and copies ran while one was open for 12% of the time, Pallas kernels for 0%

commit v1 on v0

v1 whole, which is shorter than its diff:
```python
import math

import jax
import jax.numpy as jnp
from jax import lax
from jax.experimental import pallas as pl
from jax.experimental.pallas import tpu as pltpu
from jax.sharding import PartitionSpec as P

BF = jnp.bfloat16
F32 = jnp.float32
VMEM_BYTES = 56 * 1024 * 1024


def dot(left_arg, right_arg, left_dim, right_dim):
    return lax.dot_general(
        left_arg,
        right_arg,
        (((left_dim,), (right_dim,)), ((), ())),
        preferred_element_type=F32,
    )


def product(form, left_arg, right_arg):
    return jnp.einsum(form, left_arg, right_arg, preferred_element_type=F32)


def sum_slice(parts):
    n = lax.axis_size("dp")
    mine = lax.all_to_all(parts.reshape(n, -1, parts.shape[-1]), "dp", split_axis=0, concat_axis=0, tiled=True)
    return jnp.sum(mine.astype(F32), axis=0)


def all_slices(piece):
    n = lax.axis_size("dp")
    copies = jnp.broadcast_to(piece[None], (n,) + piece.shape)
    return lax.all_to_all(copies, "dp", split_axis=0, concat_axis=0, tiled=True)


def sum_over_mp(value):
    n = lax.axis_size("mp")
    core = lax.axis_index("mp") % 2
    half = value.shape[0] // 2
    halves = value.reshape(2, half, value.shape[1])
    mine = lax.dynamic_index_in_dim(halves, core, 0, keepdims=False)
    other = lax.dynamic_index_in_dim(halves, 1 - core, 0, keepdims=False)
    swap = [(i, i ^ 1) for i in range(n)]
    mine = mine + lax.ppermute(other, "mp", swap)
    total = mine
    for d in range(2, n, 2):
        total = total + lax.ppermute(mine, "mp", [(i, i ^ d) for i in range(n)])
    other = lax.ppermute(total, "mp", swap)
    return jnp.where(core == 0, jnp.concatenate([total, other]), jnp.concatenate([other, total]))


def params():
    return pltpu.CompilerParams(vmem_limit_bytes=VMEM_BYTES)


def expand(x, weight, parts, me):
    blocks, hidden, feats = weight.shape
    tokens = x.shape[0]
    lanes = tokens // 128
    rows = hidden // parts * blocks

    def body(me_ref, x_ref, w_ref, *refs):
        outs, wide_ref = refs[:parts], refs[parts]
        for b in range(blocks):
            part = dot(w_ref[b], x_ref[:, b * feats : (b + 1) * feats], 1, 1)
            for c in range(lanes):
                wide_ref[c, pl.ds(b, hidden, stride=blocks), :] = part[:, c * 128 : (c + 1) * 128]
        for d in range(parts):
            start = pl.multiple_of((me_ref[0] ^ d) * rows, rows)
            for c in range(lanes):
                outs[d][:, c * 128 : (c + 1) * 128] = wide_ref[c, pl.ds(start, rows), :].astype(BF)

    return pl.pallas_call(
        body,
        in_specs=[pl.BlockSpec(memory_space=pltpu.SMEM)] + [pl.BlockSpec(memory_space=pltpu.VMEM)] * 2,
        out_specs=[pl.BlockSpec(memory_space=pltpu.VMEM)] * parts,
        out_shape=[jax.ShapeDtypeStruct((rows, tokens), BF)] * parts,
        scratch_shapes=[pltpu.VMEM((lanes, hidden * blocks, 128), F32)],
        compiler_params=params(),
        name="expand",
    )(me, x, weight)


def send(pieces, *which):
    n = len(pieces)
    return {d: lax.ppermute(pieces[d], "mp", [(i, i ^ d) for i in range(n)]) for d in which}


def together(*values):
    return lax.optimization_barrier(values)


def in_order(pieces, *groups):
    got = {0: pieces[0]}
    for group in groups:
        got.update(group)
    return [got[d] for d in range(len(pieces))]


STEP = 8


def gather_pair(refs, pair, me_ref, mix_ref):
    for d, ref in enumerate(refs):
        wide = ref[pair * 16 : pair * 16 + 16, :].astype(F32)
        at = pl.multiple_of((me_ref[0] ^ d) * 8, 8)
        for h in range(2):
            mix_ref[h, pl.ds(at, 8), :] = wide[h * 8 : h * 8 + 8]
    return [mix_ref[h].astype(BF) for h in range(2)]


def spread_pair(values, refs, pair, me_ref, mix_ref):
    for h in range(2):
        mix_ref[h] = values[h]
    for d, ref in enumerate(refs):
        at = pl.multiple_of((me_ref[0] ^ d) * 8, 8)
        block = jnp.concatenate([mix_ref[h, pl.ds(at, 8), :] for h in range(2)], axis=0)
        ref[pair * 16 : pair * 16 + 16, :] = block.astype(BF)


def middle_main(act, back, left_one, left_one_t, left_two_t, me):
    n = len(act)
    tokens = act[0].shape[1]
    units, width, _ = left_one.shape

    def body(me_ref, *refs):
        acts, backs, (one_ref, one_t_ref, two_t_ref) = refs[:n], refs[n : 2 * n], refs[2 * n : 2 * n + 3]
        outs = refs[2 * n + 3 : 3 * n + 3]
        x_ref, c_ref, hid_ref, bp_ref, mix_a, mix_c, mix_o = refs[3 * n + 3 :]
        for pair in range(STEP // 2):
            xs = gather_pair(acts, pair, me_ref, mix_a)
            cs = gather_pair(backs, pair, me_ref, mix_c)
            values = []
            for h in range(2):
                i = pair * 2 + h
                pre = dot(one_ref[i], xs[h], 1, 0)
                back_h = dot(two_t_ref[i], cs[h], 1, 0)
                cdf = 0.5 * (1.0 + lax.erf(pre * (1.0 / math.sqrt(2.0))))
                slope = cdf + pre * jnp.exp(-0.5 * pre * pre) * (1.0 / math.sqrt(2.0 * math.pi))
                back_pre = (back_h * slope).astype(BF)
                x_ref[i] = xs[h]
                c_ref[i] = cs[h]
                hid_ref[i] = (pre * cdf).astype(BF)
                bp_ref[i] = back_pre
                values.append(dot(one_t_ref[i], back_pre, 1, 0))
            spread_pair(values, outs, pair, me_ref, mix_o)

    piece = pl.BlockSpec((STEP * 8, tokens), lambda g: (g, 0))
    weights = pl.BlockSpec((STEP, width, width), lambda g: (g, 0, 0))
    local = pl.BlockSpec((STEP, width, tokens), lambda g: (g, 0, 0))
    results = pl.pallas_call(
        body,
        grid=(units // STEP,),
        in_specs=[pl.BlockSpec(memory_space=pltpu.SMEM)] + [piece] * (2 * n) + [weights] * 3,
        out_specs=[piece] * n + [local] * 4,
        out_shape=[jax.ShapeDtypeStruct(act[0].shape, BF)] * n
        + [jax.ShapeDtypeStruct((units, width, tokens), BF)] * 4,
        scratch_shapes=[pltpu.VMEM((2, width, tokens), F32)] * 3,
        compiler_params=params(),
        name="middle_main",
    )(me, *act, *back, left_one, left_one_t, left_two_t)
    return results[:n], results[n:]


def middle_rest(x, back, hid, back_pre, left_two, n, me):
    units, width, tokens = x.shape

    def body(me_ref, x_ref, c_ref, hid_ref, bp_ref, two_ref, *refs):
        outs, grad_ref, mix_o = refs[:n], refs[n], refs[n + 1]
        for pair in range(STEP // 2):
            values = []
            for h in range(2):
                i = pair * 2 + h
                values.append(dot(two_ref[i], hid_ref[i], 1, 0))
                grads = [dot(bp_ref[i], x_ref[i], 1, 1), dot(c_ref[i], hid_ref[i], 1, 1)]
                grad_ref[i] = jnp.concatenate(grads, axis=1).astype(BF)
            spread_pair(values, outs, pair, me_ref, mix_o)

    piece = pl.BlockSpec((STEP * 8, tokens), lambda g: (g, 0))
    weights = pl.BlockSpec((STEP, width, width), lambda g: (g, 0, 0))
    local = pl.BlockSpec((STEP, width, tokens), lambda g: (g, 0, 0))
    results = pl.pallas_call(
        body,
        grid=(units // STEP,),
        in_specs=[pl.BlockSpec(memory_space=pltpu.SMEM)] + [local] * 4 + [weights],
        out_specs=[piece] * n + [pl.BlockSpec((STEP, width, 2 * width), lambda g: (g, 0, 0))],
        out_shape=[jax.ShapeDtypeStruct((units * 8, tokens), BF)] * n
        + [jax.ShapeDtypeStruct((units, width, 2 * width), BF)],
        scratch_shapes=[pltpu.VMEM((2, width, tokens), F32)],
        compiler_params=params(),
        name="middle_rest",
    )(me, x, back, hid, back_pre, left_two)
    return results[:n], results[n]


def load_wide(pieces, me_ref, wide_ref):
    rows = pieces[0].shape[0]

    @pl.when(pl.program_id(0) == 0)
    def _():
        for d, ref in enumerate(pieces):
            start = pl.multiple_of((me_ref[0] ^ d) * rows, rows)
            for c in range(wide_ref.shape[0]):
                wide_ref[c, pl.ds(start, rows), :] = ref[:, c * 128 : (c + 1) * 128].astype(F32)


def pick_block(wide_ref, hidden, blocks):
    rows = pl.ds(pl.program_id(0), hidden, stride=blocks)
    parts = [wide_ref[c, rows, :].astype(BF) for c in range(wide_ref.shape[0])]
    return jnp.concatenate(parts, axis=1)


def output_side(act, zed, cot, right_two, me):
    n = len(act)
    rows, tokens = act[0].shape
    blocks, feats, hidden = right_two.shape

    def body(me_ref, *refs):
        z_ref, g_ref, w_ref, out_ref, r2_ref, wide_ref = refs[n:]
        load_wide(refs[:n], me_ref, wide_ref)
        mine = pick_block(wide_ref, hidden, blocks)
        last = dot(w_ref[0], mine, 1, 0)
        out_ref[...] = (z_ref[...].astype(F32) + last.T).astype(BF)
        r2_ref[0] = dot(g_ref[...], mine, 0, 1).astype(BF)

    column = pl.BlockSpec((tokens, feats), lambda b: (0, b))
    return pl.pallas_call(
        body,
        grid=(blocks,),
        in_specs=[pl.BlockSpec(memory_space=pltpu.SMEM)]
        + [pl.BlockSpec((rows, tokens), lambda b: (0, 0))] * n
        + [
            column,
            column,
            pl.BlockSpec((1, feats, hidden), lambda b: (b, 0, 0)),
        ],
        out_specs=[column, pl.BlockSpec((1, feats, hidden), lambda b: (b, 0, 0))],
        out_shape=[
            jax.ShapeDtypeStruct(zed.shape, BF),
            jax.ShapeDtypeStruct(right_two.shape, BF),
        ],
        scratch_shapes=[pltpu.VMEM((tokens // 128, n * rows, 128), F32)],
        compiler_params=params(),
        name="output_side",
    )(me, *act, zed, cot, right_two)


def input_side(act, zed, cot, mixed, gain, right_one_t, me):
    n = len(act)
    rows, tokens = act[0].shape
    blocks, feats, hidden = right_one_t.shape

    def body(me_ref, *refs):
        z_ref, g_ref, m_ref, s_ref, w_ref, bz_ref, bm_ref, r1_ref, wide_ref = refs[n:]
        load_wide(refs[:n], me_ref, wide_ref)
        mine = pick_block(wide_ref, hidden, blocks)
        back_z = g_ref[...].astype(F32) + dot(w_ref[0], mine, 1, 0).T
        bz_ref[...] = back_z
        bm_ref[...] = (back_z * s_ref[...]).astype(BF)
        gain_part = jnp.sum(back_z * m_ref[...].astype(F32), axis=0, keepdims=True)
        high = gain_part.astype(BF).astype(F32)
        row = lax.broadcasted_iota(jnp.int32, (8, feats), 0)
        tail = jnp.where(row == 0, high, jnp.where(row == 1, gain_part - high, 0.0)).astype(BF)
        grad = dot(mine, z_ref[...], 1, 0).astype(BF)
        for h in range(2):
            r1_ref[h, : hidden // 2, :] = grad[h * hidden // 2 : (h + 1) * hidden // 2]
            r1_ref[h, hidden // 2 :, :] = tail

    column = pl.BlockSpec((tokens, feats), lambda b: (0, b))
    row = pl.BlockSpec((1, feats), lambda b: (0, b))
    return pl.pallas_call(
        body,
        grid=(blocks,),
        in_specs=[pl.BlockSpec(memory_space=pltpu.SMEM)]
        + [pl.BlockSpec((rows, tokens), lambda b: (0, 0))] * n
        + [
            column,
            column,
            column,
            row,
            pl.BlockSpec((1, feats, hidden), lambda b: (b, 0, 0)),
        ],
        out_specs=[
            column,
            column,
            pl.BlockSpec((2, hidden // 2 + 8, feats), lambda b: (b, 0, 0)),
        ],
        out_shape=[
            jax.ShapeDtypeStruct(zed.shape, F32),
            jax.ShapeDtypeStruct(zed.shape, BF),
            jax.ShapeDtypeStruct((blocks * 2, hidden // 2 + 8, feats), BF),
        ],
        scratch_shapes=[pltpu.VMEM((tokens // 128, n * rows, 128), F32)],
        compiler_params=params(),
        name="input_side",
    )(me, *act, zed, cot, mixed, gain, right_one_t)


def per_device(
    tokens, cotangent, seq_right, seq_left, seq_gain, right_one, left_one, left_two, right_two
):
    rows_here, cols_here = tokens.shape
    block_len = seq_right.shape[1]
    blocks_here = rows_here // block_len
    n_mp = lax.axis_size("mp")
    me = lax.axis_index("mp").astype(jnp.int32)
    me1 = me.reshape(1)
    scale_rows = float(rows_here * lax.axis_size("dp")) ** (-0.5)
    scale_cols = float(cols_here * n_mp) ** (-0.5)

    pieces = expand(cotangent, jnp.swapaxes(right_two, 1, 2), n_mp, me1)
    seq_view = tokens.reshape(blocks_here, block_len, cols_here)
    first = product("sij,sjc->sic", seq_right, seq_view).astype(BF)
    first, pieces = together(first, pieces)
    back_c1 = send(pieces, 2, 6, 1, 3, 7)
    first_moved = lax.all_to_all(first, "dp", split_axis=1, concat_axis=0, tiled=True)
    first_moved, back_c1 = together(first_moved, back_c1)
    mixed_moved = product("isk,kic->sic", seq_left, first_moved).astype(BF)
    back_c2 = send(pieces, 4, 5)
    mixed = lax.all_to_all(mixed_moved, "dp", split_axis=0, concat_axis=1, tiled=True)
    mixed = mixed.reshape(rows_here, cols_here)
    mixed, back_c2 = together(mixed, back_c2)
    back_c = in_order(pieces, back_c1, back_c2)
    zed = (tokens.astype(F32) + seq_gain * mixed.astype(F32)).astype(BF)

    pieces = expand(zed, right_one, n_mp, me1)
    act_a = in_order(pieces, send(pieces, 2, 6, 4, 3, 7, 5, 1))
    pieces, (x, back, hid, back_pre) = middle_main(
        act_a, back_c, left_one, jnp.swapaxes(left_one, 1, 2), jnp.swapaxes(left_two, 1, 2), me1
    )
    back_a1 = send(pieces, 2, 6, 1)
    pieces_c, part_left = middle_rest(x, back, hid, back_pre, left_two, n_mp, me1)
    part_left, back_a1 = together(part_left, back_a1)
    back_a2 = send(pieces, 3, 7, 4)
    slice_left = (sum_slice(part_left) * scale_rows).astype(BF)
    slice_left, back_a2 = together(slice_left, back_a2)
    back_a3 = send(pieces, 5)
    sum_left = all_slices(slice_left)
    sum_left, back_a3 = together(sum_left, back_a3)
    sum_left = sum_left.astype(F32).reshape(part_left.shape)
    back_a = in_order(pieces, back_a1, back_a2, back_a3)

    pieces_c, back_a = together(pieces_c, back_a)
    act_c1 = send(pieces_c, 2, 6)
    back_z, back_mixed, part_r1 = input_side(
        back_a,
        zed,
        cotangent,
        mixed,
        seq_gain.reshape(1, cols_here),
        jnp.swapaxes(right_one, 1, 2),
        me1,
    )
    back_mixed, act_c1 = together(back_mixed, act_c1)
    back_z = back_z.reshape(blocks_here, block_len, cols_here)
    back_mixed = back_mixed.reshape(blocks_here, block_len, cols_here)
    act_c2 = send(pieces_c, 3, 7, 4)
    back_mixed_moved = lax.all_to_all(back_mixed, "dp", split_axis=1, concat_axis=0, tiled=True)
    back_mixed_moved, act_c2 = together(back_mixed_moved, act_c2)
    back_first_moved = product("isk,sic->kic", seq_left, back_mixed_moved).astype(BF)
    part_seq_left = product("sic,kic->isk", back_mixed_moved, first_moved)
    act_c3 = send(pieces_c, 5, 1)
    back_first = lax.all_to_all(back_first_moved, "dp", split_axis=0, concat_axis=1, tiled=True)
    back_first, act_c3 = together(back_first, act_c3)
    act_c = in_order(pieces_c, act_c1, act_c2, act_c3)

    part_r1, back_first = together(part_r1, back_first)
    slice_r1 = sum_slice(part_r1)
    output, part_r2 = output_side(act_c, zed, cotangent, right_two, me1)
    slice_r1, part_r2 = together(slice_r1, part_r2)
    half = right_one.shape[1] // 2
    slice_gain = slice_r1[half : half + 1] + slice_r1[half + 1 : half + 2]
    slice_r1 = jnp.concatenate([slice_r1[:half], jnp.broadcast_to(slice_gain, (8, block_len))])
    slice_r2 = sum_slice(part_r2)
    slice_r1, slice_r2 = together((slice_r1 * scale_rows).astype(BF), (slice_r2 * scale_rows).astype(BF))
    sum_r1 = all_slices(slice_r1).astype(F32)
    sum_r2 = all_slices(slice_r2).astype(F32)

    grad_tokens = (back_z + product("sij,sic->sjc", seq_right, back_first)).astype(BF)
    part_seq_right = product("sic,sjc->sij", back_first, seq_view)
    seq_sum = sum_over_mp(
        jnp.concatenate([part_seq_right.reshape(-1, 128), part_seq_left.reshape(-1, 128)])
    )
    seq_rows = part_seq_right.size // 128
    return (
        output,
        grad_tokens.reshape(rows_here, cols_here),
        seq_sum[:seq_rows].reshape(part_seq_right.shape) * scale_cols,
        seq_sum[seq_rows:].reshape(part_seq_left.shape) * scale_cols,
        sum_r1[::2, half].reshape(cols_here),
        sum_r1[:, :half].reshape(right_one.shape),
        sum_left[:, :, : left_one.shape[2]],
        sum_left[:, :, left_one.shape[2] :],
        sum_r2.reshape(right_two.shape),
    )


def solution(mesh):
    specs = (
        P("dp", "mp"),
        P("dp", "mp"),
        P("dp", None, None),
        P("dp", None, None),
        P("mp"),
        P("mp", None, None),
        P("mp", None, None),
        P("mp", None, None),
        P("mp", None, None),
    )
    return jax.shard_map(per_device, mesh=mesh, in_specs=specs, out_specs=specs, check_vma=False)
```

time: 534 us -> 370 us (0.69)
  waiting for transfers between devices: 304 us -> 175 us
  blocking collectives: 64.5 us -> 0 us
  starting transfers between devices: 29.9 us -> 93 us
  Pallas kernels: 0 us -> 55.4 us
  matrix products: 51.1 us -> 8.43 us
  local copies, waits for them, and re-layouts: 51.5 us -> 26.5 us
  between operations: 14.4 us -> 1.26 us
  other arithmetic: 17.6 us -> 8.45 us
    psum x2 -> x0, waiting for transfers between devices: 152 us -> none  [the longest x1 145 us: per_device(): sum_r1, sum_gain = lax.psum((part_r1, part_gain), 'dp')]
    ppermute x0 -> x33, waiting for transfers between devices: none -> 63.4 us  [the longest x28 58.8 us: send(): lax.ppermute(pieces[d], 'mp', [(i, i ^ d) for i in range(n)])]
    all_to_all x4 -> x7, waiting for transfers between devices: 129 us -> 71.8 us  [the longest x3 35.3 us: sum_slice(): lax.all_to_all(parts.reshape(n, -1, parts.shape[-1]), 'dp', split_axis=0,...]
    pallas_call x0 -> x6, Pallas kernels: none -> 55.4 us  [the longest x1 16.9 us: middle_main(): pl.pallas_call(body, grid=(units // STEP,), in_specs=[pl.BlockSpec(memory...]
    dot_general x18 -> x6, matrix products: 51.1 us -> 8.43 us  [product(): return jnp.einsum(form, left_arg, right_arg, preferred_element_type=F32)]
    psum x1 -> x0, blocking collectives: 39.4 us -> none  [per_device(): sum_r1, sum_gain = lax.psum((part_r1, part_gain), 'dp')]
    ppermute x0 -> x33, starting transfers between devices: none -> 36.1 us  [the longest x28 31.1 us: send(): lax.ppermute(pieces[d], 'mp', [(i, i ^ d) for i in range(n)])]
    all_to_all x1 -> x0, blocking collectives: 25 us -> none  [per_device(): lax.all_to_all(first, 'dp', split_axis=1, concat_axis=0, tiled=True)]
  transfers between devices with their start and end apart: 9 -> 43, of which waited for: 9 -> 28; matrix products, arithmetic and copies ran while one was open for 12% -> 6% of each run, Pallas kernels for 0% -> 8%
where the time goes in v1:
time: 370 us; the launch traced here: 368 us
  waiting for transfers between devices  175 us (47%)
  starting transfers between devices  93 us (25%)
  Pallas kernels  55.4 us (15%)
  local copies, waits for them, and re-layouts  26.5 us (7%)
  other arithmetic  8.45 us (2%)
  matrix products  8.43 us (2%)
    ppermute x28, waiting for transfers between devices, send(): lax.ppermute(pieces[d], 'mp', [(i, i ^ d) for i in range(n)])  58.8 us
    all_to_all x3, waiting for transfers between devices, sum_slice(): lax.all_to_all(parts.reshape(n, -1, parts.shape[-1]), 'dp', split_axis=0,...  35.3 us
    ppermute x28, starting transfers between devices, send(): lax.ppermute(pieces[d], 'mp', [(i, i ^ d) for i in range(n)])  31.1 us
    all_to_all x3, waiting for transfers between devices, all_slices(): return lax.all_to_all(copies, 'dp', split_axis=0, concat_axis=0, tiled=True)  23.8 us
    pallas_call x1, Pallas kernels, middle_main(): pl.pallas_call(body, grid=(units // STEP,), in_specs=[pl.BlockSpec(memory...  16.9 us
    all_to_all x3, starting transfers between devices, sum_slice(): lax.all_to_all(parts.reshape(n, -1, parts.shape[-1]), 'dp', split_axis=0,...  16.4 us
    all_to_all x3, starting transfers between devices, all_slices(): return lax.all_to_all(copies, 'dp', split_axis=0, concat_axis=0, tiled=True)  14.7 us
    all_to_all x1, waiting for transfers between devices, per_device(): lax.all_to_all(back_first_moved, 'dp', split_axis=0, concat_axis=1, tiled...  14.6 us
  transfers between devices with their start and end apart: 43, of which 28 were waited for; matrix products, arithmetic and copies ran while one was open for 6% of the time, Pallas kernels for 8%

profile of v1, /device:TPU:0, one launch (start us, length us, event | category | flops | bytes accessed | tf_op | source)
XLA Modules:
  0.0 367.8 jit_solution(668783333914853493)
XLA Ops:
  0.7 2.3 copy.76
  3.4 4.9 %expand.2 = (bf16[512,384]{1,0:T(8,128)(2,1)}, bf16[512,384]{1,0:T(8,128)(2,1)}, bf16[512,384]{1,0:T(8,128)(2,1)}, bf16[512,384]{1,0:T(8,128)(2,1)}, bf16[512,38...) custom-call(s32[1]{0:T(128)} %bitcast.me_ref, ...), custom_call_target="tpu_custom_call" | custom-call | tf_op jit(solution)/shard_map/expand/pallas_call | solution.py:77
  10.0 8.0 %all-to-all-start = ((bf16[3,128,1024]{2,0,1:T(4,128)(2,1)}), bf16[3,128,1024]{2,0,1:T(4,128)(2,1)S(1)}, u32[]{:S(2)}, u32[]{:S(2)}) async-start(bf16[3,128,1024]{2,0,1:T(4,128)(2,1)} %copy.77), calls=%async_computation | async-start | bytes 2097152 | tf_op jit(solution)/shard_map/all_to_all | solution.py:320
  19.9 3.0 collective-permute-start.3
  22.9 12.7 %all-to-all-done = bf16[3,128,1024]{2,0,1:T(4,128)(2,1)S(1)} async-done(((bf16[3,128,1024]{2,0,1:T(4,128)(2,1)}), bf16[3,128,1024]{2,0,1:T(4,128)(2,1)S(1)}, u32[]{:S(2)}, u32[]{:S(2)}) %all-to-all-start) | async-done | bytes 786464 | tf_op jit(solution)/shard_map/all_to_all | solution.py:320
  37.7 3.1 collective-permute-done.4.refs_15_
  43.3 7.2 %all-to-all-start.1 = ((bf16[48,8,1024]{2,1,0:T(8,128)(2,1)}), bf16[48,8,1024]{2,1,0:T(8,128)(2,1)S(1)}, u32[]{:S(2)}, u32[]{:S(2)}) async-start(bf16[48,8,1024]{2,1,0:T(8,128)(2,1)} %copy.81), calls=%async_computation.1 | async-start | bytes 1572864 | tf_op jit(solution)/shard_map/all_to_all | solution.py:324
  53.4 11.9 %all-to-all-done.1 = bf16[48,8,1024]{2,1,0:T(8,128)(2,1)S(1)} async-done(((bf16[48,8,1024]{2,1,0:T(8,128)(2,1)}), bf16[48,8,1024]{2,1,0:T(8,128)(2,1)S(1)}, u32[]{:S(2)}, u32[]{:S(2)}) %all-to-all-start.1) | async-done | bytes 786464 | tf_op jit(solution)/shard_map/all_to_all | solution.py:324
  65.3 5.4 %collective-permute-done.6.refs_13_ = bf16[512,384]{1,0:T(8,128)(2,1)S(1)} collective-permute-done((bf16[512,384]{1,0:T(8,128)(2,1)}, bf16[512,384]{1,0:T(8,128)(2,1)S(1)}, u32[]{:S(2)}, u32[]{:S(2)}) %collective-permute-start.6) | collective-permute-done | bytes 393248 | tf_op jit(solution)/shard_map/ppermute | solution.py:90
  72.0 4.9 %expand.3 = (bf16[512,384]{1,0:T(8,128)(2,1)}, bf16[512,384]{1,0:T(8,128)(2,1)}, bf16[512,384]{1,0:T(8,128)(2,1)}, bf16[512,384]{1,0:T(8,128)(2,1)}, bf16[512,38...) custom-call(s32[1]{0:T(128)} %bitcast.me_ref, ...), custom_call_target="tpu_custom_call" | custom-call | tf_op jit(solution)/shard_map/expand/pallas_call | solution.py:77
  80.6 3.0 collective-permute-start.12
  83.9 6.8 %collective-permute-done.10.refs_4_ = bf16[512,384]{1,0:T(8,128)(2,1)S(1)} collective-permute-done((bf16[512,384]{1,0:T(8,128)(2,1)}, bf16[512,384]{1,0:T(8,128)(2,1)S(1)}, u32[]{:S(2)}, u32[]{:S(2)}) %collective-permute-start.10) | collective-permute-done | bytes 393248 | tf_op jit(solution)/shard_map/ppermute | solution.py:90
  91.7 7.0 %collective-permute-done.11.refs_5_ = bf16[512,384]{1,0:T(8,128)(2,1)S(1)} collective-permute-done((bf16[512,384]{1,0:T(8,128)(2,1)}, bf16[512,384]{1,0:T(8,128)(2,1)S(1)}, u32[]{:S(2)}, u32[]{:S(2)}) %collective-permute-start.11) | collective-permute-done | bytes 393248 | tf_op jit(solution)/shard_map/ppermute | solution.py:90
  100.8 2.3 copy.84
  103.1 4.3 %collective-permute-done.12.refs_6_ = bf16[512,384]{1,0:T(8,128)(2,1)S(1)} collective-permute-done((bf16[512,384]{1,0:T(8,128)(2,1)}, bf16[512,384]{1,0:T(8,128)(2,1)S(1)}, u32[]{:S(2)}, u32[]{:S(2)}) %collective-permute-start.12) | collective-permute-done | bytes 393248 | tf_op jit(solution)/shard_map/ppermute | solution.py:90
  107.4 8.3 %collective-permute-done.13.refs_7_ = bf16[512,384]{1,0:T(8,128)(2,1)S(1)} collective-permute-done((bf16[512,384]{1,0:T(8,128)(2,1)}, bf16[512,384]{1,0:T(8,128)(2,1)S(1)}, u32[]{:S(2)}, u32[]{:S(2)}) %collective-permute-start.13) | collective-permute-done | bytes 393248 | tf_op jit(solution)/shard_map/ppermute | solution.py:90
  116.4 16.9 %middle_main.1 = (bf16[512,384]{1,0:T(8,128)(2,1)}, bf16[512,384]{1,0:T(8,128)(2,1)}, bf16[512,384]{1,0:T(8,128)(2,1)}, bf16[512,384]{1,0:T(8,128)(2,1)}, bf16[5...) custom-call(s32[1]{0:T(128)} %bitcast.me_ref, ...), custom_call_target="tpu_custom_call" | custom-call | tf_op jit(solution)/shard_map/middle_main/pallas_call | solution.py:155
  134.1 2.5 collective-permute-start.16
  136.7 10.0 %middle_rest.1 = (bf16[512,384]{1,0:T(8,128)(2,1)}, bf16[512,384]{1,0:T(8,128)(2,1)}, bf16[512,384]{1,0:T(8,128)(2,1)}, bf16[512,384]{1,0:T(8,128)(2,1)}, bf16[5...) custom-call(s32[1]{0:T(128)} %bitcast.me_ref, ...), custom_call_target="tpu_custom_call" | custom-call | tf_op jit(solution)/shard_map/middle_rest/pallas_call | solution.py:186
  147.6 6.9 %all-to-all-start.2 = ((bf16[16,256,128]{2,1,0:T(8,128)(2,1)}), bf16[16,256,128]{2,1,0:T(8,128)(2,1)S(1)}, u32[]{:S(2)}, u32[]{:S(2)}) async-start(bf16[16,256,128]{2,1,0:T(8,128)(2,1)} %bitcast.90), calls=%async_computation.2 | async-start | bytes 2097152 | tf_op jit(solution)/shard_map/all_to_all | solution.py:30
  158.7 13.6 %all-to-all-done.2 = bf16[16,256,128]{2,1,0:T(8,128)(2,1)S(1)} async-done(((bf16[16,256,128]{2,1,0:T(8,128)(2,1)}), bf16[16,256,128]{2,1,0:T(8,128)(2,1)S(1)}, u32[]{:S(2)}, u32[]{:S(2)}) %all-to-all-start.2) | async-done | bytes 1048608 | tf_op jit(solution)/shard_map/all_to_all | solution.py:30
  172.5 2.6 collective-permute-done.18.refs_4_
  178.1 6.6 %all-to-all-start.3 = ((bf16[16,256,128]{2,1,0:T(8,128)(2,1)}), bf16[16,256,128]{2,1,0:T(8,128)(2,1)S(1)}, u32[]{:S(2)}, u32[]{:S(2)}) async-start(bf16[16,256,128]{2,1,0:T(8,128)(2,1)} %broadcast_in_dim.12), calls=%async_computation.3 | async-start | bytes 2097152 | tf_op jit(solution)/shard_map/all_to_all | solution.py:37
  186.1 10.8 %collective-permute-done.20.refs_5_ = bf16[512,384]{1,0:T(8,128)(2,1)} collective-permute-done((bf16[512,384]{1,0:T(8,128)(2,1)}, bf16[512,384]{1,0:T(8,128)(2,1)}, u32[]{:S(2)}, u32[]{:S(2)}) %collective-permute-start.20) | collective-permute-done | bytes 393248 | tf_op jit(solution)/shard_map/ppermute | solution.py:90
  196.9 8.8 %all-to-all-done.3 = bf16[16,256,128]{2,1,0:T(8,128)(2,1)S(1)} async-done(((bf16[16,256,128]{2,1,0:T(8,128)(2,1)}), bf16[16,256,128]{2,1,0:T(8,128)(2,1)S(1)}, u32[]{:S(2)}, u32[]{:S(2)}) %all-to-all-start.3) | async-done | bytes 1048608 | tf_op jit(solution)/shard_map/all_to_all | solution.py:37
  208.1 9.6 %input_side.1 = (f32[384,1024]{1,0:T(8,128)}, bf16[384,1024]{1,0:T(8,128)(2,1)}, bf16[16,264,128]{2,1,0:T(8,128)(2,1)}) custom-call(s32[1]{0:T(128)} %bitcast.me_ref, bf16[512,384]{1,0:T(8,128)(2,1)} %get-tuple-element.176.refs_0_, bf16[512,384]{1,0:T(8,128)(2,1)} %copy-done.22, bf16[512,384]{1,0:T(8,128)(2,1)} %copy-done.23, bf16[512,384]{1,0:T(8,128)(2,1)} %copy-done.25, ...), custom_call_target="tpu_custom_call" | custom-call | tf_op jit(solution)/shard_map/input_side/pallas_call | solution.py:275
  218.4 2.8 copy.86
  221.2 3.7 all-to-all-start.4
  224.9 2.6 collective-permute-start.24
  229.0 13.1 %all-to-all-done.4 = bf16[3,128,1024]{2,0,1:T(4,128)(2,1)S(1)} async-done(((bf16[3,128,1024]{2,0,1:T(4,128)(2,1)}), bf16[3,128,1024]{2,0,1:T(4,128)(2,1)S(1)}, u32[]{:S(2)}, u32[]{:S(2)}) %all-to-all-start.4) | async-done | bytes 786464 | tf_op jit(solution)/shard_map/all_to_all | solution.py:362
  242.5 3.7 %collective-permute-done.24.refs_4_ = bf16[512,384]{1,0:T(8,128)(2,1)} collective-permute-done((bf16[512,384]{1,0:T(8,128)(2,1)}, bf16[512,384]{1,0:T(8,128)(2,1)}, u32[]{:S(2)}, u32[]{:S(2)}) %collective-permute-start.24) | collective-permute-done | bytes 393248 | tf_op jit(solution)/shard_map/ppermute | solution.py:90
  250.8 7.1 %all-to-all-start.5 = ((bf16[48,8,1024]{2,1,0:T(8,128)(2,1)}), bf16[48,8,1024]{2,1,0:T(8,128)(2,1)S(1)}, u32[]{:S(2)}, u32[]{:S(2)}) async-start(bf16[48,8,1024]{2,1,0:T(8,128)(2,1)} %copy.91), calls=%async_computation.5 | async-start | bytes 1572864 | tf_op jit(solution)/shard_map/all_to_all | solution.py:367
  258.2 14.6 %all-to-all-done.5 = bf16[48,8,1024]{2,1,0:T(8,128)(2,1)S(1)} async-done(((bf16[48,8,1024]{2,1,0:T(8,128)(2,1)}), bf16[48,8,1024]{2,1,0:T(8,128)(2,1)S(1)}, u32[]{:S(2)}, u32[]{:S(2)}) %all-to-all-start.5) | async-done | bytes 786464 | tf_op jit(solution)/shard_map/all_to_all | solution.py:367
  272.8 5.2 %all-to-all-start.6 = ((bf16[16,264,128]{2,1,0:T(8,128)(2,1)}), bf16[16,264,128]{2,1,0:T(8,128)(2,1)}, u32[]{:S(2)}, u32[]{:S(2)}) async-start(bf16[16,264,128]{2,1,0:T(8,128)(2,1)} %get-tuple-element.206), calls=%async_computation.6 | async-start | bytes 2162688 | tf_op jit(solution)/shard_map/all_to_all | solution.py:30
  278.0 9.1 %output_side.1 = (bf16[384,1024]{1,0:T(8,128)(2,1)}, bf16[8,128,512]{2,1,0:T(8,128)(2,1)}) custom-call(s32[1]{0:T(128)} %bitcast.me_ref, bf16[512,384]{1,0:T(8,128)(2,1)} %get-tuple-element.175.refs_0_, bf16[512,384]{1,0:T(8,128)(2,1)} %collective-permute-done.26.refs_1_, bf16[512,384]{1,0:T(8,128)(2,1)} %copy-done.21, bf16[512,384]{1,0:T(8,128)(2,1)} %copy-done.24, ...), custom_call_target="tpu_custom_call" | custom-call | tf_op jit(solution)/shard_map/output_side/pallas_call | solution.py:231
  287.2 9.6 %all-to-all-done.6 = bf16[16,264,128]{2,1,0:T(8,128)(2,1)} async-done(((bf16[16,264,128]{2,1,0:T(8,128)(2,1)}), bf16[16,264,128]{2,1,0:T(8,128)(2,1)}, u32[]{:S(2)}, u32[]{:S(2)}) %all-to-all-start.6) | async-done | bytes 1081376 | tf_op jit(solution)/shard_map/all_to_all | solution.py:30
  298.8 4.3 %all-to-all-start.7 = ((bf16[16,64,512]{2,1,0:T(8,128)(2,1)}), bf16[16,64,512]{2,1,0:T(8,128)(2,1)}, u32[]{:S(2)}, u32[]{:S(2)}) async-start(bf16[16,64,512]{2,1,0:T(8,128)(2,1)} %bitcast.91), calls=%async_computation.7 | async-start | bytes 2097152 | tf_op jit(solution)/shard_map/all_to_all | solution.py:30
  303.2 2.7 fusion.3
  307.5 12.1 %all-to-all-done.7 = bf16[16,64,512]{2,1,0:T(8,128)(2,1)} async-done(((bf16[16,64,512]{2,1,0:T(8,128)(2,1)}), bf16[16,64,512]{2,1,0:T(8,128)(2,1)}, u32[]{:S(2)}, u32[]{:S(2)}) %all-to-all-start.7) | async-done | bytes 1048608 | tf_op jit(solution)/shard_map/all_to_all | solution.py:30
  322.1 4.3 %all-to-all-start.9 = ((bf16[16,64,512]{2,1,0:T(8,128)(2,1)}), bf16[16,64,512]{2,1,0:T(8,128)(2,1)}, u32[]{:S(2)}, u32[]{:S(2)}) async-start(bf16[16,64,512]{2,1,0:T(8,128)(2,1)} %broadcast_in_dim.33), calls=%async_computation.9 | async-start | bytes 2097152 | tf_op jit(solution)/shard_map/all_to_all | solution.py:37
  329.6 3.1 collective-permute-start.31
  332.7 2.6 fusion.9
  336.2 2.4 collective-permute-done.31
  338.8 3.9 %all-to-all-done.9 = bf16[16,64,512]{2,1,0:T(8,128)(2,1)} async-done(((bf16[16,64,512]{2,1,0:T(8,128)(2,1)}), bf16[16,64,512]{2,1,0:T(8,128)(2,1)}, u32[]{:S(2)}, u32[]{:S(2)}) %all-to-all-start.9) | async-done | bytes 1048608 | tf_op jit(solution)/shard_map/all_to_all | solution.py:37
  343.8 3.7 %all-to-all-start.8 = ((bf16[16,264,128]{2,1,0:T(8,128)(2,1)}), bf16[16,264,128]{2,1,0:T(8,128)(2,1)S(1)}, u32[]{:S(2)}, u32[]{:S(2)}) async-start(bf16[16,264,128]{2,1,0:T(8,128)(2,1)} %broadcast_in_dim.32), calls=%async_computation.8 | async-start | bytes 2162688 | tf_op jit(solution)/shard_map/all_to_all | solution.py:37
  347.5 2.7 fusion
  351.7 2.8 bitcast_convert_fusion
  354.6 11.1 %all-to-all-done.8 = bf16[16,264,128]{2,1,0:T(8,128)(2,1)S(1)} async-done(((bf16[16,264,128]{2,1,0:T(8,128)(2,1)}), bf16[16,264,128]{2,1,0:T(8,128)(2,1)S(1)}, u32[]{:S(2)}, u32[]{:S(2)}) %all-to-all-start.8) | async-done | bytes 1081376 | tf_op jit(solution)/shard_map/all_to_all | solution.py:37
  (145 shorter events, 56.0 us)
Async XLA Ops:
  0.6 40.1 %copy-start = (bf16[8,48,48]{2,1,0:T(8,128)(2,1)S(1)}, bf16[8,48,48]{2,1,0:T(8,128)(2,1)}, u32[]{:S(2)}) copy-start(bf16[8,48,48]{2,1,0:T(8,128)(2,1)} %param.12) | copy-start | bytes 110596
  10.0 25.6 %all-to-all-start = ((bf16[3,128,1024]{2,0,1:T(4,128)(2,1)}), bf16[3,128,1024]{2,0,1:T(4,128)(2,1)S(1)}, u32[]{:S(2)}, u32[]{:S(2)}) async-start(bf16[3,128,1024]{2,0,1:T(4,128)(2,1)} %copy.77), calls=%async_computation | async-start | bytes 2097152 | tf_op jit(solution)/shard_map/all_to_all | solution.py:320
  17.9 18.0 %collective-permute-start = (bf16[512,384]{1,0:T(8,128)(2,1)}, bf16[512,384]{1,0:T(8,128)(2,1)S(1)}, u32[]{:S(2)}, u32[]{:S(2)}) collective-permute-start(bf16[512,384]{1,0:T(8,128)(2,1)} %get-tuple-element.120), channel_id=1, source_target_pairs={{0,1},{1,0},{2,3},{3,2},{4,5},{5,4},{6,7},{7,6},{8,9},{9,8},{10,11... | collective-permute-start | bytes 1179656 | tf_op jit(solution)/shard_map/ppermute | solution.py:90
  18.0 17.9 %collective-permute-start.1 = (bf16[512,384]{1,0:T(8,128)(2,1)}, bf16[512,384]{1,0:T(8,128)(2,1)S(1)}, u32[]{:S(2)}, u32[]{:S(2)}) collective-permute-start(bf16[512,384]{1,0:T(8,128)(2,1)} %get-tuple-element.121), channel_id=1, source_target_pairs={{0,2},{1,3},{2,0},{3,1},{4,6},{5,7},{6,4},{7,5},{8,10},{9,11},{10,... | collective-permute-start | bytes 1179656 | tf_op jit(solution)/shard_map/ppermute | solution.py:90
  19.7 18.0 %collective-permute-start.2 = (bf16[512,384]{1,0:T(8,128)(2,1)}, bf16[512,384]{1,0:T(8,128)(2,1)S(1)}, u32[]{:S(2)}, u32[]{:S(2)}) collective-permute-start(bf16[512,384]{1,0:T(8,128)(2,1)} %get-tuple-element.122), channel_id=1, source_target_pairs={{0,3},{1,2},{2,1},{3,0},{4,7},{5,6},{6,5},{7,4},{8,11},{9,10},{10,... | collective-permute-start | bytes 1179656 | tf_op jit(solution)/shard_map/ppermute | solution.py:90
  19.9 17.8 %collective-permute-start.3 = (bf16[512,384]{1,0:T(8,128)(2,1)}, bf16[512,384]{1,0:T(8,128)(2,1)S(1)}, u32[]{:S(2)}, u32[]{:S(2)}) collective-permute-start(bf16[512,384]{1,0:T(8,128)(2,1)} %get-tuple-element.123), channel_id=1, source_target_pairs={{0,6},{1,7},{2,4},{3,5},{4,2},{5,3},{6,0},{7,1},{8,14},{9,15},{10,... | collective-permute-start | bytes 1179656 | tf_op jit(solution)/shard_map/ppermute | solution.py:90
  22.9 17.9 %collective-permute-start.4 = (bf16[512,384]{1,0:T(8,128)(2,1)}, bf16[512,384]{1,0:T(8,128)(2,1)}, u32[]{:S(2)}, u32[]{:S(2)}) collective-permute-start(bf16[512,384]{1,0:T(8,128)(2,1)} %get-tuple-element.124), channel_id=1, source_target_pairs={{0,7},{1,6},{2,5},{3,4},{4,3},{5,2},{6,1},{7,0},{8,15},{9,14},{10,... | collective-permute-start | bytes 1179656 | tf_op jit(solution)/shard_map/ppermute | solution.py:90
  43.3 27.5 %copy-start.26 = (f32[1024]{0:T(1024)S(1)}, f32[1024]{0:T(1024)}, u32[]{:S(2)}) copy-start(f32[1024]{0:T(1024)} %param.13) | copy-start | bytes 12292
  43.3 22.0 %all-to-all-start.1 = ((bf16[48,8,1024]{2,1,0:T(8,128)(2,1)}), bf16[48,8,1024]{2,1,0:T(8,128)(2,1)S(1)}, u32[]{:S(2)}, u32[]{:S(2)}) async-start(bf16[48,8,1024]{2,1,0:T(8,128)(2,1)} %copy.81), calls=%async_computation.1 | async-start | bytes 1572864 | tf_op jit(solution)/shard_map/all_to_all | solution.py:324
  50.4 14.9 %collective-permute-start.5 = (bf16[512,384]{1,0:T(8,128)(2,1)}, bf16[512,384]{1,0:T(8,128)(2,1)S(1)}, u32[]{:S(2)}, u32[]{:S(2)}) collective-permute-start(bf16[512,384]{1,0:T(8,128)(2,1)} %get-tuple-element.126), channel_id=1, source_target_pairs={{0,4},{1,5},{2,6},{3,7},{4,0},{5,1},{6,2},{7,3},{8,12},{9,13},{10,... | collective-permute-start | bytes 1179656 | tf_op jit(solution)/shard_map/ppermute | solution.py:90
  52.4 18.4 %collective-permute-start.6 = (bf16[512,384]{1,0:T(8,128)(2,1)}, bf16[512,384]{1,0:T(8,128)(2,1)S(1)}, u32[]{:S(2)}, u32[]{:S(2)}) collective-permute-start(bf16[512,384]{1,0:T(8,128)(2,1)} %get-tuple-element.127), channel_id=1, source_target_pairs={{0,5},{1,4},{2,7},{3,6},{4,1},{5,0},{6,3},{7,2},{8,13},{9,12},{10,... | collective-permute-start | bytes 1179656 | tf_op jit(solution)/shard_map/ppermute | solution.py:90
  70.8 28.8 %copy-start.3 = (bf16[64,64,64]{2,1,0:T(8,128)(2,1)S(1)}, bf16[64,64,64]{2,1,0:T(8,128)(2,1)}, u32[]{:S(2)}) copy-start(bf16[64,64,64]{2,1,0:T(8,128)(2,1)} %refs_16_.1) | copy-start | bytes 1572868
  76.9 13.9 %collective-permute-start.10 = (bf16[512,384]{1,0:T(8,128)(2,1)}, bf16[512,384]{1,0:T(8,128)(2,1)S(1)}, u32[]{:S(2)}, u32[]{:S(2)}) collective-permute-start(bf16[512,384]{1,0:T(8,128)(2,1)} %get-tuple-element.133), channel_id=1, source_target_pairs={{0,4},{1,5},{2,6},{3,7},{4,0},{5,1},{6,2},{7,3},{8,12},{9,13},{10,... | collective-permute-start | bytes 1179656 | tf_op jit(solution)/shard_map/ppermute | solution.py:90
  79.0 19.8 %collective-permute-start.11 = (bf16[512,384]{1,0:T(8,128)(2,1)}, bf16[512,384]{1,0:T(8,128)(2,1)S(1)}, u32[]{:S(2)}, u32[]{:S(2)}) collective-permute-start(bf16[512,384]{1,0:T(8,128)(2,1)} %get-tuple-element.134), channel_id=1, source_target_pairs={{0,5},{1,4},{2,7},{3,6},{4,1},{5,0},{6,3},{7,2},{8,13},{9,12},{10,... | collective-permute-start | bytes 1179656 | tf_op jit(solution)/shard_map/ppermute | solution.py:90
  80.6 26.8 %collective-permute-start.12 = (bf16[512,384]{1,0:T(8,128)(2,1)}, bf16[512,384]{1,0:T(8,128)(2,1)S(1)}, u32[]{:S(2)}, u32[]{:S(2)}) collective-permute-start(bf16[512,384]{1,0:T(8,128)(2,1)} %get-tuple-element.135), channel_id=1, source_target_pairs={{0,6},{1,7},{2,4},{3,5},{4,2},{5,3},{6,0},{7,1},{8,14},{9,15},{10,... | collective-permute-start | bytes 1179656 | tf_op jit(solution)/shard_map/ppermute | solution.py:90
  83.6 32.1 %collective-permute-start.13 = (bf16[512,384]{1,0:T(8,128)(2,1)}, bf16[512,384]{1,0:T(8,128)(2,1)S(1)}, u32[]{:S(2)}, u32[]{:S(2)}) collective-permute-start(bf16[512,384]{1,0:T(8,128)(2,1)} %get-tuple-element.136), channel_id=1, source_target_pairs={{0,7},{1,6},{2,5},{3,4},{4,3},{5,2},{6,1},{7,0},{8,15},{9,14},{10,... | collective-permute-start | bytes 1179656 | tf_op jit(solution)/shard_map/ppermute | solution.py:90
  83.6 32.1 %collective-permute-start.7 = (bf16[512,384]{1,0:T(8,128)(2,1)}, bf16[512,384]{1,0:T(8,128)(2,1)}, u32[]{:S(2)}, u32[]{:S(2)}) collective-permute-start(bf16[512,384]{1,0:T(8,128)(2,1)} %get-tuple-element.130), channel_id=1, source_target_pairs={{0,1},{1,0},{2,3},{3,2},{4,5},{5,4},{6,7},{7,6},{8,9},{9,8},{10,11... | collective-permute-start | bytes 1179656 | tf_op jit(solution)/shard_map/ppermute | solution.py:90
  90.8 24.9 %collective-permute-start.8 = (bf16[512,384]{1,0:T(8,128)(2,1)}, bf16[512,384]{1,0:T(8,128)(2,1)}, u32[]{:S(2)}, u32[]{:S(2)}) collective-permute-start(bf16[512,384]{1,0:T(8,128)(2,1)} %get-tuple-element.131), channel_id=1, source_target_pairs={{0,2},{1,3},{2,0},{3,1},{4,6},{5,7},{6,4},{7,5},{8,10},{9,11},{10,... | collective-permute-start | bytes 1179656 | tf_op jit(solution)/shard_map/ppermute | solution.py:90
  98.8 17.2 %collective-permute-start.9 = (bf16[512,384]{1,0:T(8,128)(2,1)}, bf16[512,384]{1,0:T(8,128)(2,1)}, u32[]{:S(2)}, u32[]{:S(2)}) collective-permute-start(bf16[512,384]{1,0:T(8,128)(2,1)} %get-tuple-element.132), channel_id=1, source_target_pairs={{0,3},{1,2},{2,1},{3,0},{4,7},{5,6},{6,5},{7,4},{8,11},{9,10},{10,... | collective-permute-start | bytes 1179656 | tf_op jit(solution)/shard_map/ppermute | solution.py:90
  133.3 13.4 %collective-permute-start.14 = (bf16[512,384]{1,0:T(8,128)(2,1)}, bf16[512,384]{1,0:T(8,128)(2,1)S(1)}, u32[]{:S(2)}, u32[]{:S(2)}) collective-permute-start(bf16[512,384]{1,0:T(8,128)(2,1)} %get-tuple-element.159), channel_id=1, source_target_pairs={{0,1},{1,0},{2,3},{3,2},{4,5},{5,4},{6,7},{7,6},{8,9},{9,8},{10,11... | collective-permute-start | bytes 1179656 | tf_op jit(solution)/shard_map/ppermute | solution.py:90
  133.5 13.3 %collective-permute-start.15 = (bf16[512,384]{1,0:T(8,128)(2,1)}, bf16[512,384]{1,0:T(8,128)(2,1)S(1)}, u32[]{:S(2)}, u32[]{:S(2)}) collective-permute-start(bf16[512,384]{1,0:T(8,128)(2,1)} %get-tuple-element.160), channel_id=1, source_target_pairs={{0,2},{1,3},{2,0},{3,1},{4,6},{5,7},{6,4},{7,5},{8,10},{9,11},{10,... | collective-permute-start | bytes 1179656 | tf_op jit(solution)/shard_map/ppermute | solution.py:90
  134.1 12.7 %collective-permute-start.16 = (bf16[512,384]{1,0:T(8,128)(2,1)}, bf16[512,384]{1,0:T(8,128)(2,1)}, u32[]{:S(2)}, u32[]{:S(2)}) collective-permute-start(bf16[512,384]{1,0:T(8,128)(2,1)} %get-tuple-element.161), channel_id=1, source_target_pairs={{0,6},{1,7},{2,4},{3,5},{4,2},{5,3},{6,0},{7,1},{8,14},{9,15},{10,... | collective-permute-start | bytes 1179656 | tf_op jit(solution)/shard_map/ppermute | solution.py:90
  147.6 24.7 %all-to-all-start.2 = ((bf16[16,256,128]{2,1,0:T(8,128)(2,1)}), bf16[16,256,128]{2,1,0:T(8,128)(2,1)S(1)}, u32[]{:S(2)}, u32[]{:S(2)}) async-start(bf16[16,256,128]{2,1,0:T(8,128)(2,1)} %bitcast.90), calls=%async_computation.2 | async-start | bytes 2097152 | tf_op jit(solution)/shard_map/all_to_all | solution.py:30
  154.5 18.0 %collective-permute-start.17 = (bf16[512,384]{1,0:T(8,128)(2,1)}, bf16[512,384]{1,0:T(8,128)(2,1)S(1)}, u32[]{:S(2)}, u32[]{:S(2)}) collective-permute-start(bf16[512,384]{1,0:T(8,128)(2,1)} %get-tuple-element.165), channel_id=1, source_target_pairs={{0,3},{1,2},{2,1},{3,0},{4,7},{5,6},{6,5},{7,4},{8,11},{9,10},{10,... | collective-permute-start | bytes 1179656 | tf_op jit(solution)/shard_map/ppermute | solution.py:90
  155.1 20.0 %collective-permute-start.18 = (bf16[512,384]{1,0:T(8,128)(2,1)}, bf16[512,384]{1,0:T(8,128)(2,1)}, u32[]{:S(2)}, u32[]{:S(2)}) collective-permute-start(bf16[512,384]{1,0:T(8,128)(2,1)} %get-tuple-element.166), channel_id=1, source_target_pairs={{0,4},{1,5},{2,6},{3,7},{4,0},{5,1},{6,2},{7,3},{8,12},{9,13},{10,... | collective-permute-start | bytes 1179656 | tf_op jit(solution)/shard_map/ppermute | solution.py:90
  156.8 20.2 %collective-permute-start.19 = (bf16[512,384]{1,0:T(8,128)(2,1)}, bf16[512,384]{1,0:T(8,128)(2,1)}, u32[]{:S(2)}, u32[]{:S(2)}) collective-permute-start(bf16[512,384]{1,0:T(8,128)(2,1)} %get-tuple-element.167), channel_id=1, source_target_pairs={{0,7},{1,6},{2,5},{3,4},{4,3},{5,2},{6,1},{7,0},{8,15},{9,14},{10,... | collective-permute-start | bytes 1179656 | tf_op jit(solution)/shard_map/ppermute | solution.py:90
  172.4 34.4 %copy-start.4 = (bf16[8,512,128]{2,1,0:T(8,128)(2,1)S(1)}, bf16[8,512,128]{2,1,0:T(8,128)(2,1)}, u32[]{:S(2)}) copy-start(bf16[8,512,128]{2,1,0:T(8,128)(2,1)} %w_ref.1) | copy-start | bytes 3145732
  178.1 27.6 %all-to-all-start.3 = ((bf16[16,256,128]{2,1,0:T(8,128)(2,1)}), bf16[16,256,128]{2,1,0:T(8,128)(2,1)S(1)}, u32[]{:S(2)}, u32[]{:S(2)}) async-start(bf16[16,256,128]{2,1,0:T(8,128)(2,1)} %broadcast_in_dim.12), calls=%async_computation.3 | async-start | bytes 2097152 | tf_op jit(solution)/shard_map/all_to_all | solution.py:37
  184.8 12.1 %collective-permute-start.20 = (bf16[512,384]{1,0:T(8,128)(2,1)}, bf16[512,384]{1,0:T(8,128)(2,1)}, u32[]{:S(2)}, u32[]{:S(2)}) collective-permute-start(bf16[512,384]{1,0:T(8,128)(2,1)} %get-tuple-element.171), channel_id=1, source_target_pairs={{0,5},{1,4},{2,7},{3,6},{4,1},{5,0},{6,3},{7,2},{8,13},{9,12},{10,... | collective-permute-start | bytes 1179656 | tf_op jit(solution)/shard_map/ppermute | solution.py:90
  205.7 12.0 %collective-permute-start.21 = (bf16[512,384]{1,0:T(8,128)(2,1)}, bf16[512,384]{1,0:T(8,128)(2,1)S(1)}, u32[]{:S(2)}, u32[]{:S(2)}) collective-permute-start(bf16[512,384]{1,0:T(8,128)(2,1)} %get-tuple-element.185), channel_id=1, source_target_pairs={{0,2},{1,3},{2,0},{3,1},{4,6},{5,7},{6,4},{7,5},{8,10},{9,11},{10,... | collective-permute-start | bytes 1179656 | tf_op jit(solution)/shard_map/ppermute | solution.py:90
  205.7 12.7 %collective-permute-start.22 = (bf16[512,384]{1,0:T(8,128)(2,1)}, bf16[512,384]{1,0:T(8,128)(2,1)}, u32[]{:S(2)}, u32[]{:S(2)}) collective-permute-start(bf16[512,384]{1,0:T(8,128)(2,1)} %get-tuple-element.186), channel_id=1, source_target_pairs={{0,6},{1,7},{2,4},{3,5},{4,2},{5,3},{6,0},{7,1},{8,14},{9,15},{10,... | collective-permute-start | bytes 1179656 | tf_op jit(solution)/shard_map/ppermute | solution.py:90
  221.2 21.0 %all-to-all-start.4 = ((bf16[3,128,1024]{2,0,1:T(4,128)(2,1)}), bf16[3,128,1024]{2,0,1:T(4,128)(2,1)S(1)}, u32[]{:S(2)}, u32[]{:S(2)}) async-start(bf16[3,128,1024]{2,0,1:T(4,128)(2,1)} %copy.86), calls=%async_computation.4 | async-start | bytes 2097152 | tf_op jit(solution)/shard_map/all_to_all | solution.py:362
  224.8 17.7 %collective-permute-start.23 = (bf16[512,384]{1,0:T(8,128)(2,1)}, bf16[512,384]{1,0:T(8,128)(2,1)S(1)}, u32[]{:S(2)}, u32[]{:S(2)}) collective-permute-start(bf16[512,384]{1,0:T(8,128)(2,1)} %get-tuple-element.188), channel_id=1, source_target_pairs={{0,3},{1,2},{2,1},{3,0},{4,7},{5,6},{6,5},{7,4},{8,11},{9,10},{10,... | collective-permute-start | bytes 1179656 | tf_op jit(solution)/shard_map/ppermute | solution.py:90
  224.9 21.3 %collective-permute-start.24 = (bf16[512,384]{1,0:T(8,128)(2,1)}, bf16[512,384]{1,0:T(8,128)(2,1)}, u32[]{:S(2)}, u32[]{:S(2)}) collective-permute-start(bf16[512,384]{1,0:T(8,128)(2,1)} %get-tuple-element.189), channel_id=1, source_target_pairs={{0,4},{1,5},{2,6},{3,7},{4,0},{5,1},{6,2},{7,3},{8,12},{9,13},{10,... | collective-permute-start | bytes 1179656 | tf_op jit(solution)/shard_map/ppermute | solution.py:90
  227.5 20.9 %collective-permute-start.25 = (bf16[512,384]{1,0:T(8,128)(2,1)}, bf16[512,384]{1,0:T(8,128)(2,1)}, u32[]{:S(2)}, u32[]{:S(2)}) collective-permute-start(bf16[512,384]{1,0:T(8,128)(2,1)} %get-tuple-element.190), channel_id=1, source_target_pairs={{0,7},{1,6},{2,5},{3,4},{4,3},{5,2},{6,1},{7,0},{8,15},{9,14},{10,... | collective-permute-start | bytes 1179656 | tf_op jit(solution)/shard_map/ppermute | solution.py:90
  250.8 21.9 %all-to-all-start.5 = ((bf16[48,8,1024]{2,1,0:T(8,128)(2,1)}), bf16[48,8,1024]{2,1,0:T(8,128)(2,1)S(1)}, u32[]{:S(2)}, u32[]{:S(2)}) async-start(bf16[48,8,1024]{2,1,0:T(8,128)(2,1)} %copy.91), calls=%async_computation.5 | async-start | bytes 1572864 | tf_op jit(solution)/shard_map/all_to_all | solution.py:367
  258.0 14.8 %collective-permute-start.26 = (bf16[512,384]{1,0:T(8,128)(2,1)}, bf16[512,384]{1,0:T(8,128)(2,1)}, u32[]{:S(2)}, u32[]{:S(2)}) collective-permute-start(bf16[512,384]{1,0:T(8,128)(2,1)} %get-tuple-element.192), channel_id=1, source_target_pairs={{0,1},{1,0},{2,3},{3,2},{4,5},{5,4},{6,7},{7,6},{8,9},{9,8},{10,11... | collective-permute-start | bytes 1179656 | tf_op jit(solution)/shard_map/ppermute | solution.py:90
  258.0 14.8 %collective-permute-start.27 = (bf16[512,384]{1,0:T(8,128)(2,1)}, bf16[512,384]{1,0:T(8,128)(2,1)}, u32[]{:S(2)}, u32[]{:S(2)}) collective-permute-start(bf16[512,384]{1,0:T(8,128)(2,1)} %get-tuple-element.193), channel_id=1, source_target_pairs={{0,5},{1,4},{2,7},{3,6},{4,1},{5,0},{6,3},{7,2},{8,13},{9,12},{10,... | collective-permute-start | bytes 1179656 | tf_op jit(solution)/shard_map/ppermute | solution.py:90
  272.8 24.0 %all-to-all-start.6 = ((bf16[16,264,128]{2,1,0:T(8,128)(2,1)}), bf16[16,264,128]{2,1,0:T(8,128)(2,1)}, u32[]{:S(2)}, u32[]{:S(2)}) async-start(bf16[16,264,128]{2,1,0:T(8,128)(2,1)} %get-tuple-element.206), calls=%async_computation.6 | async-start | bytes 2162688 | tf_op jit(solution)/shard_map/all_to_all | solution.py:30
  287.1 16.0 %copy-start.6 = (bf16[16,3,8,1024]{3,2,1,0:T(8,128)(2,1)S(1)}, bf16[16,3,8,1024]{3,2,1,0:T(8,128)(2,1)}, u32[]{:S(2)}) copy-start(bf16[16,3,8,1024]{3,2,1,0:T(8,128)(2,1)} %copy-done.5) | copy-start | bytes 2359300
  298.8 20.8 %all-to-all-start.7 = ((bf16[16,64,512]{2,1,0:T(8,128)(2,1)}), bf16[16,64,512]{2,1,0:T(8,128)(2,1)}, u32[]{:S(2)}, u32[]{:S(2)}) async-start(bf16[16,64,512]{2,1,0:T(8,128)(2,1)} %bitcast.91), calls=%async_computation.7 | async-start | bytes 2097152 | tf_op jit(solution)/shard_map/all_to_all | solution.py:30
  322.1 20.5 %all-to-all-start.9 = ((bf16[16,64,512]{2,1,0:T(8,128)(2,1)}), bf16[16,64,512]{2,1,0:T(8,128)(2,1)}, u32[]{:S(2)}, u32[]{:S(2)}) async-start(bf16[16,64,512]{2,1,0:T(8,128)(2,1)} %broadcast_in_dim.33), calls=%async_computation.9 | async-start | bytes 2097152 | tf_op jit(solution)/shard_map/all_to_all | solution.py:37
  326.5 1.4 collective-permute-start.28
  328.0 7.3 %collective-permute-start.29 = (f32[264,128]{1,0:T(8,128)S(1)}, f32[264,128]{1,0:T(8,128)S(1)}, u32[]{:S(2)}, u32[]{:S(2)}) collective-permute-start(f32[264,128]{1,0:T(8,128)S(1)} %bitcast_add_fusion.1), channel_id=1, source_target_pairs={{0,2},{1,3},{2,0},{3,1},{4,6},{5,7},{6,4},{7,5},{8,10},{9,11},{10,... | collective-permute-start | bytes 405512 | tf_op jit(solution)/shard_map/ppermute | solution.py:51
  328.0 8.2 %collective-permute-start.30 = (f32[264,128]{1,0:T(8,128)S(1)}, f32[264,128]{1,0:T(8,128)S(1)}, u32[]{:S(2)}, u32[]{:S(2)}) collective-permute-start(f32[264,128]{1,0:T(8,128)S(1)} %bitcast_add_fusion.1), channel_id=1, source_target_pairs={{0,4},{1,5},{2,6},{3,7},{4,0},{5,1},{6,2},{7,3},{8,12},{9,13},{10,... | collective-permute-start | bytes 405512 | tf_op jit(solution)/shard_map/ppermute | solution.py:51
  329.6 9.0 %collective-permute-start.31 = (f32[264,128]{1,0:T(8,128)S(1)}, f32[264,128]{1,0:T(8,128)S(1)}, u32[]{:S(2)}, u32[]{:S(2)}) collective-permute-start(f32[264,128]{1,0:T(8,128)S(1)} %bitcast_add_fusion.1), channel_id=1, source_target_pairs={{0,6},{1,7},{2,4},{3,5},{4,2},{5,3},{6,0},{7,1},{8,14},{9,15},{10,... | collective-permute-start | bytes 405512 | tf_op jit(solution)/shard_map/ppermute | solution.py:51
  338.7 11.5 %collective-permute-start.32 = (f32[264,128]{1,0:T(8,128)S(1)}, f32[264,128]{1,0:T(8,128)S(1)}, u32[]{:S(2)}, u32[]{:S(2)}) collective-permute-start(f32[264,128]{1,0:T(8,128)S(1)} %add_add_fusion), channel_id=1, source_target_pairs={{0,1},{1,0},{2,3},{3,2},{4,5},{5,4},{6,7},{7,6},{8,9},{9,8},{10,11... | collective-permute-start | bytes 405512 | tf_op jit(solution)/shard_map/ppermute | solution.py:52
  343.8 21.9 %all-to-all-start.8 = ((bf16[16,264,128]{2,1,0:T(8,128)(2,1)}), bf16[16,264,128]{2,1,0:T(8,128)(2,1)S(1)}, u32[]{:S(2)}, u32[]{:S(2)}) async-start(bf16[16,264,128]{2,1,0:T(8,128)(2,1)} %broadcast_in_dim.32), calls=%async_computation.8 | async-start | bytes 2162688 | tf_op jit(solution)/shard_map/all_to_all | solution.py:37
  (23 other events, 129.6 us)

commit v2 on v1

--- a/solution.py
+++ b/solution.py
@@ -25,10 +25,14 @@
     return jnp.einsum(form, left_arg, right_arg, preferred_element_type=F32)
 
 
-def sum_slice(parts):
+def slice_parts(parts):
     n = lax.axis_size("dp")
-    mine = lax.all_to_all(parts.reshape(n, -1, parts.shape[-1]), "dp", split_axis=0, concat_axis=0, tiled=True)
-    return jnp.sum(mine.astype(F32), axis=0)
+    parts = parts.reshape(n, -1, parts.shape[-1])
+    return lax.all_to_all(parts, "dp", split_axis=0, concat_axis=0, tiled=True)
+
+
+def add_parts(parts, scale):
+    return jnp.sum(parts.astype(F32), axis=0) * scale
 
 
 def all_slices(piece):
@@ -335,14 +339,9 @@
     back_a1 = send(pieces, 2, 6, 1)
     pieces_c, part_left = middle_rest(x, back, hid, back_pre, left_two, n_mp, me1)
     part_left, back_a1 = together(part_left, back_a1)
-    back_a2 = send(pieces, 3, 7, 4)
-    slice_left = (sum_slice(part_left) * scale_rows).astype(BF)
-    slice_left, back_a2 = together(slice_left, back_a2)
-    back_a3 = send(pieces, 5)
-    sum_left = all_slices(slice_left)
-    sum_left, back_a3 = together(sum_left, back_a3)
-    sum_left = sum_left.astype(F32).reshape(part_left.shape)
-    back_a = in_order(pieces, back_a1, back_a2, back_a3)
+    back_a2 = send(pieces, 3, 7, 4, 5)
+    back_a = in_order(pieces, back_a1, back_a2)
+    left_parts = slice_parts(part_left)
 
     pieces_c, back_a = together(pieces_c, back_a)
     act_c1 = send(pieces_c, 2, 6)
@@ -355,29 +354,37 @@
         jnp.swapaxes(right_one, 1, 2),
         me1,
     )
-    back_mixed, act_c1 = together(back_mixed, act_c1)
+    back_mixed, act_c1, left_parts = together(back_mixed, act_c1, left_parts)
     back_z = back_z.reshape(blocks_here, block_len, cols_here)
     back_mixed = back_mixed.reshape(blocks_here, block_len, cols_here)
-    act_c2 = send(pieces_c, 3, 7, 4)
+    act_c2 = send(pieces_c, 3, 7)
     back_mixed_moved = lax.all_to_all(back_mixed, "dp", split_axis=1, concat_axis=0, tiled=True)
-    back_mixed_moved, act_c2 = together(back_mixed_moved, act_c2)
+    back_mixed_moved, act_c2, part_r1 = together(back_mixed_moved, act_c2, part_r1)
     back_first_moved = product("isk,sic->kic", seq_left, back_mixed_moved).astype(BF)
     part_seq_left = product("sic,kic->isk", back_mixed_moved, first_moved)
-    act_c3 = send(pieces_c, 5, 1)
+    act_c3 = send(pieces_c, 4, 1)
+    r1_parts = slice_parts(part_r1)
+    back_first_moved, r1_parts, act_c3 = together(back_first_moved, r1_parts, act_c3)
+    act_c4 = send(pieces_c, 5)
     back_first = lax.all_to_all(back_first_moved, "dp", split_axis=0, concat_axis=1, tiled=True)
-    back_first, act_c3 = together(back_first, act_c3)
-    act_c = in_order(pieces_c, act_c1, act_c2, act_c3)
-
-    part_r1, back_first = together(part_r1, back_first)
-    slice_r1 = sum_slice(part_r1)
-    output, part_r2 = output_side(act_c, zed, cotangent, right_two, me1)
-    slice_r1, part_r2 = together(slice_r1, part_r2)
+    act_c = in_order(pieces_c, act_c1, act_c2, act_c3, act_c4)
+    slice_left = add_parts(left_parts, scale_rows)
+    slice_r1 = add_parts(r1_parts, scale_rows)
     half = right_one.shape[1] // 2
     slice_gain = slice_r1[half : half + 1] + slice_r1[half + 1 : half + 2]
-    slice_r1 = jnp.concatenate([slice_r1[:half], jnp.broadcast_to(slice_gain, (8, block_len))])
-    slice_r2 = sum_slice(part_r2)
-    slice_r1, slice_r2 = together((slice_r1 * scale_rows).astype(BF), (slice_r2 * scale_rows).astype(BF))
-    sum_r1 = all_slices(slice_r1).astype(F32)
+    slice_gain = jnp.broadcast_to(slice_gain, (8, block_len))
+    slices = jnp.concatenate([slice_left, slice_r1[:half], slice_gain]).astype(BF)
+    rows_left = slice_left.shape[0]
+    gathered = lax.all_gather(slices, "dp")
+
+    output, part_r2 = output_side(act_c, zed, cotangent, right_two, me1)
+    back_first, part_r2 = together(back_first, part_r2)
+    slice_r2 = add_parts(slice_parts(part_r2), scale_rows).astype(BF)
+    slice_r2, gathered = together(slice_r2, gathered)
+    gathered = gathered.astype(F32)
+    sum_left = gathered[:, :rows_left].reshape(part_left.shape)
+    sum_r1 = gathered[:, rows_left : rows_left + half].reshape(right_one.shape)
+    sum_gain = gathered[::2, rows_left + half].reshape(cols_here)
     sum_r2 = all_slices(slice_r2).astype(F32)
 
     grad_tokens = (back_z + product("sij,sic->sjc", seq_right, back_first)).astype(BF)
@@ -391,8 +398,8 @@
         grad_tokens.reshape(rows_here, cols_here),
         seq_sum[:seq_rows].reshape(part_seq_right.shape) * scale_cols,
         seq_sum[seq_rows:].reshape(part_seq_left.shape) * scale_cols,
-        sum_r1[::2, half].reshape(cols_here),
-        sum_r1[:, :half].reshape(right_one.shape),
+        sum_gain,
+        sum_r1,
         sum_left[:, :, : left_one.shape[2]],
         sum_left[:, :, left_one.shape[2] :],
         sum_r2.reshape(right_two.shape),

time: 370 us -> 347 us (0.938)
  waiting for transfers between devices: 175 us -> 153 us
  between operations: 1.26 us -> 14.6 us
  starting transfers between devices: 93 us -> 83.8 us
    ppermute x28, waiting for transfers between devices: 58.8 us -> 85.6 us  [send(): lax.ppermute(pieces[d], 'mp', [(i, i ^ d) for i in range(n)])]
    all_to_all x3, waiting for transfers between devices: 35.3 us -> 10.4 us  [slice_parts(): return lax.all_to_all(parts, 'dp', split_axis=0, concat_axis=0, tiled=True)]
    all_to_all x1, waiting for transfers between devices: 14.6 us -> 0.01 us  [per_device(): lax.all_to_all(back_first_moved, 'dp', split_axis=0, concat_axis=1, tiled...]
    all_to_all x3 -> x1, waiting for transfers between devices: 23.8 us -> 9.56 us  [all_slices(): return lax.all_to_all(copies, 'dp', split_axis=0, concat_axis=0, tiled=True)]
    all_to_all x3 -> x1, starting transfers between devices: 14.7 us -> 3.84 us  [all_slices(): return lax.all_to_all(copies, 'dp', split_axis=0, concat_axis=0, tiled=True)]
    unnamed x58 -> x62, local copies, waits for them, and re-layouts: 8.6 us -> 9.21 us
  transfers between devices with their start and end apart: 43 -> 42, of which waited for: 28 -> 25; matrix products, arithmetic and copies ran while one was open for 6% -> 7% of each run, Pallas kernels for 8% -> 8%
where the time goes in v2:
time: 347 us; the launch traced here: 346 us
  waiting for transfers between devices  153 us (44%)
  starting transfers between devices  83.8 us (24%)
  Pallas kernels  55.4 us (16%)
  local copies, waits for them, and re-layouts  26 us (7%)
  between operations  14.6 us (4%)
  matrix products  7.76 us (2%)
  other arithmetic  5.36 us (2%)
    ppermute x28, waiting for transfers between devices, send(): lax.ppermute(pieces[d], 'mp', [(i, i ^ d) for i in range(n)])  85.6 us
    ppermute x28, starting transfers between devices, send(): lax.ppermute(pieces[d], 'mp', [(i, i ^ d) for i in range(n)])  31.4 us
    all_to_all x3, starting transfers between devices, slice_parts(): return lax.all_to_all(parts, 'dp', split_axis=0, concat_axis=0, tiled=True)  17.3 us
    pallas_call x1, Pallas kernels, middle_main(): pl.pallas_call(body, grid=(units // STEP,), in_specs=[pl.BlockSpec(memory...  16.9 us
    all_to_all x1, waiting for transfers between devices, per_device(): lax.all_to_all(back_mixed, 'dp', split_axis=1, concat_axis=0, tiled=True)  15.6 us
    all_to_all x1, waiting for transfers between devices, per_device(): lax.all_to_all(first, 'dp', split_axis=1, concat_axis=0, tiled=True)  12.7 us
    all_to_all x1, waiting for transfers between devices, per_device(): lax.all_to_all(mixed_moved, 'dp', split_axis=0, concat_axis=1, tiled=True)  11.9 us
    all_to_all x3, waiting for transfers between devices, slice_parts(): return lax.all_to_all(parts, 'dp', split_axis=0, concat_axis=0, tiled=True)  10.4 us
  transfers between devices with their start and end apart: 42, of which 25 were waited for; matrix products, arithmetic and copies ran while one was open for 7% of the time, Pallas kernels for 8%

profile of v2, /device:TPU:0, one launch (start us, length us, event | category | flops | bytes accessed | tf_op | source)
XLA Modules:
  0.0 345.6 jit_solution(18268754337749498444)
XLA Ops:
  7.2 2.3 copy.76
  9.9 4.9 %expand.2 = (bf16[512,384]{1,0:T(8,128)(2,1)}, bf16[512,384]{1,0:T(8,128)(2,1)}, bf16[512,384]{1,0:T(8,128)(2,1)}, bf16[512,384]{1,0:T(8,128)(2,1)}, bf16[512,38...) custom-call(s32[1]{0:T(128)} %bitcast.me_ref, ...), custom_call_target="tpu_custom_call" | custom-call | tf_op jit(solution)/shard_map/expand/pallas_call | solution.py:81
  16.5 8.0 %all-to-all-start = ((bf16[3,128,1024]{2,0,1:T(4,128)(2,1)}), bf16[3,128,1024]{2,0,1:T(4,128)(2,1)S(1)}, u32[]{:S(2)}, u32[]{:S(2)}) async-start(bf16[3,128,1024]{2,0,1:T(4,128)(2,1)} %copy.77), calls=%async_computation | async-start | bytes 2097152 | tf_op jit(solution)/shard_map/all_to_all | solution.py:324
  26.4 3.0 collective-permute-start.3
  29.5 12.7 %all-to-all-done = bf16[3,128,1024]{2,0,1:T(4,128)(2,1)S(1)} async-done(((bf16[3,128,1024]{2,0,1:T(4,128)(2,1)}), bf16[3,128,1024]{2,0,1:T(4,128)(2,1)S(1)}, u32[]{:S(2)}, u32[]{:S(2)}) %all-to-all-start) | async-done | bytes 786464 | tf_op jit(solution)/shard_map/all_to_all | solution.py:324
  44.3 3.1 collective-permute-done.4.refs_15_
  49.8 7.2 %all-to-all-start.1 = ((bf16[48,8,1024]{2,1,0:T(8,128)(2,1)}), bf16[48,8,1024]{2,1,0:T(8,128)(2,1)S(1)}, u32[]{:S(2)}, u32[]{:S(2)}) async-start(bf16[48,8,1024]{2,1,0:T(8,128)(2,1)} %copy.81), calls=%async_computation.1 | async-start | bytes 1572864 | tf_op jit(solution)/shard_map/all_to_all | solution.py:328
  59.9 11.9 %all-to-all-done.1 = bf16[48,8,1024]{2,1,0:T(8,128)(2,1)S(1)} async-done(((bf16[48,8,1024]{2,1,0:T(8,128)(2,1)}), bf16[48,8,1024]{2,1,0:T(8,128)(2,1)S(1)}, u32[]{:S(2)}, u32[]{:S(2)}) %all-to-all-start.1) | async-done | bytes 786464 | tf_op jit(solution)/shard_map/all_to_all | solution.py:328
  71.9 5.4 %collective-permute-done.6.refs_13_ = bf16[512,384]{1,0:T(8,128)(2,1)S(1)} collective-permute-done((bf16[512,384]{1,0:T(8,128)(2,1)}, bf16[512,384]{1,0:T(8,128)(2,1)S(1)}, u32[]{:S(2)}, u32[]{:S(2)}) %collective-permute-start.6) | collective-permute-done | bytes 393248 | tf_op jit(solution)/shard_map/ppermute | solution.py:94
  78.5 4.9 %expand.3 = (bf16[512,384]{1,0:T(8,128)(2,1)}, bf16[512,384]{1,0:T(8,128)(2,1)}, bf16[512,384]{1,0:T(8,128)(2,1)}, bf16[512,384]{1,0:T(8,128)(2,1)}, bf16[512,38...) custom-call(s32[1]{0:T(128)} %bitcast.me_ref, ...), custom_call_target="tpu_custom_call" | custom-call | tf_op jit(solution)/shard_map/expand/pallas_call | solution.py:81
  83.4 2.1 collective-permute-start.10
  87.1 3.0 collective-permute-start.12
  90.5 6.8 %collective-permute-done.10.refs_4_ = bf16[512,384]{1,0:T(8,128)(2,1)S(1)} collective-permute-done((bf16[512,384]{1,0:T(8,128)(2,1)}, bf16[512,384]{1,0:T(8,128)(2,1)S(1)}, u32[]{:S(2)}, u32[]{:S(2)}) %collective-permute-start.10) | collective-permute-done | bytes 393248 | tf_op jit(solution)/shard_map/ppermute | solution.py:94
  98.3 7.0 %collective-permute-done.11.refs_5_ = bf16[512,384]{1,0:T(8,128)(2,1)S(1)} collective-permute-done((bf16[512,384]{1,0:T(8,128)(2,1)}, bf16[512,384]{1,0:T(8,128)(2,1)S(1)}, u32[]{:S(2)}, u32[]{:S(2)}) %collective-permute-start.11) | collective-permute-done | bytes 393248 | tf_op jit(solution)/shard_map/ppermute | solution.py:94
  107.4 2.3 copy.84
  109.6 4.3 %collective-permute-done.12.refs_6_ = bf16[512,384]{1,0:T(8,128)(2,1)S(1)} collective-permute-done((bf16[512,384]{1,0:T(8,128)(2,1)}, bf16[512,384]{1,0:T(8,128)(2,1)S(1)}, u32[]{:S(2)}, u32[]{:S(2)}) %collective-permute-start.12) | collective-permute-done | bytes 393248 | tf_op jit(solution)/shard_map/ppermute | solution.py:94
  113.9 8.3 %collective-permute-done.13.refs_7_ = bf16[512,384]{1,0:T(8,128)(2,1)S(1)} collective-permute-done((bf16[512,384]{1,0:T(8,128)(2,1)}, bf16[512,384]{1,0:T(8,128)(2,1)S(1)}, u32[]{:S(2)}, u32[]{:S(2)}) %collective-permute-start.13) | collective-permute-done | bytes 393248 | tf_op jit(solution)/shard_map/ppermute | solution.py:94
  122.9 16.9 %middle_main.1 = (bf16[512,384]{1,0:T(8,128)(2,1)}, bf16[512,384]{1,0:T(8,128)(2,1)}, bf16[512,384]{1,0:T(8,128)(2,1)}, bf16[512,384]{1,0:T(8,128)(2,1)}, bf16[5...) custom-call(s32[1]{0:T(128)} %bitcast.me_ref, ...), custom_call_target="tpu_custom_call" | custom-call | tf_op jit(solution)/shard_map/middle_main/pallas_call | solution.py:159
  140.7 2.5 collective-permute-start.16
  143.2 10.0 %middle_rest.1 = (bf16[512,384]{1,0:T(8,128)(2,1)}, bf16[512,384]{1,0:T(8,128)(2,1)}, bf16[512,384]{1,0:T(8,128)(2,1)}, bf16[512,384]{1,0:T(8,128)(2,1)}, bf16[5...) custom-call(s32[1]{0:T(128)} %bitcast.me_ref, ...), custom_call_target="tpu_custom_call" | custom-call | tf_op jit(solution)/shard_map/middle_rest/pallas_call | solution.py:190
  153.4 7.0 %all-to-all-start.2 = ((bf16[16,256,128]{2,1,0:T(8,128)(2,1)}), bf16[16,256,128]{2,1,0:T(8,128)(2,1)S(1)}, u32[]{:S(2)}, u32[]{:S(2)}) async-start(bf16[16,256,128]{2,1,0:T(8,128)(2,1)} %bitcast.94), calls=%async_computation.2 | async-start | bytes 2097152 | tf_op jit(solution)/shard_map/all_to_all | solution.py:31
  160.9 2.4 collective-permute-start.18
  166.3 5.7 %collective-permute-done.17.refs_3_ = bf16[512,384]{1,0:T(8,128)(2,1)S(1)} collective-permute-done((bf16[512,384]{1,0:T(8,128)(2,1)}, bf16[512,384]{1,0:T(8,128)(2,1)S(1)}, u32[]{:S(2)}, u32[]{:S(2)}) %collective-permute-start.17) | collective-permute-done | bytes 393248 | tf_op jit(solution)/shard_map/ppermute | solution.py:94
  172.1 9.4 %collective-permute-done.18.refs_4_ = bf16[512,384]{1,0:T(8,128)(2,1)S(1)} collective-permute-done((bf16[512,384]{1,0:T(8,128)(2,1)}, bf16[512,384]{1,0:T(8,128)(2,1)S(1)}, u32[]{:S(2)}, u32[]{:S(2)}) %collective-permute-start.18) | collective-permute-done | bytes 393248 | tf_op jit(solution)/shard_map/ppermute | solution.py:94
  181.5 9.0 %collective-permute-done.19.refs_5_ = bf16[512,384]{1,0:T(8,128)(2,1)S(1)} collective-permute-done((bf16[512,384]{1,0:T(8,128)(2,1)}, bf16[512,384]{1,0:T(8,128)(2,1)S(1)}, u32[]{:S(2)}, u32[]{:S(2)}) %collective-permute-start.19) | collective-permute-done | bytes 393248 | tf_op jit(solution)/shard_map/ppermute | solution.py:94
  190.4 3.7 %collective-permute-done.20.refs_7_ = bf16[512,384]{1,0:T(8,128)(2,1)S(1)} collective-permute-done((bf16[512,384]{1,0:T(8,128)(2,1)S(1)}, bf16[512,384]{1,0:T(8,128)(2,1)S(1)}, u32[]{:S(2)}, u32[]{:S(2)}) %collective-permute-start.20) | collective-permute-done | bytes 393248 | tf_op jit(solution)/shard_map/ppermute | solution.py:94
  197.7 9.6 %input_side.1 = (f32[384,1024]{1,0:T(8,128)}, bf16[384,1024]{1,0:T(8,128)(2,1)}, bf16[16,264,128]{2,1,0:T(8,128)(2,1)}) custom-call(s32[1]{0:T(128)} %bitcast.me_ref, bf16[512,384]{1,0:T(8,128)(2,1)} %get-tuple-element.164.refs_0_, bf16[512,384]{1,0:T(8,128)(2,1)} %collective-permute-done.14.refs_1_, bf16[512,384]{1,0:T(8,128)(2,1)} %collective-permute-done.15.refs_2_, ...), custom_call_target="tpu_custom_call" | custom-call | tf_op jit(solution)/shard_map/input_side/pallas_call | solution.py:279
  207.5 2.8 copy.86
  210.3 7.1 %all-to-all-start.3 = ((bf16[3,128,1024]{2,0,1:T(4,128)(2,1)}), bf16[3,128,1024]{2,0,1:T(4,128)(2,1)S(1)}, u32[]{:S(2)}, u32[]{:S(2)}) async-start(bf16[3,128,1024]{2,0,1:T(4,128)(2,1)} %copy.86), calls=%async_computation.3 | async-start | bytes 2097152 | tf_op jit(solution)/shard_map/all_to_all | solution.py:361
  217.5 2.0 collective-permute-start.24
  219.5 15.6 %all-to-all-done.3 = bf16[3,128,1024]{2,0,1:T(4,128)(2,1)S(1)} async-done(((bf16[3,128,1024]{2,0,1:T(4,128)(2,1)}), bf16[3,128,1024]{2,0,1:T(4,128)(2,1)S(1)}, u32[]{:S(2)}, u32[]{:S(2)}) %all-to-all-start.3) | async-done | bytes 786464 | tf_op jit(solution)/shard_map/all_to_all | solution.py:361
  236.3 3.7 %all-to-all-start.4 = ((bf16[16,264,128]{2,1,0:T(8,128)(2,1)}), bf16[16,264,128]{2,1,0:T(8,128)(2,1)S(1)}, u32[]{:S(2)}, u32[]{:S(2)}) async-start(bf16[16,264,128]{2,1,0:T(8,128)(2,1)} %get-tuple-element.181), calls=%async_computation.4 | async-start | bytes 2162688 | tf_op jit(solution)/shard_map/all_to_all | solution.py:31
  241.5 2.3 fusion.1
  244.5 9.0 %collective-permute-done.26.refs_4_ = bf16[512,384]{1,0:T(8,128)(2,1)} collective-permute-done((bf16[512,384]{1,0:T(8,128)(2,1)}, bf16[512,384]{1,0:T(8,128)(2,1)}, u32[]{:S(2)}, u32[]{:S(2)}) %collective-permute-start.26) | collective-permute-done | bytes 393248 | tf_op jit(solution)/shard_map/ppermute | solution.py:94
  253.5 3.2 all-to-all-done.4
  258.9 4.0 %all-to-all-start.5 = ((bf16[48,8,1024]{2,1,0:T(8,128)(2,1)}), bf16[48,8,1024]{2,1,0:T(8,128)(2,1)S(1)}, u32[]{:S(2)}, u32[]{:S(2)}) async-start(bf16[48,8,1024]{2,1,0:T(8,128)(2,1)} %copy.91), calls=%async_computation.5 | async-start | bytes 1572864 | tf_op jit(solution)/shard_map/all_to_all | solution.py:369
  264.3 11.7 %collective-permute-done.27.refs_5_ = bf16[512,384]{1,0:T(8,128)(2,1)} collective-permute-done((bf16[512,384]{1,0:T(8,128)(2,1)}, bf16[512,384]{1,0:T(8,128)(2,1)}, u32[]{:S(2)}, u32[]{:S(2)}) %collective-permute-start.27) | collective-permute-done | bytes 393248 | tf_op jit(solution)/shard_map/ppermute | solution.py:94
  276.0 9.1 %output_side.1 = (bf16[384,1024]{1,0:T(8,128)(2,1)}, bf16[8,128,512]{2,1,0:T(8,128)(2,1)}) custom-call(s32[1]{0:T(128)} %bitcast.me_ref, bf16[512,384]{1,0:T(8,128)(2,1)} %get-tuple-element.163.refs_0_, bf16[512,384]{1,0:T(8,128)(2,1)} %copy-done.22, bf16[512,384]{1,0:T(8,128)(2,1)} %copy-done.21, bf16[512,384]{1,0:T(8,128)(2,1)} %collective-permute-done.23.refs_3_, ...), custom_call_target="tpu_custom_call" | custom-call | tf_op jit(solution)/shard_map/output_side/pallas_call | solution.py:235
  285.7 6.7 %all-to-all-start.6 = ((bf16[16,64,512]{2,1,0:T(8,128)(2,1)}), bf16[16,64,512]{2,1,0:T(8,128)(2,1)S(1)}, u32[]{:S(2)}, u32[]{:S(2)}) async-start(bf16[16,64,512]{2,1,0:T(8,128)(2,1)} %bitcast.95), calls=%async_computation.6 | async-start | bytes 2097152 | tf_op jit(solution)/shard_map/all_to_all | solution.py:31
  292.9 2.3 collective-permute-start.30
  295.2 2.0 collective-permute-start.31
  298.9 3.0 collective-permute-done.30
  301.9 2.3 collective-permute-done.31
  304.3 2.7 fusion
  307.1 7.2 %all-to-all-done.6 = bf16[16,64,512]{2,1,0:T(8,128)(2,1)S(1)} async-done(((bf16[16,64,512]{2,1,0:T(8,128)(2,1)}), bf16[16,64,512]{2,1,0:T(8,128)(2,1)S(1)}, u32[]{:S(2)}, u32[]{:S(2)}) %all-to-all-start.6) | async-done | bytes 1048608 | tf_op jit(solution)/shard_map/all_to_all | solution.py:31
  315.6 3.8 %all-to-all-start.7 = ((bf16[16,64,512]{2,1,0:T(8,128)(2,1)}), bf16[16,64,512]{2,1,0:T(8,128)(2,1)S(1)}, u32[]{:S(2)}, u32[]{:S(2)}) async-start(bf16[16,64,512]{2,1,0:T(8,128)(2,1)} %broadcast_in_dim.16), calls=%async_computation.7 | async-start | bytes 2097152 | tf_op jit(solution)/shard_map/all_to_all | solution.py:41
  324.8 2.8 fusion.13
  327.6 9.6 %all-to-all-done.7 = bf16[16,64,512]{2,1,0:T(8,128)(2,1)S(1)} async-done(((bf16[16,64,512]{2,1,0:T(8,128)(2,1)}), bf16[16,64,512]{2,1,0:T(8,128)(2,1)S(1)}, u32[]{:S(2)}, u32[]{:S(2)}) %all-to-all-start.7) | async-done | bytes 1048608 | tf_op jit(solution)/shard_map/all_to_all | solution.py:41
  (146 shorter events, 45.2 us)
Async XLA Ops:
  7.2 40.2 %copy-start = (bf16[8,48,48]{2,1,0:T(8,128)(2,1)S(1)}, bf16[8,48,48]{2,1,0:T(8,128)(2,1)}, u32[]{:S(2)}) copy-start(bf16[8,48,48]{2,1,0:T(8,128)(2,1)} %param.12) | copy-start | bytes 110596
  16.5 25.6 %all-to-all-start = ((bf16[3,128,1024]{2,0,1:T(4,128)(2,1)}), bf16[3,128,1024]{2,0,1:T(4,128)(2,1)S(1)}, u32[]{:S(2)}, u32[]{:S(2)}) async-start(bf16[3,128,1024]{2,0,1:T(4,128)(2,1)} %copy.77), calls=%async_computation | async-start | bytes 2097152 | tf_op jit(solution)/shard_map/all_to_all | solution.py:324
  24.5 18.0 %collective-permute-start = (bf16[512,384]{1,0:T(8,128)(2,1)}, bf16[512,384]{1,0:T(8,128)(2,1)S(1)}, u32[]{:S(2)}, u32[]{:S(2)}) collective-permute-start(bf16[512,384]{1,0:T(8,128)(2,1)} %get-tuple-element.114), channel_id=1, source_target_pairs={{0,1},{1,0},{2,3},{3,2},{4,5},{5,4},{6,7},{7,6},{8,9},{9,8},{10,11... | collective-permute-start | bytes 1179656 | tf_op jit(solution)/shard_map/ppermute | solution.py:94
  24.6 17.9 %collective-permute-start.1 = (bf16[512,384]{1,0:T(8,128)(2,1)}, bf16[512,384]{1,0:T(8,128)(2,1)S(1)}, u32[]{:S(2)}, u32[]{:S(2)}) collective-permute-start(bf16[512,384]{1,0:T(8,128)(2,1)} %get-tuple-element.115), channel_id=1, source_target_pairs={{0,2},{1,3},{2,0},{3,1},{4,6},{5,7},{6,4},{7,5},{8,10},{9,11},{10,... | collective-permute-start | bytes 1179656 | tf_op jit(solution)/shard_map/ppermute | solution.py:94
  26.2 18.0 %collective-permute-start.2 = (bf16[512,384]{1,0:T(8,128)(2,1)}, bf16[512,384]{1,0:T(8,128)(2,1)S(1)}, u32[]{:S(2)}, u32[]{:S(2)}) collective-permute-start(bf16[512,384]{1,0:T(8,128)(2,1)} %get-tuple-element.116), channel_id=1, source_target_pairs={{0,3},{1,2},{2,1},{3,0},{4,7},{5,6},{6,5},{7,4},{8,11},{9,10},{10,... | collective-permute-start | bytes 1179656 | tf_op jit(solution)/shard_map/ppermute | solution.py:94
  26.4 17.8 %collective-permute-start.3 = (bf16[512,384]{1,0:T(8,128)(2,1)}, bf16[512,384]{1,0:T(8,128)(2,1)S(1)}, u32[]{:S(2)}, u32[]{:S(2)}) collective-permute-start(bf16[512,384]{1,0:T(8,128)(2,1)} %get-tuple-element.117), channel_id=1, source_target_pairs={{0,6},{1,7},{2,4},{3,5},{4,2},{5,3},{6,0},{7,1},{8,14},{9,15},{10,... | collective-permute-start | bytes 1179656 | tf_op jit(solution)/shard_map/ppermute | solution.py:94
  29.5 17.9 %collective-permute-start.4 = (bf16[512,384]{1,0:T(8,128)(2,1)}, bf16[512,384]{1,0:T(8,128)(2,1)}, u32[]{:S(2)}, u32[]{:S(2)}) collective-permute-start(bf16[512,384]{1,0:T(8,128)(2,1)} %get-tuple-element.118), channel_id=1, source_target_pairs={{0,7},{1,6},{2,5},{3,4},{4,3},{5,2},{6,1},{7,0},{8,15},{9,14},{10,... | collective-permute-start | bytes 1179656 | tf_op jit(solution)/shard_map/ppermute | solution.py:94
  48.5 28.8 %copy-start.27 = (f32[1024]{0:T(1024)S(1)}, f32[1024]{0:T(1024)}, u32[]{:S(2)}) copy-start(f32[1024]{0:T(1024)} %param.13) | copy-start | bytes 12292
  49.8 22.0 %all-to-all-start.1 = ((bf16[48,8,1024]{2,1,0:T(8,128)(2,1)}), bf16[48,8,1024]{2,1,0:T(8,128)(2,1)S(1)}, u32[]{:S(2)}, u32[]{:S(2)}) async-start(bf16[48,8,1024]{2,1,0:T(8,128)(2,1)} %copy.81), calls=%async_computation.1 | async-start | bytes 1572864 | tf_op jit(solution)/shard_map/all_to_all | solution.py:328
  57.0 14.9 %collective-permute-start.5 = (bf16[512,384]{1,0:T(8,128)(2,1)}, bf16[512,384]{1,0:T(8,128)(2,1)S(1)}, u32[]{:S(2)}, u32[]{:S(2)}) collective-permute-start(bf16[512,384]{1,0:T(8,128)(2,1)} %get-tuple-element.120), channel_id=1, source_target_pairs={{0,4},{1,5},{2,6},{3,7},{4,0},{5,1},{6,2},{7,3},{8,12},{9,13},{10,... | collective-permute-start | bytes 1179656 | tf_op jit(solution)/shard_map/ppermute | solution.py:94
  58.9 18.4 %collective-permute-start.6 = (bf16[512,384]{1,0:T(8,128)(2,1)}, bf16[512,384]{1,0:T(8,128)(2,1)S(1)}, u32[]{:S(2)}, u32[]{:S(2)}) collective-permute-start(bf16[512,384]{1,0:T(8,128)(2,1)} %get-tuple-element.121), channel_id=1, source_target_pairs={{0,5},{1,4},{2,7},{3,6},{4,1},{5,0},{6,3},{7,2},{8,13},{9,12},{10,... | collective-permute-start | bytes 1179656 | tf_op jit(solution)/shard_map/ppermute | solution.py:94
  77.3 28.7 %copy-start.4 = (bf16[64,64,64]{2,1,0:T(8,128)(2,1)S(1)}, bf16[64,64,64]{2,1,0:T(8,128)(2,1)}, u32[]{:S(2)}) copy-start(bf16[64,64,64]{2,1,0:T(8,128)(2,1)} %refs_16_.1) | copy-start | bytes 1572868
  83.4 13.9 %collective-permute-start.10 = (bf16[512,384]{1,0:T(8,128)(2,1)}, bf16[512,384]{1,0:T(8,128)(2,1)S(1)}, u32[]{:S(2)}, u32[]{:S(2)}) collective-permute-start(bf16[512,384]{1,0:T(8,128)(2,1)} %get-tuple-element.127), channel_id=1, source_target_pairs={{0,4},{1,5},{2,6},{3,7},{4,0},{5,1},{6,2},{7,3},{8,12},{9,13},{10,... | collective-permute-start | bytes 1179656 | tf_op jit(solution)/shard_map/ppermute | solution.py:94
  85.5 19.8 %collective-permute-start.11 = (bf16[512,384]{1,0:T(8,128)(2,1)}, bf16[512,384]{1,0:T(8,128)(2,1)S(1)}, u32[]{:S(2)}, u32[]{:S(2)}) collective-permute-start(bf16[512,384]{1,0:T(8,128)(2,1)} %get-tuple-element.128), channel_id=1, source_target_pairs={{0,5},{1,4},{2,7},{3,6},{4,1},{5,0},{6,3},{7,2},{8,13},{9,12},{10,... | collective-permute-start | bytes 1179656 | tf_op jit(solution)/shard_map/ppermute | solution.py:94
  87.1 26.8 %collective-permute-start.12 = (bf16[512,384]{1,0:T(8,128)(2,1)}, bf16[512,384]{1,0:T(8,128)(2,1)S(1)}, u32[]{:S(2)}, u32[]{:S(2)}) collective-permute-start(bf16[512,384]{1,0:T(8,128)(2,1)} %get-tuple-element.129), channel_id=1, source_target_pairs={{0,6},{1,7},{2,4},{3,5},{4,2},{5,3},{6,0},{7,1},{8,14},{9,15},{10,... | collective-permute-start | bytes 1179656 | tf_op jit(solution)/shard_map/ppermute | solution.py:94
  90.1 32.1 %collective-permute-start.13 = (bf16[512,384]{1,0:T(8,128)(2,1)}, bf16[512,384]{1,0:T(8,128)(2,1)S(1)}, u32[]{:S(2)}, u32[]{:S(2)}) collective-permute-start(bf16[512,384]{1,0:T(8,128)(2,1)} %get-tuple-element.130), channel_id=1, source_target_pairs={{0,7},{1,6},{2,5},{3,4},{4,3},{5,2},{6,1},{7,0},{8,15},{9,14},{10,... | collective-permute-start | bytes 1179656 | tf_op jit(solution)/shard_map/ppermute | solution.py:94
  90.1 32.1 %collective-permute-start.7 = (bf16[512,384]{1,0:T(8,128)(2,1)}, bf16[512,384]{1,0:T(8,128)(2,1)}, u32[]{:S(2)}, u32[]{:S(2)}) collective-permute-start(bf16[512,384]{1,0:T(8,128)(2,1)} %get-tuple-element.124), channel_id=1, source_target_pairs={{0,1},{1,0},{2,3},{3,2},{4,5},{5,4},{6,7},{7,6},{8,9},{9,8},{10,11... | collective-permute-start | bytes 1179656 | tf_op jit(solution)/shard_map/ppermute | solution.py:94
  97.3 24.9 %collective-permute-start.8 = (bf16[512,384]{1,0:T(8,128)(2,1)}, bf16[512,384]{1,0:T(8,128)(2,1)}, u32[]{:S(2)}, u32[]{:S(2)}) collective-permute-start(bf16[512,384]{1,0:T(8,128)(2,1)} %get-tuple-element.125), channel_id=1, source_target_pairs={{0,2},{1,3},{2,0},{3,1},{4,6},{5,7},{6,4},{7,5},{8,10},{9,11},{10,... | collective-permute-start | bytes 1179656 | tf_op jit(solution)/shard_map/ppermute | solution.py:94
  105.3 17.2 %collective-permute-start.9 = (bf16[512,384]{1,0:T(8,128)(2,1)}, bf16[512,384]{1,0:T(8,128)(2,1)}, u32[]{:S(2)}, u32[]{:S(2)}) collective-permute-start(bf16[512,384]{1,0:T(8,128)(2,1)} %get-tuple-element.126), channel_id=1, source_target_pairs={{0,3},{1,2},{2,1},{3,0},{4,7},{5,6},{6,5},{7,4},{8,11},{9,10},{10,... | collective-permute-start | bytes 1179656 | tf_op jit(solution)/shard_map/ppermute | solution.py:94
  139.8 13.4 %collective-permute-start.14 = (bf16[512,384]{1,0:T(8,128)(2,1)}, bf16[512,384]{1,0:T(8,128)(2,1)}, u32[]{:S(2)}, u32[]{:S(2)}) collective-permute-start(bf16[512,384]{1,0:T(8,128)(2,1)} %get-tuple-element.153), channel_id=1, source_target_pairs={{0,1},{1,0},{2,3},{3,2},{4,5},{5,4},{6,7},{7,6},{8,9},{9,8},{10,11... | collective-permute-start | bytes 1179656 | tf_op jit(solution)/shard_map/ppermute | solution.py:94
  140.0 13.3 %collective-permute-start.15 = (bf16[512,384]{1,0:T(8,128)(2,1)}, bf16[512,384]{1,0:T(8,128)(2,1)}, u32[]{:S(2)}, u32[]{:S(2)}) collective-permute-start(bf16[512,384]{1,0:T(8,128)(2,1)} %get-tuple-element.154), channel_id=1, source_target_pairs={{0,2},{1,3},{2,0},{3,1},{4,6},{5,7},{6,4},{7,5},{8,10},{9,11},{10,... | collective-permute-start | bytes 1179656 | tf_op jit(solution)/shard_map/ppermute | solution.py:94
  140.7 12.7 %collective-permute-start.16 = (bf16[512,384]{1,0:T(8,128)(2,1)}, bf16[512,384]{1,0:T(8,128)(2,1)}, u32[]{:S(2)}, u32[]{:S(2)}) collective-permute-start(bf16[512,384]{1,0:T(8,128)(2,1)} %get-tuple-element.155), channel_id=1, source_target_pairs={{0,6},{1,7},{2,4},{3,5},{4,2},{5,3},{6,0},{7,1},{8,14},{9,15},{10,... | collective-permute-start | bytes 1179656 | tf_op jit(solution)/shard_map/ppermute | solution.py:94
  153.2 43.2 %copy-start.5 = (bf16[8,512,128]{2,1,0:T(8,128)(2,1)S(1)}, bf16[8,512,128]{2,1,0:T(8,128)(2,1)}, u32[]{:S(2)}) copy-start(bf16[8,512,128]{2,1,0:T(8,128)(2,1)} %w_ref.1) | copy-start | bytes 3145732
  153.4 54.2 %all-to-all-start.2 = ((bf16[16,256,128]{2,1,0:T(8,128)(2,1)}), bf16[16,256,128]{2,1,0:T(8,128)(2,1)S(1)}, u32[]{:S(2)}, u32[]{:S(2)}) async-start(bf16[16,256,128]{2,1,0:T(8,128)(2,1)} %bitcast.94), calls=%async_computation.2 | async-start | bytes 2097152 | tf_op jit(solution)/shard_map/all_to_all | solution.py:31
  160.3 11.7 %collective-permute-start.17 = (bf16[512,384]{1,0:T(8,128)(2,1)}, bf16[512,384]{1,0:T(8,128)(2,1)S(1)}, u32[]{:S(2)}, u32[]{:S(2)}) collective-permute-start(bf16[512,384]{1,0:T(8,128)(2,1)} %get-tuple-element.158), channel_id=1, source_target_pairs={{0,3},{1,2},{2,1},{3,0},{4,7},{5,6},{6,5},{7,4},{8,11},{9,10},{10,... | collective-permute-start | bytes 1179656 | tf_op jit(solution)/shard_map/ppermute | solution.py:94
  160.9 20.6 %collective-permute-start.18 = (bf16[512,384]{1,0:T(8,128)(2,1)}, bf16[512,384]{1,0:T(8,128)(2,1)S(1)}, u32[]{:S(2)}, u32[]{:S(2)}) collective-permute-start(bf16[512,384]{1,0:T(8,128)(2,1)} %get-tuple-element.159), channel_id=1, source_target_pairs={{0,4},{1,5},{2,6},{3,7},{4,0},{5,1},{6,2},{7,3},{8,12},{9,13},{10,... | collective-permute-start | bytes 1179656 | tf_op jit(solution)/shard_map/ppermute | solution.py:94
  163.3 27.1 %collective-permute-start.19 = (bf16[512,384]{1,0:T(8,128)(2,1)}, bf16[512,384]{1,0:T(8,128)(2,1)S(1)}, u32[]{:S(2)}, u32[]{:S(2)}) collective-permute-start(bf16[512,384]{1,0:T(8,128)(2,1)} %get-tuple-element.160), channel_id=1, source_target_pairs={{0,5},{1,4},{2,7},{3,6},{4,1},{5,0},{6,3},{7,2},{8,13},{9,12},{10,... | collective-permute-start | bytes 1179656 | tf_op jit(solution)/shard_map/ppermute | solution.py:94
  164.7 29.4 %collective-permute-start.20 = (bf16[512,384]{1,0:T(8,128)(2,1)S(1)}, bf16[512,384]{1,0:T(8,128)(2,1)S(1)}, u32[]{:S(2)}, u32[]{:S(2)}) collective-permute-start(bf16[512,384]{1,0:T(8,128)(2,1)S(1)} %copy-done.28), channel_id=1, source_target_pairs={{0,7},{1,6},{2,5},{3,4},{4,3},{5,2},{6,1},{7,0},{8,15},{9,14},{10,... | collective-permute-start | bytes 1179656 | tf_op jit(solution)/shard_map/ppermute | solution.py:94
  172.1 22.1 %copy-start.23 = (bf16[512,384]{1,0:T(8,128)(2,1)}, bf16[512,384]{1,0:T(8,128)(2,1)S(1)}, u32[]{:S(2)}) copy-start(bf16[512,384]{1,0:T(8,128)(2,1)S(1)} %collective-permute-done.17.refs_3_) | copy-start | bytes 1179652
  194.1 13.2 %collective-permute-start.21 = (bf16[512,384]{1,0:T(8,128)(2,1)}, bf16[512,384]{1,0:T(8,128)(2,1)S(1)}, u32[]{:S(2)}, u32[]{:S(2)}) collective-permute-start(bf16[512,384]{1,0:T(8,128)(2,1)} %get-tuple-element.173), channel_id=1, source_target_pairs={{0,2},{1,3},{2,0},{3,1},{4,6},{5,7},{6,4},{7,5},{8,10},{9,11},{10,... | collective-permute-start | bytes 1179656 | tf_op jit(solution)/shard_map/ppermute | solution.py:94
  194.9 12.7 %collective-permute-start.22 = (bf16[512,384]{1,0:T(8,128)(2,1)}, bf16[512,384]{1,0:T(8,128)(2,1)}, u32[]{:S(2)}, u32[]{:S(2)}) collective-permute-start(bf16[512,384]{1,0:T(8,128)(2,1)} %get-tuple-element.174), channel_id=1, source_target_pairs={{0,6},{1,7},{2,4},{3,5},{4,2},{5,3},{6,0},{7,1},{8,14},{9,15},{10,... | collective-permute-start | bytes 1179656 | tf_op jit(solution)/shard_map/ppermute | solution.py:94
  207.3 28.0 %copy-start.21 = (bf16[512,384]{1,0:T(8,128)(2,1)}, bf16[512,384]{1,0:T(8,128)(2,1)S(1)}, u32[]{:S(2)}) copy-start(bf16[512,384]{1,0:T(8,128)(2,1)S(1)} %collective-permute-done.21.refs_2_) | copy-start | bytes 1179652
  210.3 24.8 %all-to-all-start.3 = ((bf16[3,128,1024]{2,0,1:T(4,128)(2,1)}), bf16[3,128,1024]{2,0,1:T(4,128)(2,1)S(1)}, u32[]{:S(2)}, u32[]{:S(2)}) async-start(bf16[3,128,1024]{2,0,1:T(4,128)(2,1)} %copy.86), calls=%async_computation.3 | async-start | bytes 2097152 | tf_op jit(solution)/shard_map/all_to_all | solution.py:361
  217.4 18.9 %collective-permute-start.23 = (bf16[512,384]{1,0:T(8,128)(2,1)}, bf16[512,384]{1,0:T(8,128)(2,1)}, u32[]{:S(2)}, u32[]{:S(2)}) collective-permute-start(bf16[512,384]{1,0:T(8,128)(2,1)} %get-tuple-element.177), channel_id=1, source_target_pairs={{0,3},{1,2},{2,1},{3,0},{4,7},{5,6},{6,5},{7,4},{8,11},{9,10},{10,... | collective-permute-start | bytes 1179656 | tf_op jit(solution)/shard_map/ppermute | solution.py:94
  217.5 18.8 %collective-permute-start.24 = (bf16[512,384]{1,0:T(8,128)(2,1)}, bf16[512,384]{1,0:T(8,128)(2,1)}, u32[]{:S(2)}, u32[]{:S(2)}) collective-permute-start(bf16[512,384]{1,0:T(8,128)(2,1)} %get-tuple-element.178), channel_id=1, source_target_pairs={{0,7},{1,6},{2,5},{3,4},{4,3},{5,2},{6,1},{7,0},{8,15},{9,14},{10,... | collective-permute-start | bytes 1179656 | tf_op jit(solution)/shard_map/ppermute | solution.py:94
  236.3 20.4 %all-to-all-start.4 = ((bf16[16,264,128]{2,1,0:T(8,128)(2,1)}), bf16[16,264,128]{2,1,0:T(8,128)(2,1)S(1)}, u32[]{:S(2)}, u32[]{:S(2)}) async-start(bf16[16,264,128]{2,1,0:T(8,128)(2,1)} %get-tuple-element.181), calls=%async_computation.4 | async-start | bytes 2162688 | tf_op jit(solution)/shard_map/all_to_all | solution.py:31
  240.0 74.4 %all-gather.2.cloned.1.call-start = ((), (), s32[]{:S(2)}) async-start(), calls=%async_computation.8 | async-start | bytes 2263040 | tf_op jit(solution)/shard_map/all_gather | solution.py:378
  240.1 3.7 %collective-permute-start.25 = (bf16[512,384]{1,0:T(8,128)(2,1)}, bf16[512,384]{1,0:T(8,128)(2,1)S(1)}, u32[]{:S(2)}, u32[]{:S(2)}) collective-permute-start(bf16[512,384]{1,0:T(8,128)(2,1)} %get-tuple-element.182), channel_id=1, source_target_pairs={{0,1},{1,0},{2,3},{3,2},{4,5},{5,4},{6,7},{7,6},{8,9},{9,8},{10,11... | collective-permute-start | bytes 1179656 | tf_op jit(solution)/shard_map/ppermute | solution.py:94
  240.2 13.4 %collective-permute-start.26 = (bf16[512,384]{1,0:T(8,128)(2,1)}, bf16[512,384]{1,0:T(8,128)(2,1)}, u32[]{:S(2)}, u32[]{:S(2)}) collective-permute-start(bf16[512,384]{1,0:T(8,128)(2,1)} %get-tuple-element.183), channel_id=1, source_target_pairs={{0,4},{1,5},{2,6},{3,7},{4,0},{5,1},{6,2},{7,3},{8,12},{9,13},{10,... | collective-permute-start | bytes 1179656 | tf_op jit(solution)/shard_map/ppermute | solution.py:94
  258.9 26.2 %all-to-all-start.5 = ((bf16[48,8,1024]{2,1,0:T(8,128)(2,1)}), bf16[48,8,1024]{2,1,0:T(8,128)(2,1)S(1)}, u32[]{:S(2)}, u32[]{:S(2)}) async-start(bf16[48,8,1024]{2,1,0:T(8,128)(2,1)} %copy.91), calls=%async_computation.5 | async-start | bytes 1572864 | tf_op jit(solution)/shard_map/all_to_all | solution.py:369
  262.9 13.1 %collective-permute-start.27 = (bf16[512,384]{1,0:T(8,128)(2,1)}, bf16[512,384]{1,0:T(8,128)(2,1)}, u32[]{:S(2)}, u32[]{:S(2)}) collective-permute-start(bf16[512,384]{1,0:T(8,128)(2,1)} %get-tuple-element.188), channel_id=1, source_target_pairs={{0,5},{1,4},{2,7},{3,6},{4,1},{5,0},{6,3},{7,2},{8,13},{9,12},{10,... | collective-permute-start | bytes 1179656 | tf_op jit(solution)/shard_map/ppermute | solution.py:94
  285.6 6.8 %collective-permute-start.28 = (f32[264,128]{1,0:T(8,128)S(1)}, f32[264,128]{1,0:T(8,128)S(1)}, u32[]{:S(2)}, u32[]{:S(2)}) collective-permute-start(f32[264,128]{1,0:T(8,128)S(1)} %dynamic-slice_bitcast_fusion), channel_id=1, source_target_pairs={{0,1},{1,0},{2,3},{3,2},{4,5},{5,4},{6,7},{7,6},{8,9},{9,8},{10,11... | collective-permute-start | bytes 405512 | tf_op jit(solution)/shard_map/ppermute | solution.py:52
  285.7 28.6 %all-to-all-start.6 = ((bf16[16,64,512]{2,1,0:T(8,128)(2,1)}), bf16[16,64,512]{2,1,0:T(8,128)(2,1)S(1)}, u32[]{:S(2)}, u32[]{:S(2)}) async-start(bf16[16,64,512]{2,1,0:T(8,128)(2,1)} %bitcast.95), calls=%async_computation.6 | async-start | bytes 2097152 | tf_op jit(solution)/shard_map/all_to_all | solution.py:31
  292.4 6.5 %collective-permute-start.29 = (f32[264,128]{1,0:T(8,128)S(1)}, f32[264,128]{1,0:T(8,128)S(1)}, u32[]{:S(2)}, u32[]{:S(2)}) collective-permute-start(f32[264,128]{1,0:T(8,128)S(1)} %bitcast_add_fusion.1), channel_id=1, source_target_pairs={{0,2},{1,3},{2,0},{3,1},{4,6},{5,7},{6,4},{7,5},{8,10},{9,11},{10,... | collective-permute-start | bytes 405512 | tf_op jit(solution)/shard_map/ppermute | solution.py:55
  292.9 9.0 %collective-permute-start.30 = (f32[264,128]{1,0:T(8,128)S(1)}, f32[264,128]{1,0:T(8,128)S(1)}, u32[]{:S(2)}, u32[]{:S(2)}) collective-permute-start(f32[264,128]{1,0:T(8,128)S(1)} %bitcast_add_fusion.1), channel_id=1, source_target_pairs={{0,4},{1,5},{2,6},{3,7},{4,0},{5,1},{6,2},{7,3},{8,12},{9,13},{10,... | collective-permute-start | bytes 405512 | tf_op jit(solution)/shard_map/ppermute | solution.py:55
  295.2 9.0 %collective-permute-start.31 = (f32[264,128]{1,0:T(8,128)S(1)}, f32[264,128]{1,0:T(8,128)S(1)}, u32[]{:S(2)}, u32[]{:S(2)}) collective-permute-start(f32[264,128]{1,0:T(8,128)S(1)} %bitcast_add_fusion.1), channel_id=1, source_target_pairs={{0,6},{1,7},{2,4},{3,5},{4,2},{5,3},{6,0},{7,1},{8,14},{9,15},{10,... | collective-permute-start | bytes 405512 | tf_op jit(solution)/shard_map/ppermute | solution.py:55
  304.2 2.8 collective-permute-start.32
  315.6 21.6 %all-to-all-start.7 = ((bf16[16,64,512]{2,1,0:T(8,128)(2,1)}), bf16[16,64,512]{2,1,0:T(8,128)(2,1)S(1)}, u32[]{:S(2)}, u32[]{:S(2)}) async-start(bf16[16,64,512]{2,1,0:T(8,128)(2,1)} %broadcast_in_dim.16), calls=%async_computation.7 | async-start | bytes 2097152 | tf_op jit(solution)/shard_map/all_to_all | solution.py:41
  (23 other events, 159.3 us)
Sparse Core Ops, SparseCore 0:
  257.7 54.3 all-gather.1

commit v3 on v2

--- a/solution.py
+++ b/solution.py
@@ -253,7 +253,14 @@
     )(me, *act, zed, cot, right_two)
 
 
-def input_side(act, zed, cot, mixed, gain, right_one_t, me):
+def by_residue(value, shape):
+    parts, rows, cols = shape
+    value = value.reshape(rows // 8, parts, 8, cols)
+    moved = [value[:, p].reshape(rows, cols)[None] for p in range(parts)]
+    return jnp.concatenate(moved, axis=0).astype(BF)
+
+
+def input_side(act, zed, cot, mixed, gain, right_one_t, n_dp, me):
     n = len(act)
     rows, tokens = act[0].shape
     blocks, feats, hidden = right_one_t.shape
@@ -264,7 +271,7 @@
         mine = pick_block(wide_ref, hidden, blocks)
         back_z = g_ref[...].astype(F32) + dot(w_ref[0], mine, 1, 0).T
         bz_ref[...] = back_z
-        bm_ref[...] = (back_z * s_ref[...]).astype(BF)
+        bm_ref[...] = by_residue(back_z * s_ref[...], bm_ref.shape)
         gain_part = jnp.sum(back_z * m_ref[...].astype(F32), axis=0, keepdims=True)
         high = gain_part.astype(BF).astype(F32)
         row = lax.broadcasted_iota(jnp.int32, (8, feats), 0)
@@ -290,12 +297,12 @@
         ],
         out_specs=[
             column,
-            column,
+            pl.BlockSpec((n_dp, tokens // n_dp, feats), lambda b: (0, 0, b)),
             pl.BlockSpec((2, hidden // 2 + 8, feats), lambda b: (b, 0, 0)),
         ],
         out_shape=[
             jax.ShapeDtypeStruct(zed.shape, F32),
-            jax.ShapeDtypeStruct(zed.shape, BF),
+            jax.ShapeDtypeStruct((n_dp, tokens // n_dp, zed.shape[1]), BF),
             jax.ShapeDtypeStruct((blocks * 2, hidden // 2 + 8, feats), BF),
         ],
         scratch_shapes=[pltpu.VMEM((tokens // 128, n * rows, 128), F32)],
@@ -336,10 +343,11 @@
     pieces, (x, back, hid, back_pre) = middle_main(
         act_a, back_c, left_one, jnp.swapaxes(left_one, 1, 2), jnp.swapaxes(left_two, 1, 2), me1
     )
-    back_a1 = send(pieces, 2, 6, 1)
+    back_a1 = send(pieces, 2, 6, 3, 7, 1)
     pieces_c, part_left = middle_rest(x, back, hid, back_pre, left_two, n_mp, me1)
-    part_left, back_a1 = together(part_left, back_a1)
-    back_a2 = send(pieces, 3, 7, 4, 5)
+    right_one_t = jnp.swapaxes(right_one, 1, 2)
+    part_left, back_a1, right_one_t = together(part_left, back_a1, right_one_t)
+    back_a2 = send(pieces, 4, 5)
     back_a = in_order(pieces, back_a1, back_a2)
     left_parts = slice_parts(part_left)
 
@@ -351,23 +359,23 @@
         cotangent,
         mixed,
         seq_gain.reshape(1, cols_here),
-        jnp.swapaxes(right_one, 1, 2),
+        right_one_t,
+        lax.axis_size("dp"),
         me1,
     )
     back_mixed, act_c1, left_parts = together(back_mixed, act_c1, left_parts)
     back_z = back_z.reshape(blocks_here, block_len, cols_here)
-    back_mixed = back_mixed.reshape(blocks_here, block_len, cols_here)
-    act_c2 = send(pieces_c, 3, 7)
-    back_mixed_moved = lax.all_to_all(back_mixed, "dp", split_axis=1, concat_axis=0, tiled=True)
+    act_c2 = send(pieces_c, 3, 7, 1)
+    back_mixed_moved = lax.all_to_all(back_mixed, "dp", split_axis=0, concat_axis=0, tiled=True)
+    back_mixed_moved = back_mixed_moved.reshape(first_moved.shape)
     back_mixed_moved, act_c2, part_r1 = together(back_mixed_moved, act_c2, part_r1)
     back_first_moved = product("isk,sic->kic", seq_left, back_mixed_moved).astype(BF)
     part_seq_left = product("sic,kic->isk", back_mixed_moved, first_moved)
-    act_c3 = send(pieces_c, 4, 1)
+    act_c3 = send(pieces_c, 4, 5)
     r1_parts = slice_parts(part_r1)
     back_first_moved, r1_parts, act_c3 = together(back_first_moved, r1_parts, act_c3)
-    act_c4 = send(pieces_c, 5)
     back_first = lax.all_to_all(back_first_moved, "dp", split_axis=0, concat_axis=1, tiled=True)
-    act_c = in_order(pieces_c, act_c1, act_c2, act_c3, act_c4)
+    act_c = in_order(pieces_c, act_c1, act_c2, act_c3)
     slice_left = add_parts(left_parts, scale_rows)
     slice_r1 = add_parts(r1_parts, scale_rows)
     half = right_one.shape[1] // 2
@@ -380,12 +388,12 @@
     output, part_r2 = output_side(act_c, zed, cotangent, right_two, me1)
     back_first, part_r2 = together(back_first, part_r2)
     slice_r2 = add_parts(slice_parts(part_r2), scale_rows).astype(BF)
-    slice_r2, gathered = together(slice_r2, gathered)
+    sum_r2, gathered = together(all_slices(slice_r2), gathered)
     gathered = gathered.astype(F32)
     sum_left = gathered[:, :rows_left].reshape(part_left.shape)
     sum_r1 = gathered[:, rows_left : rows_left + half].reshape(right_one.shape)
     sum_gain = gathered[::2, rows_left + half].reshape(cols_here)
-    sum_r2 = all_slices(slice_r2).astype(F32)
+    sum_r2 = sum_r2.astype(F32)
 
     grad_tokens = (back_z + product("sij,sic->sjc", seq_right, back_first)).astype(BF)
     part_seq_right = product("sic,sjc->sij", back_first, seq_view)

time: 347 us -> 344 us (level)
  waiting for transfers between devices: 153 us -> 144 us
  starting transfers between devices: 83.8 us -> 88.7 us
    all_to_all x1, waiting for transfers between devices: 15.6 us -> 0.67 us  [per_device(): lax.all_to_all(back_mixed, 'dp', split_axis=0, concat_axis=0, tiled=True)]
    all_to_all x1, waiting for transfers between devices: 0.01 us -> 9.09 us  [per_device(): lax.all_to_all(back_first_moved, 'dp', split_axis=0, concat_axis=1, tiled...]
    ppermute x3, waiting for transfers between devices: 6.99 us -> 0.01 us  [sum_over_mp(): total = total + lax.ppermute(mine, 'mp', [(i, i ^ d) for i in range(n)])]
    unnamed x62 -> x64, local copies, waits for them, and re-layouts: 9.21 us -> 10.2 us
  transfers between devices with their start and end apart: 42 -> 42, of which waited for: 25 -> 24; matrix products, arithmetic and copies ran while one was open for 7% -> 5% of each run, Pallas kernels for 8% -> 8%
where the time goes in v3:
time: 344 us; the launch traced here: 342 us
  waiting for transfers between devices  144 us (42%)
  starting transfers between devices  88.7 us (26%)
  Pallas kernels  55.7 us (16%)
  local copies, waits for them, and re-layouts  25.4 us (7%)
  between operations  14.6 us (4%)
  matrix products  9.56 us (3%)
  other arithmetic  4.75 us (1%)
    ppermute x28, waiting for transfers between devices, send(): lax.ppermute(pieces[d], 'mp', [(i, i ^ d) for i in range(n)])  86.5 us
    ppermute x28, starting transfers between devices, send(): lax.ppermute(pieces[d], 'mp', [(i, i ^ d) for i in range(n)])  33.6 us
    all_to_all x3, starting transfers between devices, slice_parts(): return lax.all_to_all(parts, 'dp', split_axis=0, concat_axis=0, tiled=True)  17.2 us
    pallas_call x1, Pallas kernels, middle_main(): pl.pallas_call(body, grid=(units // STEP,), in_specs=[pl.BlockSpec(memory...  17 us
    all_to_all x1, waiting for transfers between devices, per_device(): lax.all_to_all(first, 'dp', split_axis=1, concat_axis=0, tiled=True)  12.7 us
    all_to_all x1, waiting for transfers between devices, per_device(): lax.all_to_all(mixed_moved, 'dp', split_axis=0, concat_axis=1, tiled=True)  11.9 us
    all_to_all x1, waiting for transfers between devices, all_slices(): return lax.all_to_all(copies, 'dp', split_axis=0, concat_axis=0, tiled=True)  11.7 us
    unnamed x64, local copies, waits for them, and re-layouts  10.2 us
  transfers between devices with their start and end apart: 42, of which 24 were waited for; matrix products, arithmetic and copies ran while one was open for 5% of the time, Pallas kernels for 8%

profile of v3, /device:TPU:0, one launch (start us, length us, event | category | flops | bytes accessed | tf_op | source)
XLA Modules:
  0.0 342.4 jit_solution(15574610819806346765)
XLA Ops:
  7.2 2.3 copy.73
  9.9 4.9 %expand.2 = (bf16[512,384]{1,0:T(8,128)(2,1)}, bf16[512,384]{1,0:T(8,128)(2,1)}, bf16[512,384]{1,0:T(8,128)(2,1)}, bf16[512,384]{1,0:T(8,128)(2,1)}, bf16[512,38...) custom-call(s32[1]{0:T(128)} %bitcast.me_ref, ...), custom_call_target="tpu_custom_call" | custom-call | tf_op jit(solution)/shard_map/expand/pallas_call | solution.py:81
  16.5 8.0 %all-to-all-start = ((bf16[3,128,1024]{2,0,1:T(4,128)(2,1)}), bf16[3,128,1024]{2,0,1:T(4,128)(2,1)S(1)}, u32[]{:S(2)}, u32[]{:S(2)}) async-start(bf16[3,128,1024]{2,0,1:T(4,128)(2,1)} %copy.74), calls=%async_computation | async-start | bytes 2097152 | tf_op jit(solution)/shard_map/all_to_all | solution.py:331
  26.4 3.0 collective-permute-start.3
  29.4 12.7 %all-to-all-done = bf16[3,128,1024]{2,0,1:T(4,128)(2,1)S(1)} async-done(((bf16[3,128,1024]{2,0,1:T(4,128)(2,1)}), bf16[3,128,1024]{2,0,1:T(4,128)(2,1)S(1)}, u32[]{:S(2)}, u32[]{:S(2)}) %all-to-all-start) | async-done | bytes 786464 | tf_op jit(solution)/shard_map/all_to_all | solution.py:331
  44.2 3.1 collective-permute-done.4.refs_15_
  49.8 7.2 %all-to-all-start.1 = ((bf16[48,8,1024]{2,1,0:T(8,128)(2,1)}), bf16[48,8,1024]{2,1,0:T(8,128)(2,1)S(1)}, u32[]{:S(2)}, u32[]{:S(2)}) async-start(bf16[48,8,1024]{2,1,0:T(8,128)(2,1)} %copy.78), calls=%async_computation.1 | async-start | bytes 1572864 | tf_op jit(solution)/shard_map/all_to_all | solution.py:335
  56.9 1.9 collective-permute-start.5
  59.9 11.9 %all-to-all-done.1 = bf16[48,8,1024]{2,1,0:T(8,128)(2,1)S(1)} async-done(((bf16[48,8,1024]{2,1,0:T(8,128)(2,1)}), bf16[48,8,1024]{2,1,0:T(8,128)(2,1)S(1)}, u32[]{:S(2)}, u32[]{:S(2)}) %all-to-all-start.1) | async-done | bytes 786464 | tf_op jit(solution)/shard_map/all_to_all | solution.py:335
  71.8 5.4 %collective-permute-done.6.refs_13_ = bf16[512,384]{1,0:T(8,128)(2,1)S(1)} collective-permute-done((bf16[512,384]{1,0:T(8,128)(2,1)}, bf16[512,384]{1,0:T(8,128)(2,1)S(1)}, u32[]{:S(2)}, u32[]{:S(2)}) %collective-permute-start.6) | collective-permute-done | bytes 393248 | tf_op jit(solution)/shard_map/ppermute | solution.py:94
  79.2 5.0 %expand.3 = (bf16[512,384]{1,0:T(8,128)(2,1)}, bf16[512,384]{1,0:T(8,128)(2,1)}, bf16[512,384]{1,0:T(8,128)(2,1)}, bf16[512,384]{1,0:T(8,128)(2,1)}, bf16[512,38...) custom-call(s32[1]{0:T(128)} %bitcast.me_ref, ...), custom_call_target="tpu_custom_call" | custom-call | tf_op jit(solution)/shard_map/expand/pallas_call | solution.py:81
  84.2 2.1 collective-permute-start.10
  87.9 3.0 collective-permute-start.12
  91.3 6.8 %collective-permute-done.10.refs_4_ = bf16[512,384]{1,0:T(8,128)(2,1)S(1)} collective-permute-done((bf16[512,384]{1,0:T(8,128)(2,1)}, bf16[512,384]{1,0:T(8,128)(2,1)S(1)}, u32[]{:S(2)}, u32[]{:S(2)}) %collective-permute-start.10) | collective-permute-done | bytes 393248 | tf_op jit(solution)/shard_map/ppermute | solution.py:94
  99.1 7.1 %collective-permute-done.11.refs_5_ = bf16[512,384]{1,0:T(8,128)(2,1)} collective-permute-done((bf16[512,384]{1,0:T(8,128)(2,1)}, bf16[512,384]{1,0:T(8,128)(2,1)}, u32[]{:S(2)}, u32[]{:S(2)}) %collective-permute-start.11) | collective-permute-done | bytes 393248 | tf_op jit(solution)/shard_map/ppermute | solution.py:94
  109.6 5.2 %collective-permute-done.12.refs_6_ = bf16[512,384]{1,0:T(8,128)(2,1)} collective-permute-done((bf16[512,384]{1,0:T(8,128)(2,1)}, bf16[512,384]{1,0:T(8,128)(2,1)}, u32[]{:S(2)}, u32[]{:S(2)}) %collective-permute-start.12) | collective-permute-done | bytes 393248 | tf_op jit(solution)/shard_map/ppermute | solution.py:94
  114.8 8.3 %collective-permute-done.13.refs_7_ = bf16[512,384]{1,0:T(8,128)(2,1)} collective-permute-done((bf16[512,384]{1,0:T(8,128)(2,1)}, bf16[512,384]{1,0:T(8,128)(2,1)}, u32[]{:S(2)}, u32[]{:S(2)}) %collective-permute-start.13) | collective-permute-done | bytes 393248 | tf_op jit(solution)/shard_map/ppermute | solution.py:94
  123.2 17.0 %middle_main.1 = (bf16[512,384]{1,0:T(8,128)(2,1)}, bf16[512,384]{1,0:T(8,128)(2,1)}, bf16[512,384]{1,0:T(8,128)(2,1)}, bf16[512,384]{1,0:T(8,128)(2,1)}, bf16[5...) custom-call(s32[1]{0:T(128)} %bitcast.me_ref, ...), custom_call_target="tpu_custom_call" | custom-call | tf_op jit(solution)/shard_map/middle_main/pallas_call | solution.py:159
  142.1 3.1 collective-permute-start.17
  146.5 10.0 %middle_rest.1 = (bf16[512,384]{1,0:T(8,128)(2,1)}, bf16[512,384]{1,0:T(8,128)(2,1)}, bf16[512,384]{1,0:T(8,128)(2,1)}, bf16[512,384]{1,0:T(8,128)(2,1)}, bf16[5...) custom-call(s32[1]{0:T(128)} %bitcast.me_ref, ...), custom_call_target="tpu_custom_call" | custom-call | tf_op jit(solution)/shard_map/middle_rest/pallas_call | solution.py:190
  156.6 3.2 collective-permute-done.16.refs_3_
  159.8 3.4 collective-permute-done.18.refs_7_
  163.2 6.9 %all-to-all-start.2 = ((bf16[16,256,128]{2,1,0:T(8,128)(2,1)}), bf16[16,256,128]{2,1,0:T(8,128)(2,1)S(1)}, u32[]{:S(2)}, u32[]{:S(2)}) async-start(bf16[16,256,128]{2,1,0:T(8,128)(2,1)} %bitcast.87), calls=%async_computation.2 | async-start | bytes 2097152 | tf_op jit(solution)/shard_map/all_to_all | solution.py:31
  171.0 2.1 collective-permute-start.20
  173.1 10.7 %collective-permute-done.19.refs_4_ = bf16[512,384]{1,0:T(8,128)(2,1)S(1)} collective-permute-done((bf16[512,384]{1,0:T(8,128)(2,1)}, bf16[512,384]{1,0:T(8,128)(2,1)S(1)}, u32[]{:S(2)}, u32[]{:S(2)}) %collective-permute-start.19) | collective-permute-done | bytes 393248 | tf_op jit(solution)/shard_map/ppermute | solution.py:94
  183.9 6.7 %collective-permute-done.20.refs_5_ = bf16[512,384]{1,0:T(8,128)(2,1)S(1)} collective-permute-done((bf16[512,384]{1,0:T(8,128)(2,1)}, bf16[512,384]{1,0:T(8,128)(2,1)S(1)}, u32[]{:S(2)}, u32[]{:S(2)}) %collective-permute-start.20) | collective-permute-done | bytes 393248 | tf_op jit(solution)/shard_map/ppermute | solution.py:94
  191.3 2.1 collective-permute-start.22
  193.5 9.6 %input_side.1 = (f32[384,1024]{1,0:T(8,128)}, bf16[16,24,1024]{2,1,0:T(8,128)(2,1)}, bf16[16,264,128]{2,1,0:T(8,128)(2,1)}) custom-call(s32[1]{0:T(128)} %bitcast.me_ref, bf16[512,384]{1,0:T(8,128)(2,1)} %get-tuple-element.170.refs_0_, bf16[512,384]{1,0:T(8,128)(2,1)} %copy-done.23, bf16[512,384]{1,0:T(8,128)(2,1)} %copy-done.24, ...), custom_call_target="tpu_custom_call" | custom-call | tf_op jit(solution)/shard_map/input_side/pallas_call | solution.py:286
  204.6 6.9 %all-to-all-start.3 = ((bf16[16,24,1024]{2,1,0:T(8,128)(2,1)}), bf16[16,24,1024]{2,1,0:T(8,128)(2,1)S(1)}, u32[]{:S(2)}, u32[]{:S(2)}) async-start(bf16[16,24,1024]{2,1,0:T(8,128)(2,1)} %get-tuple-element.183), calls=%async_computation.3 | async-start | bytes 1572864 | tf_op jit(solution)/shard_map/all_to_all | solution.py:369
  212.5 2.1 collective-permute-start.25
  214.6 8.1 %collective-permute-done.24.refs_3_ = bf16[512,384]{1,0:T(8,128)(2,1)S(1)} collective-permute-done((bf16[512,384]{1,0:T(8,128)(2,1)}, bf16[512,384]{1,0:T(8,128)(2,1)S(1)}, u32[]{:S(2)}, u32[]{:S(2)}) %collective-permute-start.24) | collective-permute-done | bytes 393248 | tf_op jit(solution)/shard_map/ppermute | solution.py:94
  226.7 6.5 %all-to-all-start.4 = ((bf16[16,264,128]{2,1,0:T(8,128)(2,1)}), bf16[16,264,128]{2,1,0:T(8,128)(2,1)S(1)}, u32[]{:S(2)}, u32[]{:S(2)}) async-start(bf16[16,264,128]{2,1,0:T(8,128)(2,1)} %get-tuple-element.192), calls=%async_computation.4 | async-start | bytes 2162688 | tf_op jit(solution)/shard_map/all_to_all | solution.py:31
  233.2 2.2 collective-permute-start.26
  236.2 2.3 fusion.1
  238.4 8.6 %collective-permute-done.26.refs_4_ = bf16[512,384]{1,0:T(8,128)(2,1)S(1)} collective-permute-done((bf16[512,384]{1,0:T(8,128)(2,1)}, bf16[512,384]{1,0:T(8,128)(2,1)S(1)}, u32[]{:S(2)}, u32[]{:S(2)}) %collective-permute-start.26) | collective-permute-done | bytes 393248 | tf_op jit(solution)/shard_map/ppermute | solution.py:94
  247.8 5.5 %collective-permute-done.27.refs_5_ = bf16[512,384]{1,0:T(8,128)(2,1)} collective-permute-done((bf16[512,384]{1,0:T(8,128)(2,1)}, bf16[512,384]{1,0:T(8,128)(2,1)}, u32[]{:S(2)}, u32[]{:S(2)}) %collective-permute-start.27) | collective-permute-done | bytes 393248 | tf_op jit(solution)/shard_map/ppermute | solution.py:94
  255.5 6.6 %all-to-all-start.5 = ((bf16[48,8,1024]{2,1,0:T(8,128)(2,1)}), bf16[48,8,1024]{2,1,0:T(8,128)(2,1)S(1)}, u32[]{:S(2)}, u32[]{:S(2)}) async-start(bf16[48,8,1024]{2,1,0:T(8,128)(2,1)} %copy.85), calls=%async_computation.5 | async-start | bytes 1572864 | tf_op jit(solution)/shard_map/all_to_all | solution.py:377
  262.1 9.2 %output_side.1 = (bf16[384,1024]{1,0:T(8,128)(2,1)}, bf16[8,128,512]{2,1,0:T(8,128)(2,1)}) custom-call(s32[1]{0:T(128)} %bitcast.me_ref, bf16[512,384]{1,0:T(8,128)(2,1)} %get-tuple-element.169.refs_0_, bf16[512,384]{1,0:T(8,128)(2,1)} %copy-done.20, bf16[512,384]{1,0:T(8,128)(2,1)} %copy-done.18, bf16[512,384]{1,0:T(8,128)(2,1)} %copy-done.21, ...), custom_call_target="tpu_custom_call" | custom-call | tf_op jit(solution)/shard_map/output_side/pallas_call | solution.py:235
  271.3 9.1 %all-to-all-done.5 = bf16[48,8,1024]{2,1,0:T(8,128)(2,1)S(1)} async-done(((bf16[48,8,1024]{2,1,0:T(8,128)(2,1)}), bf16[48,8,1024]{2,1,0:T(8,128)(2,1)S(1)}, u32[]{:S(2)}, u32[]{:S(2)}) %all-to-all-start.5) | async-done | bytes 786464 | tf_op jit(solution)/shard_map/all_to_all | solution.py:377
  280.4 3.9 %all-to-all-start.6 = ((bf16[16,64,512]{2,1,0:T(8,128)(2,1)}), bf16[16,64,512]{2,1,0:T(8,128)(2,1)S(1)}, u32[]{:S(2)}, u32[]{:S(2)}) async-start(bf16[16,64,512]{2,1,0:T(8,128)(2,1)} %bitcast.88), calls=%async_computation.6 | async-start | bytes 2097152 | tf_op jit(solution)/shard_map/all_to_all | solution.py:31
  284.3 2.7 fusion.3
  290.1 3.9 %collective-permute-start.30 = (f32[264,128]{1,0:T(8,128)S(1)}, f32[264,128]{1,0:T(8,128)S(1)}, u32[]{:S(2)}, u32[]{:S(2)}) collective-permute-start(f32[264,128]{1,0:T(8,128)S(1)} %bitcast_add_fusion.1), channel_id=1, source_target_pairs={{0,4},{1,5},{2,6},{3,7},{4,0},{5,1},{6,2},{7,3},{8,12},{9,13},{10,... | collective-permute-start | bytes 405512 | tf_op jit(solution)/shard_map/ppermute | solution.py:55
  294.8 10.0 %all-to-all-done.6 = bf16[16,64,512]{2,1,0:T(8,128)(2,1)S(1)} async-done(((bf16[16,64,512]{2,1,0:T(8,128)(2,1)}), bf16[16,64,512]{2,1,0:T(8,128)(2,1)S(1)}, u32[]{:S(2)}, u32[]{:S(2)}) %all-to-all-start.6) | async-done | bytes 1048608 | tf_op jit(solution)/shard_map/all_to_all | solution.py:31
  306.0 4.3 %all-to-all-start.7 = ((bf16[16,64,512]{2,1,0:T(8,128)(2,1)}), bf16[16,64,512]{2,1,0:T(8,128)(2,1)S(1)}, u32[]{:S(2)}, u32[]{:S(2)}) async-start(bf16[16,64,512]{2,1,0:T(8,128)(2,1)} %broadcast_in_dim.7), calls=%async_computation.7 | async-start | bytes 2097152 | tf_op jit(solution)/shard_map/all_to_all | solution.py:41
  310.5 2.7 fusion
  314.7 11.7 %all-to-all-done.7 = bf16[16,64,512]{2,1,0:T(8,128)(2,1)S(1)} async-done(((bf16[16,64,512]{2,1,0:T(8,128)(2,1)}), bf16[16,64,512]{2,1,0:T(8,128)(2,1)S(1)}, u32[]{:S(2)}, u32[]{:S(2)}) %all-to-all-start.7) | async-done | bytes 1048608 | tf_op jit(solution)/shard_map/all_to_all | solution.py:41
  326.5 3.3 fusion.12
  331.1 2.8 fusion.13
  (145 shorter events, 42.7 us)
Async XLA Ops:
  7.2 40.1 %copy-start = (bf16[8,48,48]{2,1,0:T(8,128)(2,1)S(1)}, bf16[8,48,48]{2,1,0:T(8,128)(2,1)}, u32[]{:S(2)}) copy-start(bf16[8,48,48]{2,1,0:T(8,128)(2,1)} %param.12) | copy-start | bytes 110596
  16.5 25.6 %all-to-all-start = ((bf16[3,128,1024]{2,0,1:T(4,128)(2,1)}), bf16[3,128,1024]{2,0,1:T(4,128)(2,1)S(1)}, u32[]{:S(2)}, u32[]{:S(2)}) async-start(bf16[3,128,1024]{2,0,1:T(4,128)(2,1)} %copy.74), calls=%async_computation | async-start | bytes 2097152 | tf_op jit(solution)/shard_map/all_to_all | solution.py:331
  24.5 18.0 %collective-permute-start = (bf16[512,384]{1,0:T(8,128)(2,1)}, bf16[512,384]{1,0:T(8,128)(2,1)S(1)}, u32[]{:S(2)}, u32[]{:S(2)}) collective-permute-start(bf16[512,384]{1,0:T(8,128)(2,1)} %get-tuple-element.118), channel_id=1, source_target_pairs={{0,1},{1,0},{2,3},{3,2},{4,5},{5,4},{6,7},{7,6},{8,9},{9,8},{10,11... | collective-permute-start | bytes 1179656 | tf_op jit(solution)/shard_map/ppermute | solution.py:94
  24.5 18.0 %collective-permute-start.1 = (bf16[512,384]{1,0:T(8,128)(2,1)}, bf16[512,384]{1,0:T(8,128)(2,1)S(1)}, u32[]{:S(2)}, u32[]{:S(2)}) collective-permute-start(bf16[512,384]{1,0:T(8,128)(2,1)} %get-tuple-element.119), channel_id=1, source_target_pairs={{0,2},{1,3},{2,0},{3,1},{4,6},{5,7},{6,4},{7,5},{8,10},{9,11},{10,... | collective-permute-start | bytes 1179656 | tf_op jit(solution)/shard_map/ppermute | solution.py:94
  26.2 18.0 %collective-permute-start.2 = (bf16[512,384]{1,0:T(8,128)(2,1)}, bf16[512,384]{1,0:T(8,128)(2,1)S(1)}, u32[]{:S(2)}, u32[]{:S(2)}) collective-permute-start(bf16[512,384]{1,0:T(8,128)(2,1)} %get-tuple-element.120), channel_id=1, source_target_pairs={{0,3},{1,2},{2,1},{3,0},{4,7},{5,6},{6,5},{7,4},{8,11},{9,10},{10,... | collective-permute-start | bytes 1179656 | tf_op jit(solution)/shard_map/ppermute | solution.py:94
  26.4 17.8 %collective-permute-start.3 = (bf16[512,384]{1,0:T(8,128)(2,1)}, bf16[512,384]{1,0:T(8,128)(2,1)}, u32[]{:S(2)}, u32[]{:S(2)}) collective-permute-start(bf16[512,384]{1,0:T(8,128)(2,1)} %get-tuple-element.121), channel_id=1, source_target_pairs={{0,6},{1,7},{2,4},{3,5},{4,2},{5,3},{6,0},{7,1},{8,14},{9,15},{10,... | collective-permute-start | bytes 1179656 | tf_op jit(solution)/shard_map/ppermute | solution.py:94
  29.4 17.9 %collective-permute-start.4 = (bf16[512,384]{1,0:T(8,128)(2,1)}, bf16[512,384]{1,0:T(8,128)(2,1)}, u32[]{:S(2)}, u32[]{:S(2)}) collective-permute-start(bf16[512,384]{1,0:T(8,128)(2,1)} %get-tuple-element.122), channel_id=1, source_target_pairs={{0,7},{1,6},{2,5},{3,4},{4,3},{5,2},{6,1},{7,0},{8,15},{9,14},{10,... | collective-permute-start | bytes 1179656 | tf_op jit(solution)/shard_map/ppermute | solution.py:94
  49.8 22.0 %all-to-all-start.1 = ((bf16[48,8,1024]{2,1,0:T(8,128)(2,1)}), bf16[48,8,1024]{2,1,0:T(8,128)(2,1)S(1)}, u32[]{:S(2)}, u32[]{:S(2)}) async-start(bf16[48,8,1024]{2,1,0:T(8,128)(2,1)} %copy.78), calls=%async_computation.1 | async-start | bytes 1572864 | tf_op jit(solution)/shard_map/all_to_all | solution.py:335
  56.9 14.9 %collective-permute-start.5 = (bf16[512,384]{1,0:T(8,128)(2,1)}, bf16[512,384]{1,0:T(8,128)(2,1)S(1)}, u32[]{:S(2)}, u32[]{:S(2)}) collective-permute-start(bf16[512,384]{1,0:T(8,128)(2,1)} %get-tuple-element.124), channel_id=1, source_target_pairs={{0,4},{1,5},{2,6},{3,7},{4,0},{5,1},{6,2},{7,3},{8,12},{9,13},{10,... | collective-permute-start | bytes 1179656 | tf_op jit(solution)/shard_map/ppermute | solution.py:94
  58.9 18.4 %collective-permute-start.6 = (bf16[512,384]{1,0:T(8,128)(2,1)}, bf16[512,384]{1,0:T(8,128)(2,1)S(1)}, u32[]{:S(2)}, u32[]{:S(2)}) collective-permute-start(bf16[512,384]{1,0:T(8,128)(2,1)} %get-tuple-element.125), channel_id=1, source_target_pairs={{0,5},{1,4},{2,7},{3,6},{4,1},{5,0},{6,3},{7,2},{8,13},{9,12},{10,... | collective-permute-start | bytes 1179656 | tf_op jit(solution)/shard_map/ppermute | solution.py:94
  84.2 13.9 %collective-permute-start.10 = (bf16[512,384]{1,0:T(8,128)(2,1)}, bf16[512,384]{1,0:T(8,128)(2,1)S(1)}, u32[]{:S(2)}, u32[]{:S(2)}) collective-permute-start(bf16[512,384]{1,0:T(8,128)(2,1)} %get-tuple-element.131), channel_id=1, source_target_pairs={{0,4},{1,5},{2,6},{3,7},{4,0},{5,1},{6,2},{7,3},{8,12},{9,13},{10,... | collective-permute-start | bytes 1179656 | tf_op jit(solution)/shard_map/ppermute | solution.py:94
  86.3 19.9 %collective-permute-start.11 = (bf16[512,384]{1,0:T(8,128)(2,1)}, bf16[512,384]{1,0:T(8,128)(2,1)}, u32[]{:S(2)}, u32[]{:S(2)}) collective-permute-start(bf16[512,384]{1,0:T(8,128)(2,1)} %get-tuple-element.132), channel_id=1, source_target_pairs={{0,5},{1,4},{2,7},{3,6},{4,1},{5,0},{6,3},{7,2},{8,13},{9,12},{10,... | collective-permute-start | bytes 1179656 | tf_op jit(solution)/shard_map/ppermute | solution.py:94
  87.9 26.9 %collective-permute-start.12 = (bf16[512,384]{1,0:T(8,128)(2,1)}, bf16[512,384]{1,0:T(8,128)(2,1)}, u32[]{:S(2)}, u32[]{:S(2)}) collective-permute-start(bf16[512,384]{1,0:T(8,128)(2,1)} %get-tuple-element.133), channel_id=1, source_target_pairs={{0,6},{1,7},{2,4},{3,5},{4,2},{5,3},{6,0},{7,1},{8,14},{9,15},{10,... | collective-permute-start | bytes 1179656 | tf_op jit(solution)/shard_map/ppermute | solution.py:94
  90.9 32.2 %collective-permute-start.13 = (bf16[512,384]{1,0:T(8,128)(2,1)}, bf16[512,384]{1,0:T(8,128)(2,1)}, u32[]{:S(2)}, u32[]{:S(2)}) collective-permute-start(bf16[512,384]{1,0:T(8,128)(2,1)} %get-tuple-element.134), channel_id=1, source_target_pairs={{0,7},{1,6},{2,5},{3,4},{4,3},{5,2},{6,1},{7,0},{8,15},{9,14},{10,... | collective-permute-start | bytes 1179656 | tf_op jit(solution)/shard_map/ppermute | solution.py:94
  90.9 32.2 %collective-permute-start.7 = (bf16[512,384]{1,0:T(8,128)(2,1)}, bf16[512,384]{1,0:T(8,128)(2,1)}, u32[]{:S(2)}, u32[]{:S(2)}) collective-permute-start(bf16[512,384]{1,0:T(8,128)(2,1)} %get-tuple-element.128), channel_id=1, source_target_pairs={{0,1},{1,0},{2,3},{3,2},{4,5},{5,4},{6,7},{7,6},{8,9},{9,8},{10,11... | collective-permute-start | bytes 1179656 | tf_op jit(solution)/shard_map/ppermute | solution.py:94
  98.1 25.0 %collective-permute-start.8 = (bf16[512,384]{1,0:T(8,128)(2,1)}, bf16[512,384]{1,0:T(8,128)(2,1)}, u32[]{:S(2)}, u32[]{:S(2)}) collective-permute-start(bf16[512,384]{1,0:T(8,128)(2,1)} %get-tuple-element.129), channel_id=1, source_target_pairs={{0,2},{1,3},{2,0},{3,1},{4,6},{5,7},{6,4},{7,5},{8,10},{9,11},{10,... | collective-permute-start | bytes 1179656 | tf_op jit(solution)/shard_map/ppermute | solution.py:94
  106.2 17.0 %collective-permute-start.9 = (bf16[512,384]{1,0:T(8,128)(2,1)}, bf16[512,384]{1,0:T(8,128)(2,1)}, u32[]{:S(2)}, u32[]{:S(2)}) collective-permute-start(bf16[512,384]{1,0:T(8,128)(2,1)} %get-tuple-element.130), channel_id=1, source_target_pairs={{0,3},{1,2},{2,1},{3,0},{4,7},{5,6},{6,5},{7,4},{8,11},{9,10},{10,... | collective-permute-start | bytes 1179656 | tf_op jit(solution)/shard_map/ppermute | solution.py:94
  140.2 16.4 %collective-permute-start.14 = (bf16[512,384]{1,0:T(8,128)(2,1)}, bf16[512,384]{1,0:T(8,128)(2,1)S(1)}, u32[]{:S(2)}, u32[]{:S(2)}) collective-permute-start(bf16[512,384]{1,0:T(8,128)(2,1)} %get-tuple-element.157), channel_id=1, source_target_pairs={{0,1},{1,0},{2,3},{3,2},{4,5},{5,4},{6,7},{7,6},{8,9},{9,8},{10,11... | collective-permute-start | bytes 1179656 | tf_op jit(solution)/shard_map/ppermute | solution.py:94
  140.4 16.2 %collective-permute-start.15 = (bf16[512,384]{1,0:T(8,128)(2,1)}, bf16[512,384]{1,0:T(8,128)(2,1)S(1)}, u32[]{:S(2)}, u32[]{:S(2)}) collective-permute-start(bf16[512,384]{1,0:T(8,128)(2,1)} %get-tuple-element.158), channel_id=1, source_target_pairs={{0,2},{1,3},{2,0},{3,1},{4,6},{5,7},{6,4},{7,5},{8,10},{9,11},{10,... | collective-permute-start | bytes 1179656 | tf_op jit(solution)/shard_map/ppermute | solution.py:94
  141.0 18.8 %collective-permute-start.16 = (bf16[512,384]{1,0:T(8,128)(2,1)}, bf16[512,384]{1,0:T(8,128)(2,1)S(1)}, u32[]{:S(2)}, u32[]{:S(2)}) collective-permute-start(bf16[512,384]{1,0:T(8,128)(2,1)} %get-tuple-element.159), channel_id=1, source_target_pairs={{0,3},{1,2},{2,1},{3,0},{4,7},{5,6},{6,5},{7,4},{8,11},{9,10},{10,... | collective-permute-start | bytes 1179656 | tf_op jit(solution)/shard_map/ppermute | solution.py:94
  142.1 17.7 %collective-permute-start.17 = (bf16[512,384]{1,0:T(8,128)(2,1)}, bf16[512,384]{1,0:T(8,128)(2,1)S(1)}, u32[]{:S(2)}, u32[]{:S(2)}) collective-permute-start(bf16[512,384]{1,0:T(8,128)(2,1)} %get-tuple-element.160), channel_id=1, source_target_pairs={{0,6},{1,7},{2,4},{3,5},{4,2},{5,3},{6,0},{7,1},{8,14},{9,15},{10,... | collective-permute-start | bytes 1179656 | tf_op jit(solution)/shard_map/ppermute | solution.py:94
  145.2 18.0 %collective-permute-start.18 = (bf16[512,384]{1,0:T(8,128)(2,1)}, bf16[512,384]{1,0:T(8,128)(2,1)}, u32[]{:S(2)}, u32[]{:S(2)}) collective-permute-start(bf16[512,384]{1,0:T(8,128)(2,1)} %get-tuple-element.161), channel_id=1, source_target_pairs={{0,7},{1,6},{2,5},{3,4},{4,3},{5,2},{6,1},{7,0},{8,15},{9,14},{10,... | collective-permute-start | bytes 1179656 | tf_op jit(solution)/shard_map/ppermute | solution.py:94
  156.6 36.9 %copy-start.23 = (bf16[512,384]{1,0:T(8,128)(2,1)}, bf16[512,384]{1,0:T(8,128)(2,1)S(1)}, u32[]{:S(2)}) copy-start(bf16[512,384]{1,0:T(8,128)(2,1)S(1)} %collective-permute-done.14.refs_1_) | copy-start | bytes 1179652
  156.6 33.9 %copy-start.24 = (bf16[512,384]{1,0:T(8,128)(2,1)}, bf16[512,384]{1,0:T(8,128)(2,1)S(1)}, u32[]{:S(2)}) copy-start(bf16[512,384]{1,0:T(8,128)(2,1)S(1)} %collective-permute-done.15.refs_2_) | copy-start | bytes 1179652
  159.8 30.7 %copy-start.25 = (bf16[512,384]{1,0:T(8,128)(2,1)}, bf16[512,384]{1,0:T(8,128)(2,1)S(1)}, u32[]{:S(2)}) copy-start(bf16[512,384]{1,0:T(8,128)(2,1)S(1)} %collective-permute-done.16.refs_3_) | copy-start | bytes 1179652
  159.8 30.7 %copy-start.26 = (bf16[512,384]{1,0:T(8,128)(2,1)}, bf16[512,384]{1,0:T(8,128)(2,1)S(1)}, u32[]{:S(2)}) copy-start(bf16[512,384]{1,0:T(8,128)(2,1)S(1)} %collective-permute-done.17.refs_6_) | copy-start | bytes 1179652
  163.2 40.7 %all-to-all-start.2 = ((bf16[16,256,128]{2,1,0:T(8,128)(2,1)}), bf16[16,256,128]{2,1,0:T(8,128)(2,1)S(1)}, u32[]{:S(2)}, u32[]{:S(2)}) async-start(bf16[16,256,128]{2,1,0:T(8,128)(2,1)} %bitcast.87), calls=%async_computation.2 | async-start | bytes 2097152 | tf_op jit(solution)/shard_map/all_to_all | solution.py:31
  170.1 13.8 %collective-permute-start.19 = (bf16[512,384]{1,0:T(8,128)(2,1)}, bf16[512,384]{1,0:T(8,128)(2,1)S(1)}, u32[]{:S(2)}, u32[]{:S(2)}) collective-permute-start(bf16[512,384]{1,0:T(8,128)(2,1)} %get-tuple-element.165), channel_id=1, source_target_pairs={{0,4},{1,5},{2,6},{3,7},{4,0},{5,1},{6,2},{7,3},{8,12},{9,13},{10,... | collective-permute-start | bytes 1179656 | tf_op jit(solution)/shard_map/ppermute | solution.py:94
  171.0 19.5 %collective-permute-start.20 = (bf16[512,384]{1,0:T(8,128)(2,1)}, bf16[512,384]{1,0:T(8,128)(2,1)S(1)}, u32[]{:S(2)}, u32[]{:S(2)}) collective-permute-start(bf16[512,384]{1,0:T(8,128)(2,1)} %get-tuple-element.166), channel_id=1, source_target_pairs={{0,5},{1,4},{2,7},{3,6},{4,1},{5,0},{6,3},{7,2},{8,13},{9,12},{10,... | collective-permute-start | bytes 1179656 | tf_op jit(solution)/shard_map/ppermute | solution.py:94
  190.6 12.5 %collective-permute-start.21 = (bf16[512,384]{1,0:T(8,128)(2,1)}, bf16[512,384]{1,0:T(8,128)(2,1)S(1)}, u32[]{:S(2)}, u32[]{:S(2)}) collective-permute-start(bf16[512,384]{1,0:T(8,128)(2,1)} %get-tuple-element.180), channel_id=1, source_target_pairs={{0,2},{1,3},{2,0},{3,1},{4,6},{5,7},{6,4},{7,5},{8,10},{9,11},{10,... | collective-permute-start | bytes 1179656 | tf_op jit(solution)/shard_map/ppermute | solution.py:94
  191.3 12.5 %collective-permute-start.22 = (bf16[512,384]{1,0:T(8,128)(2,1)}, bf16[512,384]{1,0:T(8,128)(2,1)S(1)}, u32[]{:S(2)}, u32[]{:S(2)}) collective-permute-start(bf16[512,384]{1,0:T(8,128)(2,1)} %get-tuple-element.181), channel_id=1, source_target_pairs={{0,6},{1,7},{2,4},{3,5},{4,2},{5,3},{6,0},{7,1},{8,14},{9,15},{10,... | collective-permute-start | bytes 1179656 | tf_op jit(solution)/shard_map/ppermute | solution.py:94
  203.1 33.0 %copy-start.18 = (bf16[512,384]{1,0:T(8,128)(2,1)}, bf16[512,384]{1,0:T(8,128)(2,1)S(1)}, u32[]{:S(2)}) copy-start(bf16[512,384]{1,0:T(8,128)(2,1)S(1)} %collective-permute-done.21.refs_2_) | copy-start | bytes 1179652
  204.6 21.2 %all-to-all-start.3 = ((bf16[16,24,1024]{2,1,0:T(8,128)(2,1)}), bf16[16,24,1024]{2,1,0:T(8,128)(2,1)S(1)}, u32[]{:S(2)}, u32[]{:S(2)}) async-start(bf16[16,24,1024]{2,1,0:T(8,128)(2,1)} %get-tuple-element.183), calls=%async_computation.3 | async-start | bytes 1572864 | tf_op jit(solution)/shard_map/all_to_all | solution.py:369
  211.5 3.1 collective-permute-start.23
  211.6 11.1 %collective-permute-start.24 = (bf16[512,384]{1,0:T(8,128)(2,1)}, bf16[512,384]{1,0:T(8,128)(2,1)S(1)}, u32[]{:S(2)}, u32[]{:S(2)}) collective-permute-start(bf16[512,384]{1,0:T(8,128)(2,1)} %get-tuple-element.185), channel_id=1, source_target_pairs={{0,3},{1,2},{2,1},{3,0},{4,7},{5,6},{6,5},{7,4},{8,11},{9,10},{10,... | collective-permute-start | bytes 1179656 | tf_op jit(solution)/shard_map/ppermute | solution.py:94
  212.5 12.7 %collective-permute-start.25 = (bf16[512,384]{1,0:T(8,128)(2,1)}, bf16[512,384]{1,0:T(8,128)(2,1)}, u32[]{:S(2)}, u32[]{:S(2)}) collective-permute-start(bf16[512,384]{1,0:T(8,128)(2,1)} %get-tuple-element.186), channel_id=1, source_target_pairs={{0,7},{1,6},{2,5},{3,4},{4,3},{5,2},{6,1},{7,0},{8,15},{9,14},{10,... | collective-permute-start | bytes 1179656 | tf_op jit(solution)/shard_map/ppermute | solution.py:94
  226.7 26.6 %all-to-all-start.4 = ((bf16[16,264,128]{2,1,0:T(8,128)(2,1)}), bf16[16,264,128]{2,1,0:T(8,128)(2,1)S(1)}, u32[]{:S(2)}, u32[]{:S(2)}) async-start(bf16[16,264,128]{2,1,0:T(8,128)(2,1)} %get-tuple-element.192), calls=%async_computation.4 | async-start | bytes 2162688 | tf_op jit(solution)/shard_map/all_to_all | solution.py:31
  233.2 93.3 %all-gather.2.cloned.1.call-start = ((), (), s32[]{:S(2)}) async-start(), calls=%async_computation.8 | async-start | bytes 2263040 | tf_op jit(solution)/shard_map/all_gather | solution.py:386
  233.2 13.8 %collective-permute-start.26 = (bf16[512,384]{1,0:T(8,128)(2,1)}, bf16[512,384]{1,0:T(8,128)(2,1)S(1)}, u32[]{:S(2)}, u32[]{:S(2)}) collective-permute-start(bf16[512,384]{1,0:T(8,128)(2,1)} %get-tuple-element.193), channel_id=1, source_target_pairs={{0,4},{1,5},{2,6},{3,7},{4,0},{5,1},{6,2},{7,3},{8,12},{9,13},{10,... | collective-permute-start | bytes 1179656 | tf_op jit(solution)/shard_map/ppermute | solution.py:94
  235.5 17.8 %collective-permute-start.27 = (bf16[512,384]{1,0:T(8,128)(2,1)}, bf16[512,384]{1,0:T(8,128)(2,1)}, u32[]{:S(2)}, u32[]{:S(2)}) collective-permute-start(bf16[512,384]{1,0:T(8,128)(2,1)} %get-tuple-element.194), channel_id=1, source_target_pairs={{0,5},{1,4},{2,7},{3,6},{4,1},{5,0},{6,3},{7,2},{8,13},{9,12},{10,... | collective-permute-start | bytes 1179656 | tf_op jit(solution)/shard_map/ppermute | solution.py:94
  255.5 24.9 %all-to-all-start.5 = ((bf16[48,8,1024]{2,1,0:T(8,128)(2,1)}), bf16[48,8,1024]{2,1,0:T(8,128)(2,1)S(1)}, u32[]{:S(2)}, u32[]{:S(2)}) async-start(bf16[48,8,1024]{2,1,0:T(8,128)(2,1)} %copy.85), calls=%async_computation.5 | async-start | bytes 1572864 | tf_op jit(solution)/shard_map/all_to_all | solution.py:377
  280.4 24.3 %all-to-all-start.6 = ((bf16[16,64,512]{2,1,0:T(8,128)(2,1)}), bf16[16,64,512]{2,1,0:T(8,128)(2,1)S(1)}, u32[]{:S(2)}, u32[]{:S(2)}) async-start(bf16[16,64,512]{2,1,0:T(8,128)(2,1)} %bitcast.88), calls=%async_computation.6 | async-start | bytes 2097152 | tf_op jit(solution)/shard_map/all_to_all | solution.py:31
  288.6 1.4 collective-permute-start.28
  290.0 20.3 %collective-permute-start.29 = (f32[264,128]{1,0:T(8,128)S(1)}, f32[264,128]{1,0:T(8,128)S(1)}, u32[]{:S(2)}, u32[]{:S(2)}) collective-permute-start(f32[264,128]{1,0:T(8,128)S(1)} %bitcast_add_fusion.1), channel_id=1, source_target_pairs={{0,2},{1,3},{2,0},{3,1},{4,6},{5,7},{6,4},{7,5},{8,10},{9,11},{10,... | collective-permute-start | bytes 405512 | tf_op jit(solution)/shard_map/ppermute | solution.py:55
  290.1 20.2 %collective-permute-start.30 = (f32[264,128]{1,0:T(8,128)S(1)}, f32[264,128]{1,0:T(8,128)S(1)}, u32[]{:S(2)}, u32[]{:S(2)}) collective-permute-start(f32[264,128]{1,0:T(8,128)S(1)} %bitcast_add_fusion.1), channel_id=1, source_target_pairs={{0,4},{1,5},{2,6},{3,7},{4,0},{5,1},{6,2},{7,3},{8,12},{9,13},{10,... | collective-permute-start | bytes 405512 | tf_op jit(solution)/shard_map/ppermute | solution.py:55
  294.0 16.3 %collective-permute-start.31 = (f32[264,128]{1,0:T(8,128)S(1)}, f32[264,128]{1,0:T(8,128)S(1)}, u32[]{:S(2)}, u32[]{:S(2)}) collective-permute-start(f32[264,128]{1,0:T(8,128)S(1)} %bitcast_add_fusion.1), channel_id=1, source_target_pairs={{0,6},{1,7},{2,4},{3,5},{4,2},{5,3},{6,0},{7,1},{8,14},{9,15},{10,... | collective-permute-start | bytes 405512 | tf_op jit(solution)/shard_map/ppermute | solution.py:55
  306.0 20.5 %all-to-all-start.7 = ((bf16[16,64,512]{2,1,0:T(8,128)(2,1)}), bf16[16,64,512]{2,1,0:T(8,128)(2,1)S(1)}, u32[]{:S(2)}, u32[]{:S(2)}) async-start(bf16[16,64,512]{2,1,0:T(8,128)(2,1)} %broadcast_in_dim.7), calls=%async_computation.7 | async-start | bytes 2097152 | tf_op jit(solution)/shard_map/all_to_all | solution.py:41
  310.4 2.8 collective-permute-start.32
  (24 other events, 223.2 us)
Sparse Core Ops, SparseCore 0:
  254.3 56.7 all-gather.1

commit v4 on v3

--- a/solution.py
+++ b/solution.py
@@ -388,7 +388,7 @@
     output, part_r2 = output_side(act_c, zed, cotangent, right_two, me1)
     back_first, part_r2 = together(back_first, part_r2)
     slice_r2 = add_parts(slice_parts(part_r2), scale_rows).astype(BF)
-    sum_r2, gathered = together(all_slices(slice_r2), gathered)
+    sum_r2 = all_slices(slice_r2)
     gathered = gathered.astype(F32)
     sum_left = gathered[:, :rows_left].reshape(part_left.shape)
     sum_r1 = gathered[:, rows_left : rows_left + half].reshape(right_one.shape)

time: 344 us -> 344 us (level)
  transfers between devices with their start and end apart: 42 -> 42, of which waited for: 24 -> 24; matrix products, arithmetic and copies ran while one was open for 5% -> 6% of each run, Pallas kernels for 8% -> 8%
where the time goes in v4:
time: 344 us; the launch traced here: 342 us
  waiting for transfers between devices  144 us (42%)
  starting transfers between devices  88.7 us (26%)
  Pallas kernels  55.7 us (16%)
  local copies, waits for them, and re-layouts  25.4 us (7%)
  between operations  14.6 us (4%)
  matrix products  9.56 us (3%)
  other arithmetic  4.75 us (1%)
    ppermute x28, waiting for transfers between devices, send(): lax.ppermute(pieces[d], 'mp', [(i, i ^ d) for i in range(n)])  86.5 us
    ppermute x28, starting transfers between devices, send(): lax.ppermute(pieces[d], 'mp', [(i, i ^ d) for i in range(n)])  33.6 us
    all_to_all x3, starting transfers between devices, slice_parts(): return lax.all_to_all(parts, 'dp', split_axis=0, concat_axis=0, tiled=True)  17.2 us
    pallas_call x1, Pallas kernels, middle_main(): pl.pallas_call(body, grid=(units // STEP,), in_specs=[pl.BlockSpec(memory...  17 us
    all_to_all x1, waiting for transfers between devices, per_device(): lax.all_to_all(first, 'dp', split_axis=1, concat_axis=0, tiled=True)  12.7 us
    all_to_all x1, waiting for transfers between devices, per_device(): lax.all_to_all(mixed_moved, 'dp', split_axis=0, concat_axis=1, tiled=True)  11.9 us
    all_to_all x1, waiting for transfers between devices, all_slices(): return lax.all_to_all(copies, 'dp', split_axis=0, concat_axis=0, tiled=True)  11.7 us
    unnamed x64, local copies, waits for them, and re-layouts  10.2 us
  transfers between devices with their start and end apart: 42, of which 24 were waited for; matrix products, arithmetic and copies ran while one was open for 6% of the time, Pallas kernels for 8%

profile of v4, /device:TPU:0, one launch (start us, length us, event | category | flops | bytes accessed | tf_op | source)
XLA Modules:
  0.0 342.4 jit_solution(2639931555909641731)
XLA Ops:
  7.2 2.3 copy.73
  9.9 4.9 %expand.2 = (bf16[512,384]{1,0:T(8,128)(2,1)}, bf16[512,384]{1,0:T(8,128)(2,1)}, bf16[512,384]{1,0:T(8,128)(2,1)}, bf16[512,384]{1,0:T(8,128)(2,1)}, bf16[512,38...) custom-call(s32[1]{0:T(128)} %bitcast.me_ref, ...), custom_call_target="tpu_custom_call" | custom-call | tf_op jit(solution)/shard_map/expand/pallas_call | solution.py:81
  16.5 8.0 %all-to-all-start = ((bf16[3,128,1024]{2,0,1:T(4,128)(2,1)}), bf16[3,128,1024]{2,0,1:T(4,128)(2,1)S(1)}, u32[]{:S(2)}, u32[]{:S(2)}) async-start(bf16[3,128,1024]{2,0,1:T(4,128)(2,1)} %copy.74), calls=%async_computation | async-start | bytes 2097152 | tf_op jit(solution)/shard_map/all_to_all | solution.py:331
  26.4 3.0 collective-permute-start.3
  29.4 12.7 %all-to-all-done = bf16[3,128,1024]{2,0,1:T(4,128)(2,1)S(1)} async-done(((bf16[3,128,1024]{2,0,1:T(4,128)(2,1)}), bf16[3,128,1024]{2,0,1:T(4,128)(2,1)S(1)}, u32[]{:S(2)}, u32[]{:S(2)}) %all-to-all-start) | async-done | bytes 786464 | tf_op jit(solution)/shard_map/all_to_all | solution.py:331
  44.2 3.1 collective-permute-done.4.refs_15_
  49.8 7.2 %all-to-all-start.1 = ((bf16[48,8,1024]{2,1,0:T(8,128)(2,1)}), bf16[48,8,1024]{2,1,0:T(8,128)(2,1)S(1)}, u32[]{:S(2)}, u32[]{:S(2)}) async-start(bf16[48,8,1024]{2,1,0:T(8,128)(2,1)} %copy.78), calls=%async_computation.1 | async-start | bytes 1572864 | tf_op jit(solution)/shard_map/all_to_all | solution.py:335
  56.9 1.9 collective-permute-start.5
  59.9 11.9 %all-to-all-done.1 = bf16[48,8,1024]{2,1,0:T(8,128)(2,1)S(1)} async-done(((bf16[48,8,1024]{2,1,0:T(8,128)(2,1)}), bf16[48,8,1024]{2,1,0:T(8,128)(2,1)S(1)}, u32[]{:S(2)}, u32[]{:S(2)}) %all-to-all-start.1) | async-done | bytes 786464 | tf_op jit(solution)/shard_map/all_to_all | solution.py:335
  71.8 5.4 %collective-permute-done.6.refs_13_ = bf16[512,384]{1,0:T(8,128)(2,1)S(1)} collective-permute-done((bf16[512,384]{1,0:T(8,128)(2,1)}, bf16[512,384]{1,0:T(8,128)(2,1)S(1)}, u32[]{:S(2)}, u32[]{:S(2)}) %collective-permute-start.6) | collective-permute-done | bytes 393248 | tf_op jit(solution)/shard_map/ppermute | solution.py:94
  79.2 5.0 %expand.3 = (bf16[512,384]{1,0:T(8,128)(2,1)}, bf16[512,384]{1,0:T(8,128)(2,1)}, bf16[512,384]{1,0:T(8,128)(2,1)}, bf16[512,384]{1,0:T(8,128)(2,1)}, bf16[512,38...) custom-call(s32[1]{0:T(128)} %bitcast.me_ref, ...), custom_call_target="tpu_custom_call" | custom-call | tf_op jit(solution)/shard_map/expand/pallas_call | solution.py:81
  84.2 2.1 collective-permute-start.10
  87.9 3.0 collective-permute-start.12
  91.3 6.8 %collective-permute-done.10.refs_4_ = bf16[512,384]{1,0:T(8,128)(2,1)S(1)} collective-permute-done((bf16[512,384]{1,0:T(8,128)(2,1)}, bf16[512,384]{1,0:T(8,128)(2,1)S(1)}, u32[]{:S(2)}, u32[]{:S(2)}) %collective-permute-start.10) | collective-permute-done | bytes 393248 | tf_op jit(solution)/shard_map/ppermute | solution.py:94
  99.1 7.1 %collective-permute-done.11.refs_5_ = bf16[512,384]{1,0:T(8,128)(2,1)} collective-permute-done((bf16[512,384]{1,0:T(8,128)(2,1)}, bf16[512,384]{1,0:T(8,128)(2,1)}, u32[]{:S(2)}, u32[]{:S(2)}) %collective-permute-start.11) | collective-permute-done | bytes 393248 | tf_op jit(solution)/shard_map/ppermute | solution.py:94
  109.6 5.2 %collective-permute-done.12.refs_6_ = bf16[512,384]{1,0:T(8,128)(2,1)} collective-permute-done((bf16[512,384]{1,0:T(8,128)(2,1)}, bf16[512,384]{1,0:T(8,128)(2,1)}, u32[]{:S(2)}, u32[]{:S(2)}) %collective-permute-start.12) | collective-permute-done | bytes 393248 | tf_op jit(solution)/shard_map/ppermute | solution.py:94
  114.8 8.3 %collective-permute-done.13.refs_7_ = bf16[512,384]{1,0:T(8,128)(2,1)} collective-permute-done((bf16[512,384]{1,0:T(8,128)(2,1)}, bf16[512,384]{1,0:T(8,128)(2,1)}, u32[]{:S(2)}, u32[]{:S(2)}) %collective-permute-start.13) | collective-permute-done | bytes 393248 | tf_op jit(solution)/shard_map/ppermute | solution.py:94
  123.2 17.0 %middle_main.1 = (bf16[512,384]{1,0:T(8,128)(2,1)}, bf16[512,384]{1,0:T(8,128)(2,1)}, bf16[512,384]{1,0:T(8,128)(2,1)}, bf16[512,384]{1,0:T(8,128)(2,1)}, bf16[5...) custom-call(s32[1]{0:T(128)} %bitcast.me_ref, ...), custom_call_target="tpu_custom_call" | custom-call | tf_op jit(solution)/shard_map/middle_main/pallas_call | solution.py:159
  142.1 3.1 collective-permute-start.17
  146.5 10.0 %middle_rest.1 = (bf16[512,384]{1,0:T(8,128)(2,1)}, bf16[512,384]{1,0:T(8,128)(2,1)}, bf16[512,384]{1,0:T(8,128)(2,1)}, bf16[512,384]{1,0:T(8,128)(2,1)}, bf16[5...) custom-call(s32[1]{0:T(128)} %bitcast.me_ref, ...), custom_call_target="tpu_custom_call" | custom-call | tf_op jit(solution)/shard_map/middle_rest/pallas_call | solution.py:190
  156.6 3.2 collective-permute-done.16.refs_3_
  159.8 3.4 collective-permute-done.18.refs_7_
  163.2 6.9 %all-to-all-start.2 = ((bf16[16,256,128]{2,1,0:T(8,128)(2,1)}), bf16[16,256,128]{2,1,0:T(8,128)(2,1)S(1)}, u32[]{:S(2)}, u32[]{:S(2)}) async-start(bf16[16,256,128]{2,1,0:T(8,128)(2,1)} %bitcast.87), calls=%async_computation.2 | async-start | bytes 2097152 | tf_op jit(solution)/shard_map/all_to_all | solution.py:31
  171.0 2.1 collective-permute-start.20
  173.1 10.7 %collective-permute-done.19.refs_4_ = bf16[512,384]{1,0:T(8,128)(2,1)S(1)} collective-permute-done((bf16[512,384]{1,0:T(8,128)(2,1)}, bf16[512,384]{1,0:T(8,128)(2,1)S(1)}, u32[]{:S(2)}, u32[]{:S(2)}) %collective-permute-start.19) | collective-permute-done | bytes 393248 | tf_op jit(solution)/shard_map/ppermute | solution.py:94
  183.9 6.7 %collective-permute-done.20.refs_5_ = bf16[512,384]{1,0:T(8,128)(2,1)S(1)} collective-permute-done((bf16[512,384]{1,0:T(8,128)(2,1)}, bf16[512,384]{1,0:T(8,128)(2,1)S(1)}, u32[]{:S(2)}, u32[]{:S(2)}) %collective-permute-start.20) | collective-permute-done | bytes 393248 | tf_op jit(solution)/shard_map/ppermute | solution.py:94
  191.3 2.1 collective-permute-start.22
  193.5 9.6 %input_side.1 = (f32[384,1024]{1,0:T(8,128)}, bf16[16,24,1024]{2,1,0:T(8,128)(2,1)}, bf16[16,264,128]{2,1,0:T(8,128)(2,1)}) custom-call(s32[1]{0:T(128)} %bitcast.me_ref, bf16[512,384]{1,0:T(8,128)(2,1)} %get-tuple-element.168.refs_0_, bf16[512,384]{1,0:T(8,128)(2,1)} %copy-done.23, bf16[512,384]{1,0:T(8,128)(2,1)} %copy-done.24, ...), custom_call_target="tpu_custom_call" | custom-call | tf_op jit(solution)/shard_map/input_side/pallas_call | solution.py:286
  204.6 6.9 %all-to-all-start.3 = ((bf16[16,24,1024]{2,1,0:T(8,128)(2,1)}), bf16[16,24,1024]{2,1,0:T(8,128)(2,1)S(1)}, u32[]{:S(2)}, u32[]{:S(2)}) async-start(bf16[16,24,1024]{2,1,0:T(8,128)(2,1)} %get-tuple-element.181), calls=%async_computation.3 | async-start | bytes 1572864 | tf_op jit(solution)/shard_map/all_to_all | solution.py:369
  212.5 2.1 collective-permute-start.25
  214.6 8.1 %collective-permute-done.24.refs_3_ = bf16[512,384]{1,0:T(8,128)(2,1)S(1)} collective-permute-done((bf16[512,384]{1,0:T(8,128)(2,1)}, bf16[512,384]{1,0:T(8,128)(2,1)S(1)}, u32[]{:S(2)}, u32[]{:S(2)}) %collective-permute-start.24) | collective-permute-done | bytes 393248 | tf_op jit(solution)/shard_map/ppermute | solution.py:94
  226.7 6.5 %all-to-all-start.4 = ((bf16[16,264,128]{2,1,0:T(8,128)(2,1)}), bf16[16,264,128]{2,1,0:T(8,128)(2,1)S(1)}, u32[]{:S(2)}, u32[]{:S(2)}) async-start(bf16[16,264,128]{2,1,0:T(8,128)(2,1)} %get-tuple-element.190), calls=%async_computation.4 | async-start | bytes 2162688 | tf_op jit(solution)/shard_map/all_to_all | solution.py:31
  233.2 2.2 collective-permute-start.26
  236.2 2.3 fusion.1
  238.4 8.6 %collective-permute-done.26.refs_4_ = bf16[512,384]{1,0:T(8,128)(2,1)S(1)} collective-permute-done((bf16[512,384]{1,0:T(8,128)(2,1)}, bf16[512,384]{1,0:T(8,128)(2,1)S(1)}, u32[]{:S(2)}, u32[]{:S(2)}) %collective-permute-start.26) | collective-permute-done | bytes 393248 | tf_op jit(solution)/shard_map/ppermute | solution.py:94
  247.8 5.5 %collective-permute-done.27.refs_5_ = bf16[512,384]{1,0:T(8,128)(2,1)} collective-permute-done((bf16[512,384]{1,0:T(8,128)(2,1)}, bf16[512,384]{1,0:T(8,128)(2,1)}, u32[]{:S(2)}, u32[]{:S(2)}) %collective-permute-start.27) | collective-permute-done | bytes 393248 | tf_op jit(solution)/shard_map/ppermute | solution.py:94
  255.5 6.6 %all-to-all-start.5 = ((bf16[48,8,1024]{2,1,0:T(8,128)(2,1)}), bf16[48,8,1024]{2,1,0:T(8,128)(2,1)S(1)}, u32[]{:S(2)}, u32[]{:S(2)}) async-start(bf16[48,8,1024]{2,1,0:T(8,128)(2,1)} %copy.85), calls=%async_computation.5 | async-start | bytes 1572864 | tf_op jit(solution)/shard_map/all_to_all | solution.py:377
  262.1 9.2 %output_side.1 = (bf16[384,1024]{1,0:T(8,128)(2,1)}, bf16[8,128,512]{2,1,0:T(8,128)(2,1)}) custom-call(s32[1]{0:T(128)} %bitcast.me_ref, bf16[512,384]{1,0:T(8,128)(2,1)} %get-tuple-element.167.refs_0_, bf16[512,384]{1,0:T(8,128)(2,1)} %copy-done.20, bf16[512,384]{1,0:T(8,128)(2,1)} %copy-done.18, bf16[512,384]{1,0:T(8,128)(2,1)} %copy-done.21, ...), custom_call_target="tpu_custom_call" | custom-call | tf_op jit(solution)/shard_map/output_side/pallas_call | solution.py:235
  271.3 9.1 %all-to-all-done.5 = bf16[48,8,1024]{2,1,0:T(8,128)(2,1)S(1)} async-done(((bf16[48,8,1024]{2,1,0:T(8,128)(2,1)}), bf16[48,8,1024]{2,1,0:T(8,128)(2,1)S(1)}, u32[]{:S(2)}, u32[]{:S(2)}) %all-to-all-start.5) | async-done | bytes 786464 | tf_op jit(solution)/shard_map/all_to_all | solution.py:377
  280.4 3.9 %all-to-all-start.6 = ((bf16[16,64,512]{2,1,0:T(8,128)(2,1)}), bf16[16,64,512]{2,1,0:T(8,128)(2,1)S(1)}, u32[]{:S(2)}, u32[]{:S(2)}) async-start(bf16[16,64,512]{2,1,0:T(8,128)(2,1)} %bitcast.88), calls=%async_computation.6 | async-start | bytes 2097152 | tf_op jit(solution)/shard_map/all_to_all | solution.py:31
  284.3 2.7 fusion.3
  290.1 3.9 %collective-permute-start.30 = (f32[264,128]{1,0:T(8,128)S(1)}, f32[264,128]{1,0:T(8,128)S(1)}, u32[]{:S(2)}, u32[]{:S(2)}) collective-permute-start(f32[264,128]{1,0:T(8,128)S(1)} %bitcast_add_fusion.1), channel_id=1, source_target_pairs={{0,4},{1,5},{2,6},{3,7},{4,0},{5,1},{6,2},{7,3},{8,12},{9,13},{10,... | collective-permute-start | bytes 405512 | tf_op jit(solution)/shard_map/ppermute | solution.py:55
  294.8 10.0 %all-to-all-done.6 = bf16[16,64,512]{2,1,0:T(8,128)(2,1)S(1)} async-done(((bf16[16,64,512]{2,1,0:T(8,128)(2,1)}), bf16[16,64,512]{2,1,0:T(8,128)(2,1)S(1)}, u32[]{:S(2)}, u32[]{:S(2)}) %all-to-all-start.6) | async-done | bytes 1048608 | tf_op jit(solution)/shard_map/all_to_all | solution.py:31
  306.0 4.3 %all-to-all-start.7 = ((bf16[16,64,512]{2,1,0:T(8,128)(2,1)}), bf16[16,64,512]{2,1,0:T(8,128)(2,1)S(1)}, u32[]{:S(2)}, u32[]{:S(2)}) async-start(bf16[16,64,512]{2,1,0:T(8,128)(2,1)} %broadcast_in_dim.16), calls=%async_computation.7 | async-start | bytes 2097152 | tf_op jit(solution)/shard_map/all_to_all | solution.py:41
  310.5 2.7 fusion
  314.7 11.7 %all-to-all-done.7 = bf16[16,64,512]{2,1,0:T(8,128)(2,1)S(1)} async-done(((bf16[16,64,512]{2,1,0:T(8,128)(2,1)}), bf16[16,64,512]{2,1,0:T(8,128)(2,1)S(1)}, u32[]{:S(2)}, u32[]{:S(2)}) %all-to-all-start.7) | async-done | bytes 1048608 | tf_op jit(solution)/shard_map/all_to_all | solution.py:41
  328.1 3.3 fusion.12
  331.4 2.8 fusion.13
  (145 shorter events, 42.7 us)
Async XLA Ops:
  7.2 40.1 %copy-start = (bf16[8,48,48]{2,1,0:T(8,128)(2,1)S(1)}, bf16[8,48,48]{2,1,0:T(8,128)(2,1)}, u32[]{:S(2)}) copy-start(bf16[8,48,48]{2,1,0:T(8,128)(2,1)} %param.12) | copy-start | bytes 110596
  16.5 25.6 %all-to-all-start = ((bf16[3,128,1024]{2,0,1:T(4,128)(2,1)}), bf16[3,128,1024]{2,0,1:T(4,128)(2,1)S(1)}, u32[]{:S(2)}, u32[]{:S(2)}) async-start(bf16[3,128,1024]{2,0,1:T(4,128)(2,1)} %copy.74), calls=%async_computation | async-start | bytes 2097152 | tf_op jit(solution)/shard_map/all_to_all | solution.py:331
  24.5 18.0 %collective-permute-start = (bf16[512,384]{1,0:T(8,128)(2,1)}, bf16[512,384]{1,0:T(8,128)(2,1)S(1)}, u32[]{:S(2)}, u32[]{:S(2)}) collective-permute-start(bf16[512,384]{1,0:T(8,128)(2,1)} %get-tuple-element.116), channel_id=1, source_target_pairs={{0,1},{1,0},{2,3},{3,2},{4,5},{5,4},{6,7},{7,6},{8,9},{9,8},{10,11... | collective-permute-start | bytes 1179656 | tf_op jit(solution)/shard_map/ppermute | solution.py:94
  24.5 18.0 %collective-permute-start.1 = (bf16[512,384]{1,0:T(8,128)(2,1)}, bf16[512,384]{1,0:T(8,128)(2,1)S(1)}, u32[]{:S(2)}, u32[]{:S(2)}) collective-permute-start(bf16[512,384]{1,0:T(8,128)(2,1)} %get-tuple-element.117), channel_id=1, source_target_pairs={{0,2},{1,3},{2,0},{3,1},{4,6},{5,7},{6,4},{7,5},{8,10},{9,11},{10,... | collective-permute-start | bytes 1179656 | tf_op jit(solution)/shard_map/ppermute | solution.py:94
  26.2 18.0 %collective-permute-start.2 = (bf16[512,384]{1,0:T(8,128)(2,1)}, bf16[512,384]{1,0:T(8,128)(2,1)S(1)}, u32[]{:S(2)}, u32[]{:S(2)}) collective-permute-start(bf16[512,384]{1,0:T(8,128)(2,1)} %get-tuple-element.118), channel_id=1, source_target_pairs={{0,3},{1,2},{2,1},{3,0},{4,7},{5,6},{6,5},{7,4},{8,11},{9,10},{10,... | collective-permute-start | bytes 1179656 | tf_op jit(solution)/shard_map/ppermute | solution.py:94
  26.4 17.8 %collective-permute-start.3 = (bf16[512,384]{1,0:T(8,128)(2,1)}, bf16[512,384]{1,0:T(8,128)(2,1)}, u32[]{:S(2)}, u32[]{:S(2)}) collective-permute-start(bf16[512,384]{1,0:T(8,128)(2,1)} %get-tuple-element.119), channel_id=1, source_target_pairs={{0,6},{1,7},{2,4},{3,5},{4,2},{5,3},{6,0},{7,1},{8,14},{9,15},{10,... | collective-permute-start | bytes 1179656 | tf_op jit(solution)/shard_map/ppermute | solution.py:94
  29.4 17.9 %collective-permute-start.4 = (bf16[512,384]{1,0:T(8,128)(2,1)}, bf16[512,384]{1,0:T(8,128)(2,1)}, u32[]{:S(2)}, u32[]{:S(2)}) collective-permute-start(bf16[512,384]{1,0:T(8,128)(2,1)} %get-tuple-element.120), channel_id=1, source_target_pairs={{0,7},{1,6},{2,5},{3,4},{4,3},{5,2},{6,1},{7,0},{8,15},{9,14},{10,... | collective-permute-start | bytes 1179656 | tf_op jit(solution)/shard_map/ppermute | solution.py:94
  49.8 22.0 %all-to-all-start.1 = ((bf16[48,8,1024]{2,1,0:T(8,128)(2,1)}), bf16[48,8,1024]{2,1,0:T(8,128)(2,1)S(1)}, u32[]{:S(2)}, u32[]{:S(2)}) async-start(bf16[48,8,1024]{2,1,0:T(8,128)(2,1)} %copy.78), calls=%async_computation.1 | async-start | bytes 1572864 | tf_op jit(solution)/shard_map/all_to_all | solution.py:335
  56.9 14.9 %collective-permute-start.5 = (bf16[512,384]{1,0:T(8,128)(2,1)}, bf16[512,384]{1,0:T(8,128)(2,1)S(1)}, u32[]{:S(2)}, u32[]{:S(2)}) collective-permute-start(bf16[512,384]{1,0:T(8,128)(2,1)} %get-tuple-element.122), channel_id=1, source_target_pairs={{0,4},{1,5},{2,6},{3,7},{4,0},{5,1},{6,2},{7,3},{8,12},{9,13},{10,... | collective-permute-start | bytes 1179656 | tf_op jit(solution)/shard_map/ppermute | solution.py:94
  58.9 18.4 %collective-permute-start.6 = (bf16[512,384]{1,0:T(8,128)(2,1)}, bf16[512,384]{1,0:T(8,128)(2,1)S(1)}, u32[]{:S(2)}, u32[]{:S(2)}) collective-permute-start(bf16[512,384]{1,0:T(8,128)(2,1)} %get-tuple-element.123), channel_id=1, source_target_pairs={{0,5},{1,4},{2,7},{3,6},{4,1},{5,0},{6,3},{7,2},{8,13},{9,12},{10,... | collective-permute-start | bytes 1179656 | tf_op jit(solution)/shard_map/ppermute | solution.py:94
  84.2 13.9 %collective-permute-start.10 = (bf16[512,384]{1,0:T(8,128)(2,1)}, bf16[512,384]{1,0:T(8,128)(2,1)S(1)}, u32[]{:S(2)}, u32[]{:S(2)}) collective-permute-start(bf16[512,384]{1,0:T(8,128)(2,1)} %get-tuple-element.129), channel_id=1, source_target_pairs={{0,4},{1,5},{2,6},{3,7},{4,0},{5,1},{6,2},{7,3},{8,12},{9,13},{10,... | collective-permute-start | bytes 1179656 | tf_op jit(solution)/shard_map/ppermute | solution.py:94
  86.3 19.9 %collective-permute-start.11 = (bf16[512,384]{1,0:T(8,128)(2,1)}, bf16[512,384]{1,0:T(8,128)(2,1)}, u32[]{:S(2)}, u32[]{:S(2)}) collective-permute-start(bf16[512,384]{1,0:T(8,128)(2,1)} %get-tuple-element.130), channel_id=1, source_target_pairs={{0,5},{1,4},{2,7},{3,6},{4,1},{5,0},{6,3},{7,2},{8,13},{9,12},{10,... | collective-permute-start | bytes 1179656 | tf_op jit(solution)/shard_map/ppermute | solution.py:94
  87.9 26.9 %collective-permute-start.12 = (bf16[512,384]{1,0:T(8,128)(2,1)}, bf16[512,384]{1,0:T(8,128)(2,1)}, u32[]{:S(2)}, u32[]{:S(2)}) collective-permute-start(bf16[512,384]{1,0:T(8,128)(2,1)} %get-tuple-element.131), channel_id=1, source_target_pairs={{0,6},{1,7},{2,4},{3,5},{4,2},{5,3},{6,0},{7,1},{8,14},{9,15},{10,... | collective-permute-start | bytes 1179656 | tf_op jit(solution)/shard_map/ppermute | solution.py:94
  90.9 32.2 %collective-permute-start.13 = (bf16[512,384]{1,0:T(8,128)(2,1)}, bf16[512,384]{1,0:T(8,128)(2,1)}, u32[]{:S(2)}, u32[]{:S(2)}) collective-permute-start(bf16[512,384]{1,0:T(8,128)(2,1)} %get-tuple-element.132), channel_id=1, source_target_pairs={{0,7},{1,6},{2,5},{3,4},{4,3},{5,2},{6,1},{7,0},{8,15},{9,14},{10,... | collective-permute-start | bytes 1179656 | tf_op jit(solution)/shard_map/ppermute | solution.py:94
  90.9 32.2 %collective-permute-start.7 = (bf16[512,384]{1,0:T(8,128)(2,1)}, bf16[512,384]{1,0:T(8,128)(2,1)}, u32[]{:S(2)}, u32[]{:S(2)}) collective-permute-start(bf16[512,384]{1,0:T(8,128)(2,1)} %get-tuple-element.126), channel_id=1, source_target_pairs={{0,1},{1,0},{2,3},{3,2},{4,5},{5,4},{6,7},{7,6},{8,9},{9,8},{10,11... | collective-permute-start | bytes 1179656 | tf_op jit(solution)/shard_map/ppermute | solution.py:94
  98.1 25.0 %collective-permute-start.8 = (bf16[512,384]{1,0:T(8,128)(2,1)}, bf16[512,384]{1,0:T(8,128)(2,1)}, u32[]{:S(2)}, u32[]{:S(2)}) collective-permute-start(bf16[512,384]{1,0:T(8,128)(2,1)} %get-tuple-element.127), channel_id=1, source_target_pairs={{0,2},{1,3},{2,0},{3,1},{4,6},{5,7},{6,4},{7,5},{8,10},{9,11},{10,... | collective-permute-start | bytes 1179656 | tf_op jit(solution)/shard_map/ppermute | solution.py:94
  106.2 17.0 %collective-permute-start.9 = (bf16[512,384]{1,0:T(8,128)(2,1)}, bf16[512,384]{1,0:T(8,128)(2,1)}, u32[]{:S(2)}, u32[]{:S(2)}) collective-permute-start(bf16[512,384]{1,0:T(8,128)(2,1)} %get-tuple-element.128), channel_id=1, source_target_pairs={{0,3},{1,2},{2,1},{3,0},{4,7},{5,6},{6,5},{7,4},{8,11},{9,10},{10,... | collective-permute-start | bytes 1179656 | tf_op jit(solution)/shard_map/ppermute | solution.py:94
  140.2 16.4 %collective-permute-start.14 = (bf16[512,384]{1,0:T(8,128)(2,1)}, bf16[512,384]{1,0:T(8,128)(2,1)S(1)}, u32[]{:S(2)}, u32[]{:S(2)}) collective-permute-start(bf16[512,384]{1,0:T(8,128)(2,1)} %get-tuple-element.155), channel_id=1, source_target_pairs={{0,1},{1,0},{2,3},{3,2},{4,5},{5,4},{6,7},{7,6},{8,9},{9,8},{10,11... | collective-permute-start | bytes 1179656 | tf_op jit(solution)/shard_map/ppermute | solution.py:94
  140.4 16.2 %collective-permute-start.15 = (bf16[512,384]{1,0:T(8,128)(2,1)}, bf16[512,384]{1,0:T(8,128)(2,1)S(1)}, u32[]{:S(2)}, u32[]{:S(2)}) collective-permute-start(bf16[512,384]{1,0:T(8,128)(2,1)} %get-tuple-element.156), channel_id=1, source_target_pairs={{0,2},{1,3},{2,0},{3,1},{4,6},{5,7},{6,4},{7,5},{8,10},{9,11},{10,... | collective-permute-start | bytes 1179656 | tf_op jit(solution)/shard_map/ppermute | solution.py:94
  141.0 18.8 %collective-permute-start.16 = (bf16[512,384]{1,0:T(8,128)(2,1)}, bf16[512,384]{1,0:T(8,128)(2,1)S(1)}, u32[]{:S(2)}, u32[]{:S(2)}) collective-permute-start(bf16[512,384]{1,0:T(8,128)(2,1)} %get-tuple-element.157), channel_id=1, source_target_pairs={{0,3},{1,2},{2,1},{3,0},{4,7},{5,6},{6,5},{7,4},{8,11},{9,10},{10,... | collective-permute-start | bytes 1179656 | tf_op jit(solution)/shard_map/ppermute | solution.py:94
  142.1 17.7 %collective-permute-start.17 = (bf16[512,384]{1,0:T(8,128)(2,1)}, bf16[512,384]{1,0:T(8,128)(2,1)S(1)}, u32[]{:S(2)}, u32[]{:S(2)}) collective-permute-start(bf16[512,384]{1,0:T(8,128)(2,1)} %get-tuple-element.158), channel_id=1, source_target_pairs={{0,6},{1,7},{2,4},{3,5},{4,2},{5,3},{6,0},{7,1},{8,14},{9,15},{10,... | collective-permute-start | bytes 1179656 | tf_op jit(solution)/shard_map/ppermute | solution.py:94
  145.2 18.0 %collective-permute-start.18 = (bf16[512,384]{1,0:T(8,128)(2,1)}, bf16[512,384]{1,0:T(8,128)(2,1)}, u32[]{:S(2)}, u32[]{:S(2)}) collective-permute-start(bf16[512,384]{1,0:T(8,128)(2,1)} %get-tuple-element.159), channel_id=1, source_target_pairs={{0,7},{1,6},{2,5},{3,4},{4,3},{5,2},{6,1},{7,0},{8,15},{9,14},{10,... | collective-permute-start | bytes 1179656 | tf_op jit(solution)/shard_map/ppermute | solution.py:94
  156.6 36.9 %copy-start.23 = (bf16[512,384]{1,0:T(8,128)(2,1)}, bf16[512,384]{1,0:T(8,128)(2,1)S(1)}, u32[]{:S(2)}) copy-start(bf16[512,384]{1,0:T(8,128)(2,1)S(1)} %collective-permute-done.14.refs_1_) | copy-start | bytes 1179652
  156.6 33.9 %copy-start.24 = (bf16[512,384]{1,0:T(8,128)(2,1)}, bf16[512,384]{1,0:T(8,128)(2,1)S(1)}, u32[]{:S(2)}) copy-start(bf16[512,384]{1,0:T(8,128)(2,1)S(1)} %collective-permute-done.15.refs_2_) | copy-start | bytes 1179652
  159.8 30.7 %copy-start.25 = (bf16[512,384]{1,0:T(8,128)(2,1)}, bf16[512,384]{1,0:T(8,128)(2,1)S(1)}, u32[]{:S(2)}) copy-start(bf16[512,384]{1,0:T(8,128)(2,1)S(1)} %collective-permute-done.16.refs_3_) | copy-start | bytes 1179652
  159.8 30.7 %copy-start.26 = (bf16[512,384]{1,0:T(8,128)(2,1)}, bf16[512,384]{1,0:T(8,128)(2,1)S(1)}, u32[]{:S(2)}) copy-start(bf16[512,384]{1,0:T(8,128)(2,1)S(1)} %collective-permute-done.17.refs_6_) | copy-start | bytes 1179652
  163.2 40.7 %all-to-all-start.2 = ((bf16[16,256,128]{2,1,0:T(8,128)(2,1)}), bf16[16,256,128]{2,1,0:T(8,128)(2,1)S(1)}, u32[]{:S(2)}, u32[]{:S(2)}) async-start(bf16[16,256,128]{2,1,0:T(8,128)(2,1)} %bitcast.87), calls=%async_computation.2 | async-start | bytes 2097152 | tf_op jit(solution)/shard_map/all_to_all | solution.py:31
  170.1 13.8 %collective-permute-start.19 = (bf16[512,384]{1,0:T(8,128)(2,1)}, bf16[512,384]{1,0:T(8,128)(2,1)S(1)}, u32[]{:S(2)}, u32[]{:S(2)}) collective-permute-start(bf16[512,384]{1,0:T(8,128)(2,1)} %get-tuple-element.163), channel_id=1, source_target_pairs={{0,4},{1,5},{2,6},{3,7},{4,0},{5,1},{6,2},{7,3},{8,12},{9,13},{10,... | collective-permute-start | bytes 1179656 | tf_op jit(solution)/shard_map/ppermute | solution.py:94
  171.0 19.5 %collective-permute-start.20 = (bf16[512,384]{1,0:T(8,128)(2,1)}, bf16[512,384]{1,0:T(8,128)(2,1)S(1)}, u32[]{:S(2)}, u32[]{:S(2)}) collective-permute-start(bf16[512,384]{1,0:T(8,128)(2,1)} %get-tuple-element.164), channel_id=1, source_target_pairs={{0,5},{1,4},{2,7},{3,6},{4,1},{5,0},{6,3},{7,2},{8,13},{9,12},{10,... | collective-permute-start | bytes 1179656 | tf_op jit(solution)/shard_map/ppermute | solution.py:94
  190.6 12.5 %collective-permute-start.21 = (bf16[512,384]{1,0:T(8,128)(2,1)}, bf16[512,384]{1,0:T(8,128)(2,1)S(1)}, u32[]{:S(2)}, u32[]{:S(2)}) collective-permute-start(bf16[512,384]{1,0:T(8,128)(2,1)} %get-tuple-element.178), channel_id=1, source_target_pairs={{0,2},{1,3},{2,0},{3,1},{4,6},{5,7},{6,4},{7,5},{8,10},{9,11},{10,... | collective-permute-start | bytes 1179656 | tf_op jit(solution)/shard_map/ppermute | solution.py:94
  191.3 12.5 %collective-permute-start.22 = (bf16[512,384]{1,0:T(8,128)(2,1)}, bf16[512,384]{1,0:T(8,128)(2,1)S(1)}, u32[]{:S(2)}, u32[]{:S(2)}) collective-permute-start(bf16[512,384]{1,0:T(8,128)(2,1)} %get-tuple-element.179), channel_id=1, source_target_pairs={{0,6},{1,7},{2,4},{3,5},{4,2},{5,3},{6,0},{7,1},{8,14},{9,15},{10,... | collective-permute-start | bytes 1179656 | tf_op jit(solution)/shard_map/ppermute | solution.py:94
  203.1 33.0 %copy-start.18 = (bf16[512,384]{1,0:T(8,128)(2,1)}, bf16[512,384]{1,0:T(8,128)(2,1)S(1)}, u32[]{:S(2)}) copy-start(bf16[512,384]{1,0:T(8,128)(2,1)S(1)} %collective-permute-done.21.refs_2_) | copy-start | bytes 1179652
  204.6 21.2 %all-to-all-start.3 = ((bf16[16,24,1024]{2,1,0:T(8,128)(2,1)}), bf16[16,24,1024]{2,1,0:T(8,128)(2,1)S(1)}, u32[]{:S(2)}, u32[]{:S(2)}) async-start(bf16[16,24,1024]{2,1,0:T(8,128)(2,1)} %get-tuple-element.181), calls=%async_computation.3 | async-start | bytes 1572864 | tf_op jit(solution)/shard_map/all_to_all | solution.py:369
  211.5 3.1 collective-permute-start.23
  211.6 11.1 %collective-permute-start.24 = (bf16[512,384]{1,0:T(8,128)(2,1)}, bf16[512,384]{1,0:T(8,128)(2,1)S(1)}, u32[]{:S(2)}, u32[]{:S(2)}) collective-permute-start(bf16[512,384]{1,0:T(8,128)(2,1)} %get-tuple-element.183), channel_id=1, source_target_pairs={{0,3},{1,2},{2,1},{3,0},{4,7},{5,6},{6,5},{7,4},{8,11},{9,10},{10,... | collective-permute-start | bytes 1179656 | tf_op jit(solution)/shard_map/ppermute | solution.py:94
  212.5 12.7 %collective-permute-start.25 = (bf16[512,384]{1,0:T(8,128)(2,1)}, bf16[512,384]{1,0:T(8,128)(2,1)}, u32[]{:S(2)}, u32[]{:S(2)}) collective-permute-start(bf16[512,384]{1,0:T(8,128)(2,1)} %get-tuple-element.184), channel_id=1, source_target_pairs={{0,7},{1,6},{2,5},{3,4},{4,3},{5,2},{6,1},{7,0},{8,15},{9,14},{10,... | collective-permute-start | bytes 1179656 | tf_op jit(solution)/shard_map/ppermute | solution.py:94
  226.7 26.6 %all-to-all-start.4 = ((bf16[16,264,128]{2,1,0:T(8,128)(2,1)}), bf16[16,264,128]{2,1,0:T(8,128)(2,1)S(1)}, u32[]{:S(2)}, u32[]{:S(2)}) async-start(bf16[16,264,128]{2,1,0:T(8,128)(2,1)} %get-tuple-element.190), calls=%async_computation.4 | async-start | bytes 2162688 | tf_op jit(solution)/shard_map/all_to_all | solution.py:31
  233.2 94.9 %all-gather.2.cloned.1.call-start = ((), (), s32[]{:S(2)}) async-start(), calls=%async_computation.8 | async-start | bytes 2263040 | tf_op jit(solution)/shard_map/all_gather | solution.py:386
  233.2 13.8 %collective-permute-start.26 = (bf16[512,384]{1,0:T(8,128)(2,1)}, bf16[512,384]{1,0:T(8,128)(2,1)S(1)}, u32[]{:S(2)}, u32[]{:S(2)}) collective-permute-start(bf16[512,384]{1,0:T(8,128)(2,1)} %get-tuple-element.191), channel_id=1, source_target_pairs={{0,4},{1,5},{2,6},{3,7},{4,0},{5,1},{6,2},{7,3},{8,12},{9,13},{10,... | collective-permute-start | bytes 1179656 | tf_op jit(solution)/shard_map/ppermute | solution.py:94
  235.5 17.8 %collective-permute-start.27 = (bf16[512,384]{1,0:T(8,128)(2,1)}, bf16[512,384]{1,0:T(8,128)(2,1)}, u32[]{:S(2)}, u32[]{:S(2)}) collective-permute-start(bf16[512,384]{1,0:T(8,128)(2,1)} %get-tuple-element.192), channel_id=1, source_target_pairs={{0,5},{1,4},{2,7},{3,6},{4,1},{5,0},{6,3},{7,2},{8,13},{9,12},{10,... | collective-permute-start | bytes 1179656 | tf_op jit(solution)/shard_map/ppermute | solution.py:94
  255.5 24.9 %all-to-all-start.5 = ((bf16[48,8,1024]{2,1,0:T(8,128)(2,1)}), bf16[48,8,1024]{2,1,0:T(8,128)(2,1)S(1)}, u32[]{:S(2)}, u32[]{:S(2)}) async-start(bf16[48,8,1024]{2,1,0:T(8,128)(2,1)} %copy.85), calls=%async_computation.5 | async-start | bytes 1572864 | tf_op jit(solution)/shard_map/all_to_all | solution.py:377
  280.4 24.3 %all-to-all-start.6 = ((bf16[16,64,512]{2,1,0:T(8,128)(2,1)}), bf16[16,64,512]{2,1,0:T(8,128)(2,1)S(1)}, u32[]{:S(2)}, u32[]{:S(2)}) async-start(bf16[16,64,512]{2,1,0:T(8,128)(2,1)} %bitcast.88), calls=%async_computation.6 | async-start | bytes 2097152 | tf_op jit(solution)/shard_map/all_to_all | solution.py:31
  288.6 1.4 collective-permute-start.28
  290.0 20.3 %collective-permute-start.29 = (f32[264,128]{1,0:T(8,128)S(1)}, f32[264,128]{1,0:T(8,128)S(1)}, u32[]{:S(2)}, u32[]{:S(2)}) collective-permute-start(f32[264,128]{1,0:T(8,128)S(1)} %bitcast_add_fusion.1), channel_id=1, source_target_pairs={{0,2},{1,3},{2,0},{3,1},{4,6},{5,7},{6,4},{7,5},{8,10},{9,11},{10,... | collective-permute-start | bytes 405512 | tf_op jit(solution)/shard_map/ppermute | solution.py:55
  290.1 20.2 %collective-permute-start.30 = (f32[264,128]{1,0:T(8,128)S(1)}, f32[264,128]{1,0:T(8,128)S(1)}, u32[]{:S(2)}, u32[]{:S(2)}) collective-permute-start(f32[264,128]{1,0:T(8,128)S(1)} %bitcast_add_fusion.1), channel_id=1, source_target_pairs={{0,4},{1,5},{2,6},{3,7},{4,0},{5,1},{6,2},{7,3},{8,12},{9,13},{10,... | collective-permute-start | bytes 405512 | tf_op jit(solution)/shard_map/ppermute | solution.py:55
  294.0 16.3 %collective-permute-start.31 = (f32[264,128]{1,0:T(8,128)S(1)}, f32[264,128]{1,0:T(8,128)S(1)}, u32[]{:S(2)}, u32[]{:S(2)}) collective-permute-start(f32[264,128]{1,0:T(8,128)S(1)} %bitcast_add_fusion.1), channel_id=1, source_target_pairs={{0,6},{1,7},{2,4},{3,5},{4,2},{5,3},{6,0},{7,1},{8,14},{9,15},{10,... | collective-permute-start | bytes 405512 | tf_op jit(solution)/shard_map/ppermute | solution.py:55
  306.0 20.5 %all-to-all-start.7 = ((bf16[16,64,512]{2,1,0:T(8,128)(2,1)}), bf16[16,64,512]{2,1,0:T(8,128)(2,1)S(1)}, u32[]{:S(2)}, u32[]{:S(2)}) async-start(bf16[16,64,512]{2,1,0:T(8,128)(2,1)} %broadcast_in_dim.16), calls=%async_computation.7 | async-start | bytes 2097152 | tf_op jit(solution)/shard_map/all_to_all | solution.py:41
  310.4 2.8 collective-permute-start.32
  (24 other events, 222.9 us)
Sparse Core Ops, SparseCore 0:
  254.3 56.7 all-gather.1

commit v5 on v4

--- a/solution.py
+++ b/solution.py
@@ -352,7 +352,7 @@
     left_parts = slice_parts(part_left)
 
     pieces_c, back_a = together(pieces_c, back_a)
-    act_c1 = send(pieces_c, 2, 6)
+    act_c1 = send(pieces_c, 2, 6, 1)
     back_z, back_mixed, part_r1 = input_side(
         back_a,
         zed,
@@ -365,7 +365,7 @@
     )
     back_mixed, act_c1, left_parts = together(back_mixed, act_c1, left_parts)
     back_z = back_z.reshape(blocks_here, block_len, cols_here)
-    act_c2 = send(pieces_c, 3, 7, 1)
+    act_c2 = send(pieces_c, 3, 7)
     back_mixed_moved = lax.all_to_all(back_mixed, "dp", split_axis=0, concat_axis=0, tiled=True)
     back_mixed_moved = back_mixed_moved.reshape(first_moved.shape)
     back_mixed_moved, act_c2, part_r1 = together(back_mixed_moved, act_c2, part_r1)

time: 344 us -> 342 us (level)
  transfers between devices with their start and end apart: 42 -> 42, of which waited for: 24 -> 23; matrix products, arithmetic and copies ran while one was open for 6% -> 6% of each run, Pallas kernels for 8% -> 8%
where the time goes in v5:
time: 342 us; the launch traced here: 340 us
  waiting for transfers between devices  142 us (42%)
  starting transfers between devices  88 us (26%)
  Pallas kernels  55.7 us (16%)
  local copies, waits for them, and re-layouts  25.4 us (7%)
  between operations  14.6 us (4%)
  matrix products  9.56 us (3%)
  other arithmetic  4.75 us (1%)
    ppermute x28, waiting for transfers between devices, send(): lax.ppermute(pieces[d], 'mp', [(i, i ^ d) for i in range(n)])  85.3 us
    ppermute x28, starting transfers between devices, send(): lax.ppermute(pieces[d], 'mp', [(i, i ^ d) for i in range(n)])  34.5 us
    pallas_call x1, Pallas kernels, middle_main(): pl.pallas_call(body, grid=(units // STEP,), in_specs=[pl.BlockSpec(memory...  17 us
    all_to_all x3, starting transfers between devices, slice_parts(): return lax.all_to_all(parts, 'dp', split_axis=0, concat_axis=0, tiled=True)  15.8 us
    all_to_all x1, waiting for transfers between devices, per_device(): lax.all_to_all(first, 'dp', split_axis=1, concat_axis=0, tiled=True)  12.7 us
    all_to_all x1, waiting for transfers between devices, per_device(): lax.all_to_all(mixed_moved, 'dp', split_axis=0, concat_axis=1, tiled=True)  11.9 us
    all_to_all x1, waiting for transfers between devices, all_slices(): return lax.all_to_all(copies, 'dp', split_axis=0, concat_axis=0, tiled=True)  11.4 us
    unnamed x64, local copies, waits for them, and re-layouts  10.3 us
  transfers between devices with their start and end apart: 42, of which 23 were waited for; matrix products, arithmetic and copies ran while one was open for 6% of the time, Pallas kernels for 8%

profile of v5, /device:TPU:0, one launch (start us, length us, event | category | flops | bytes accessed | tf_op | source)
XLA Modules:
  0.0 340.4 jit_solution(4940416746781055887)
XLA Ops:
  7.2 2.3 copy.73
  9.9 4.9 %expand.2 = (bf16[512,384]{1,0:T(8,128)(2,1)}, bf16[512,384]{1,0:T(8,128)(2,1)}, bf16[512,384]{1,0:T(8,128)(2,1)}, bf16[512,384]{1,0:T(8,128)(2,1)}, bf16[512,38...) custom-call(s32[1]{0:T(128)} %bitcast.me_ref, ...), custom_call_target="tpu_custom_call" | custom-call | tf_op jit(solution)/shard_map/expand/pallas_call | solution.py:81
  16.5 8.0 %all-to-all-start = ((bf16[3,128,1024]{2,0,1:T(4,128)(2,1)}), bf16[3,128,1024]{2,0,1:T(4,128)(2,1)S(1)}, u32[]{:S(2)}, u32[]{:S(2)}) async-start(bf16[3,128,1024]{2,0,1:T(4,128)(2,1)} %copy.74), calls=%async_computation | async-start | bytes 2097152 | tf_op jit(solution)/shard_map/all_to_all | solution.py:331
  26.4 3.0 collective-permute-start.3
  29.4 12.7 %all-to-all-done = bf16[3,128,1024]{2,0,1:T(4,128)(2,1)S(1)} async-done(((bf16[3,128,1024]{2,0,1:T(4,128)(2,1)}), bf16[3,128,1024]{2,0,1:T(4,128)(2,1)S(1)}, u32[]{:S(2)}, u32[]{:S(2)}) %all-to-all-start) | async-done | bytes 786464 | tf_op jit(solution)/shard_map/all_to_all | solution.py:331
  44.2 3.1 collective-permute-done.4.refs_15_
  49.8 7.2 %all-to-all-start.1 = ((bf16[48,8,1024]{2,1,0:T(8,128)(2,1)}), bf16[48,8,1024]{2,1,0:T(8,128)(2,1)S(1)}, u32[]{:S(2)}, u32[]{:S(2)}) async-start(bf16[48,8,1024]{2,1,0:T(8,128)(2,1)} %copy.78), calls=%async_computation.1 | async-start | bytes 1572864 | tf_op jit(solution)/shard_map/all_to_all | solution.py:335
  59.9 11.9 %all-to-all-done.1 = bf16[48,8,1024]{2,1,0:T(8,128)(2,1)S(1)} async-done(((bf16[48,8,1024]{2,1,0:T(8,128)(2,1)}), bf16[48,8,1024]{2,1,0:T(8,128)(2,1)S(1)}, u32[]{:S(2)}, u32[]{:S(2)}) %all-to-all-start.1) | async-done | bytes 786464 | tf_op jit(solution)/shard_map/all_to_all | solution.py:335
  71.8 5.4 %collective-permute-done.6.refs_13_ = bf16[512,384]{1,0:T(8,128)(2,1)S(1)} collective-permute-done((bf16[512,384]{1,0:T(8,128)(2,1)}, bf16[512,384]{1,0:T(8,128)(2,1)S(1)}, u32[]{:S(2)}, u32[]{:S(2)}) %collective-permute-start.6) | collective-permute-done | bytes 393248 | tf_op jit(solution)/shard_map/ppermute | solution.py:94
  79.2 5.0 %expand.3 = (bf16[512,384]{1,0:T(8,128)(2,1)}, bf16[512,384]{1,0:T(8,128)(2,1)}, bf16[512,384]{1,0:T(8,128)(2,1)}, bf16[512,384]{1,0:T(8,128)(2,1)}, bf16[512,38...) custom-call(s32[1]{0:T(128)} %bitcast.me_ref, ...), custom_call_target="tpu_custom_call" | custom-call | tf_op jit(solution)/shard_map/expand/pallas_call | solution.py:81
  84.2 2.1 collective-permute-start.10
  87.9 3.0 collective-permute-start.12
  91.3 6.8 %collective-permute-done.10.refs_4_ = bf16[512,384]{1,0:T(8,128)(2,1)S(1)} collective-permute-done((bf16[512,384]{1,0:T(8,128)(2,1)}, bf16[512,384]{1,0:T(8,128)(2,1)S(1)}, u32[]{:S(2)}, u32[]{:S(2)}) %collective-permute-start.10) | collective-permute-done | bytes 393248 | tf_op jit(solution)/shard_map/ppermute | solution.py:94
  99.1 7.1 %collective-permute-done.11.refs_5_ = bf16[512,384]{1,0:T(8,128)(2,1)} collective-permute-done((bf16[512,384]{1,0:T(8,128)(2,1)}, bf16[512,384]{1,0:T(8,128)(2,1)}, u32[]{:S(2)}, u32[]{:S(2)}) %collective-permute-start.11) | collective-permute-done | bytes 393248 | tf_op jit(solution)/shard_map/ppermute | solution.py:94
  109.6 5.2 %collective-permute-done.12.refs_6_ = bf16[512,384]{1,0:T(8,128)(2,1)} collective-permute-done((bf16[512,384]{1,0:T(8,128)(2,1)}, bf16[512,384]{1,0:T(8,128)(2,1)}, u32[]{:S(2)}, u32[]{:S(2)}) %collective-permute-start.12) | collective-permute-done | bytes 393248 | tf_op jit(solution)/shard_map/ppermute | solution.py:94
  114.8 8.3 %collective-permute-done.13.refs_7_ = bf16[512,384]{1,0:T(8,128)(2,1)} collective-permute-done((bf16[512,384]{1,0:T(8,128)(2,1)}, bf16[512,384]{1,0:T(8,128)(2,1)}, u32[]{:S(2)}, u32[]{:S(2)}) %collective-permute-start.13) | collective-permute-done | bytes 393248 | tf_op jit(solution)/shard_map/ppermute | solution.py:94
  123.2 17.0 %middle_main.1 = (bf16[512,384]{1,0:T(8,128)(2,1)}, bf16[512,384]{1,0:T(8,128)(2,1)}, bf16[512,384]{1,0:T(8,128)(2,1)}, bf16[512,384]{1,0:T(8,128)(2,1)}, bf16[5...) custom-call(s32[1]{0:T(128)} %bitcast.me_ref, ...), custom_call_target="tpu_custom_call" | custom-call | tf_op jit(solution)/shard_map/middle_main/pallas_call | solution.py:159
  142.1 3.1 collective-permute-start.17
  146.5 10.0 %middle_rest.1 = (bf16[512,384]{1,0:T(8,128)(2,1)}, bf16[512,384]{1,0:T(8,128)(2,1)}, bf16[512,384]{1,0:T(8,128)(2,1)}, bf16[512,384]{1,0:T(8,128)(2,1)}, bf16[5...) custom-call(s32[1]{0:T(128)} %bitcast.me_ref, ...), custom_call_target="tpu_custom_call" | custom-call | tf_op jit(solution)/shard_map/middle_rest/pallas_call | solution.py:190
  156.6 3.2 collective-permute-done.16.refs_3_
  159.8 3.4 collective-permute-done.18.refs_7_
  163.2 6.9 %all-to-all-start.2 = ((bf16[16,256,128]{2,1,0:T(8,128)(2,1)}), bf16[16,256,128]{2,1,0:T(8,128)(2,1)S(1)}, u32[]{:S(2)}, u32[]{:S(2)}) async-start(bf16[16,256,128]{2,1,0:T(8,128)(2,1)} %bitcast.87), calls=%async_computation.2 | async-start | bytes 2097152 | tf_op jit(solution)/shard_map/all_to_all | solution.py:31
  171.0 2.1 collective-permute-start.20
  173.1 10.7 %collective-permute-done.19.refs_4_ = bf16[512,384]{1,0:T(8,128)(2,1)S(1)} collective-permute-done((bf16[512,384]{1,0:T(8,128)(2,1)}, bf16[512,384]{1,0:T(8,128)(2,1)S(1)}, u32[]{:S(2)}, u32[]{:S(2)}) %collective-permute-start.19) | collective-permute-done | bytes 393248 | tf_op jit(solution)/shard_map/ppermute | solution.py:94
  183.9 6.7 %collective-permute-done.20.refs_5_ = bf16[512,384]{1,0:T(8,128)(2,1)S(1)} collective-permute-done((bf16[512,384]{1,0:T(8,128)(2,1)}, bf16[512,384]{1,0:T(8,128)(2,1)S(1)}, u32[]{:S(2)}, u32[]{:S(2)}) %collective-permute-start.20) | collective-permute-done | bytes 393248 | tf_op jit(solution)/shard_map/ppermute | solution.py:94
  191.7 2.4 collective-permute-start.23
  194.1 9.6 %input_side.1 = (f32[384,1024]{1,0:T(8,128)}, bf16[16,24,1024]{2,1,0:T(8,128)(2,1)}, bf16[16,264,128]{2,1,0:T(8,128)(2,1)}) custom-call(s32[1]{0:T(128)} %bitcast.me_ref, bf16[512,384]{1,0:T(8,128)(2,1)} %get-tuple-element.168.refs_0_, bf16[512,384]{1,0:T(8,128)(2,1)} %copy-done.22, bf16[512,384]{1,0:T(8,128)(2,1)} %copy-done.24, ...), custom_call_target="tpu_custom_call" | custom-call | tf_op jit(solution)/shard_map/input_side/pallas_call | solution.py:286
  204.8 6.8 %all-to-all-start.3 = ((bf16[16,24,1024]{2,1,0:T(8,128)(2,1)}), bf16[16,24,1024]{2,1,0:T(8,128)(2,1)S(1)}, u32[]{:S(2)}, u32[]{:S(2)}) async-start(bf16[16,24,1024]{2,1,0:T(8,128)(2,1)} %get-tuple-element.184), calls=%async_computation.3 | async-start | bytes 1572864 | tf_op jit(solution)/shard_map/all_to_all | solution.py:369
  211.9 2.7 collective-permute-start.25
  214.6 8.6 %collective-permute-done.24.refs_3_ = bf16[512,384]{1,0:T(8,128)(2,1)S(1)} collective-permute-done((bf16[512,384]{1,0:T(8,128)(2,1)}, bf16[512,384]{1,0:T(8,128)(2,1)S(1)}, u32[]{:S(2)}, u32[]{:S(2)}) %collective-permute-start.24) | collective-permute-done | bytes 393248 | tf_op jit(solution)/shard_map/ppermute | solution.py:94
  223.9 2.1 all-to-all-done.3
  227.0 5.0 %all-to-all-start.4 = ((bf16[16,264,128]{2,1,0:T(8,128)(2,1)}), bf16[16,264,128]{2,1,0:T(8,128)(2,1)S(1)}, u32[]{:S(2)}, u32[]{:S(2)}) async-start(bf16[16,264,128]{2,1,0:T(8,128)(2,1)} %get-tuple-element.190), calls=%async_computation.4 | async-start | bytes 2162688 | tf_op jit(solution)/shard_map/all_to_all | solution.py:31
  232.0 2.7 collective-permute-start.26
  235.4 2.3 fusion.1
  237.7 8.1 %collective-permute-done.26.refs_4_ = bf16[512,384]{1,0:T(8,128)(2,1)S(1)} collective-permute-done((bf16[512,384]{1,0:T(8,128)(2,1)}, bf16[512,384]{1,0:T(8,128)(2,1)S(1)}, u32[]{:S(2)}, u32[]{:S(2)}) %collective-permute-start.26) | collective-permute-done | bytes 393248 | tf_op jit(solution)/shard_map/ppermute | solution.py:94
  246.5 6.5 %collective-permute-done.27.refs_5_ = bf16[512,384]{1,0:T(8,128)(2,1)} collective-permute-done((bf16[512,384]{1,0:T(8,128)(2,1)}, bf16[512,384]{1,0:T(8,128)(2,1)}, u32[]{:S(2)}, u32[]{:S(2)}) %collective-permute-start.27) | collective-permute-done | bytes 393248 | tf_op jit(solution)/shard_map/ppermute | solution.py:94
  255.2 6.6 %all-to-all-start.5 = ((bf16[48,8,1024]{2,1,0:T(8,128)(2,1)}), bf16[48,8,1024]{2,1,0:T(8,128)(2,1)S(1)}, u32[]{:S(2)}, u32[]{:S(2)}) async-start(bf16[48,8,1024]{2,1,0:T(8,128)(2,1)} %copy.85), calls=%async_computation.5 | async-start | bytes 1572864 | tf_op jit(solution)/shard_map/all_to_all | solution.py:377
  261.9 9.1 %output_side.1 = (bf16[384,1024]{1,0:T(8,128)(2,1)}, bf16[8,128,512]{2,1,0:T(8,128)(2,1)}) custom-call(s32[1]{0:T(128)} %bitcast.me_ref, bf16[512,384]{1,0:T(8,128)(2,1)} %get-tuple-element.167.refs_0_, bf16[512,384]{1,0:T(8,128)(2,1)} %copy-done.18, bf16[512,384]{1,0:T(8,128)(2,1)} %copy-done.19, bf16[512,384]{1,0:T(8,128)(2,1)} %copy-done.21, ...), custom_call_target="tpu_custom_call" | custom-call | tf_op jit(solution)/shard_map/output_side/pallas_call | solution.py:235
  271.0 8.2 %all-to-all-done.5 = bf16[48,8,1024]{2,1,0:T(8,128)(2,1)S(1)} async-done(((bf16[48,8,1024]{2,1,0:T(8,128)(2,1)}), bf16[48,8,1024]{2,1,0:T(8,128)(2,1)S(1)}, u32[]{:S(2)}, u32[]{:S(2)}) %all-to-all-start.5) | async-done | bytes 786464 | tf_op jit(solution)/shard_map/all_to_all | solution.py:377
  279.3 3.9 %all-to-all-start.6 = ((bf16[16,64,512]{2,1,0:T(8,128)(2,1)}), bf16[16,64,512]{2,1,0:T(8,128)(2,1)S(1)}, u32[]{:S(2)}, u32[]{:S(2)}) async-start(bf16[16,64,512]{2,1,0:T(8,128)(2,1)} %bitcast.88), calls=%async_computation.6 | async-start | bytes 2097152 | tf_op jit(solution)/shard_map/all_to_all | solution.py:31
  283.2 2.7 fusion.3
  290.1 3.2 collective-permute-start.30
  293.7 9.6 %all-to-all-done.6 = bf16[16,64,512]{2,1,0:T(8,128)(2,1)S(1)} async-done(((bf16[16,64,512]{2,1,0:T(8,128)(2,1)}), bf16[16,64,512]{2,1,0:T(8,128)(2,1)S(1)}, u32[]{:S(2)}, u32[]{:S(2)}) %all-to-all-start.6) | async-done | bytes 1048608 | tf_op jit(solution)/shard_map/all_to_all | solution.py:31
  304.5 4.2 %all-to-all-start.7 = ((bf16[16,64,512]{2,1,0:T(8,128)(2,1)}), bf16[16,64,512]{2,1,0:T(8,128)(2,1)S(1)}, u32[]{:S(2)}, u32[]{:S(2)}) async-start(bf16[16,64,512]{2,1,0:T(8,128)(2,1)} %broadcast_in_dim.16), calls=%async_computation.7 | async-start | bytes 2097152 | tf_op jit(solution)/shard_map/all_to_all | solution.py:41
  308.9 2.7 fusion
  313.2 11.4 %all-to-all-done.7 = bf16[16,64,512]{2,1,0:T(8,128)(2,1)S(1)} async-done(((bf16[16,64,512]{2,1,0:T(8,128)(2,1)}), bf16[16,64,512]{2,1,0:T(8,128)(2,1)S(1)}, u32[]{:S(2)}, u32[]{:S(2)}) %all-to-all-start.7) | async-done | bytes 1048608 | tf_op jit(solution)/shard_map/all_to_all | solution.py:41
  326.1 3.3 fusion.12
  329.5 2.8 fusion.13
  (145 shorter events, 42.2 us)
Async XLA Ops:
  7.2 40.1 %copy-start = (bf16[8,48,48]{2,1,0:T(8,128)(2,1)S(1)}, bf16[8,48,48]{2,1,0:T(8,128)(2,1)}, u32[]{:S(2)}) copy-start(bf16[8,48,48]{2,1,0:T(8,128)(2,1)} %param.12) | copy-start | bytes 110596
  16.5 25.6 %all-to-all-start = ((bf16[3,128,1024]{2,0,1:T(4,128)(2,1)}), bf16[3,128,1024]{2,0,1:T(4,128)(2,1)S(1)}, u32[]{:S(2)}, u32[]{:S(2)}) async-start(bf16[3,128,1024]{2,0,1:T(4,128)(2,1)} %copy.74), calls=%async_computation | async-start | bytes 2097152 | tf_op jit(solution)/shard_map/all_to_all | solution.py:331
  24.5 18.0 %collective-permute-start = (bf16[512,384]{1,0:T(8,128)(2,1)}, bf16[512,384]{1,0:T(8,128)(2,1)S(1)}, u32[]{:S(2)}, u32[]{:S(2)}) collective-permute-start(bf16[512,384]{1,0:T(8,128)(2,1)} %get-tuple-element.116), channel_id=1, source_target_pairs={{0,1},{1,0},{2,3},{3,2},{4,5},{5,4},{6,7},{7,6},{8,9},{9,8},{10,11... | collective-permute-start | bytes 1179656 | tf_op jit(solution)/shard_map/ppermute | solution.py:94
  24.5 18.0 %collective-permute-start.1 = (bf16[512,384]{1,0:T(8,128)(2,1)}, bf16[512,384]{1,0:T(8,128)(2,1)S(1)}, u32[]{:S(2)}, u32[]{:S(2)}) collective-permute-start(bf16[512,384]{1,0:T(8,128)(2,1)} %get-tuple-element.117), channel_id=1, source_target_pairs={{0,2},{1,3},{2,0},{3,1},{4,6},{5,7},{6,4},{7,5},{8,10},{9,11},{10,... | collective-permute-start | bytes 1179656 | tf_op jit(solution)/shard_map/ppermute | solution.py:94
  26.2 18.0 %collective-permute-start.2 = (bf16[512,384]{1,0:T(8,128)(2,1)}, bf16[512,384]{1,0:T(8,128)(2,1)S(1)}, u32[]{:S(2)}, u32[]{:S(2)}) collective-permute-start(bf16[512,384]{1,0:T(8,128)(2,1)} %get-tuple-element.118), channel_id=1, source_target_pairs={{0,3},{1,2},{2,1},{3,0},{4,7},{5,6},{6,5},{7,4},{8,11},{9,10},{10,... | collective-permute-start | bytes 1179656 | tf_op jit(solution)/shard_map/ppermute | solution.py:94
  26.4 17.8 %collective-permute-start.3 = (bf16[512,384]{1,0:T(8,128)(2,1)}, bf16[512,384]{1,0:T(8,128)(2,1)}, u32[]{:S(2)}, u32[]{:S(2)}) collective-permute-start(bf16[512,384]{1,0:T(8,128)(2,1)} %get-tuple-element.119), channel_id=1, source_target_pairs={{0,6},{1,7},{2,4},{3,5},{4,2},{5,3},{6,0},{7,1},{8,14},{9,15},{10,... | collective-permute-start | bytes 1179656 | tf_op jit(solution)/shard_map/ppermute | solution.py:94
  29.4 17.9 %collective-permute-start.4 = (bf16[512,384]{1,0:T(8,128)(2,1)}, bf16[512,384]{1,0:T(8,128)(2,1)}, u32[]{:S(2)}, u32[]{:S(2)}) collective-permute-start(bf16[512,384]{1,0:T(8,128)(2,1)} %get-tuple-element.120), channel_id=1, source_target_pairs={{0,7},{1,6},{2,5},{3,4},{4,3},{5,2},{6,1},{7,0},{8,15},{9,14},{10,... | collective-permute-start | bytes 1179656 | tf_op jit(solution)/shard_map/ppermute | solution.py:94
  49.8 22.0 %all-to-all-start.1 = ((bf16[48,8,1024]{2,1,0:T(8,128)(2,1)}), bf16[48,8,1024]{2,1,0:T(8,128)(2,1)S(1)}, u32[]{:S(2)}, u32[]{:S(2)}) async-start(bf16[48,8,1024]{2,1,0:T(8,128)(2,1)} %copy.78), calls=%async_computation.1 | async-start | bytes 1572864 | tf_op jit(solution)/shard_map/all_to_all | solution.py:335
  56.9 14.9 %collective-permute-start.5 = (bf16[512,384]{1,0:T(8,128)(2,1)}, bf16[512,384]{1,0:T(8,128)(2,1)S(1)}, u32[]{:S(2)}, u32[]{:S(2)}) collective-permute-start(bf16[512,384]{1,0:T(8,128)(2,1)} %get-tuple-element.122), channel_id=1, source_target_pairs={{0,4},{1,5},{2,6},{3,7},{4,0},{5,1},{6,2},{7,3},{8,12},{9,13},{10,... | collective-permute-start | bytes 1179656 | tf_op jit(solution)/shard_map/ppermute | solution.py:94
  58.9 18.4 %collective-permute-start.6 = (bf16[512,384]{1,0:T(8,128)(2,1)}, bf16[512,384]{1,0:T(8,128)(2,1)S(1)}, u32[]{:S(2)}, u32[]{:S(2)}) collective-permute-start(bf16[512,384]{1,0:T(8,128)(2,1)} %get-tuple-element.123), channel_id=1, source_target_pairs={{0,5},{1,4},{2,7},{3,6},{4,1},{5,0},{6,3},{7,2},{8,13},{9,12},{10,... | collective-permute-start | bytes 1179656 | tf_op jit(solution)/shard_map/ppermute | solution.py:94
  84.2 13.9 %collective-permute-start.10 = (bf16[512,384]{1,0:T(8,128)(2,1)}, bf16[512,384]{1,0:T(8,128)(2,1)S(1)}, u32[]{:S(2)}, u32[]{:S(2)}) collective-permute-start(bf16[512,384]{1,0:T(8,128)(2,1)} %get-tuple-element.129), channel_id=1, source_target_pairs={{0,4},{1,5},{2,6},{3,7},{4,0},{5,1},{6,2},{7,3},{8,12},{9,13},{10,... | collective-permute-start | bytes 1179656 | tf_op jit(solution)/shard_map/ppermute | solution.py:94
  86.3 19.9 %collective-permute-start.11 = (bf16[512,384]{1,0:T(8,128)(2,1)}, bf16[512,384]{1,0:T(8,128)(2,1)}, u32[]{:S(2)}, u32[]{:S(2)}) collective-permute-start(bf16[512,384]{1,0:T(8,128)(2,1)} %get-tuple-element.130), channel_id=1, source_target_pairs={{0,5},{1,4},{2,7},{3,6},{4,1},{5,0},{6,3},{7,2},{8,13},{9,12},{10,... | collective-permute-start | bytes 1179656 | tf_op jit(solution)/shard_map/ppermute | solution.py:94
  87.9 26.9 %collective-permute-start.12 = (bf16[512,384]{1,0:T(8,128)(2,1)}, bf16[512,384]{1,0:T(8,128)(2,1)}, u32[]{:S(2)}, u32[]{:S(2)}) collective-permute-start(bf16[512,384]{1,0:T(8,128)(2,1)} %get-tuple-element.131), channel_id=1, source_target_pairs={{0,6},{1,7},{2,4},{3,5},{4,2},{5,3},{6,0},{7,1},{8,14},{9,15},{10,... | collective-permute-start | bytes 1179656 | tf_op jit(solution)/shard_map/ppermute | solution.py:94
  90.9 32.2 %collective-permute-start.13 = (bf16[512,384]{1,0:T(8,128)(2,1)}, bf16[512,384]{1,0:T(8,128)(2,1)}, u32[]{:S(2)}, u32[]{:S(2)}) collective-permute-start(bf16[512,384]{1,0:T(8,128)(2,1)} %get-tuple-element.132), channel_id=1, source_target_pairs={{0,7},{1,6},{2,5},{3,4},{4,3},{5,2},{6,1},{7,0},{8,15},{9,14},{10,... | collective-permute-start | bytes 1179656 | tf_op jit(solution)/shard_map/ppermute | solution.py:94
  90.9 32.2 %collective-permute-start.7 = (bf16[512,384]{1,0:T(8,128)(2,1)}, bf16[512,384]{1,0:T(8,128)(2,1)}, u32[]{:S(2)}, u32[]{:S(2)}) collective-permute-start(bf16[512,384]{1,0:T(8,128)(2,1)} %get-tuple-element.126), channel_id=1, source_target_pairs={{0,1},{1,0},{2,3},{3,2},{4,5},{5,4},{6,7},{7,6},{8,9},{9,8},{10,11... | collective-permute-start | bytes 1179656 | tf_op jit(solution)/shard_map/ppermute | solution.py:94
  98.1 25.0 %collective-permute-start.8 = (bf16[512,384]{1,0:T(8,128)(2,1)}, bf16[512,384]{1,0:T(8,128)(2,1)}, u32[]{:S(2)}, u32[]{:S(2)}) collective-permute-start(bf16[512,384]{1,0:T(8,128)(2,1)} %get-tuple-element.127), channel_id=1, source_target_pairs={{0,2},{1,3},{2,0},{3,1},{4,6},{5,7},{6,4},{7,5},{8,10},{9,11},{10,... | collective-permute-start | bytes 1179656 | tf_op jit(solution)/shard_map/ppermute | solution.py:94
  106.2 17.0 %collective-permute-start.9 = (bf16[512,384]{1,0:T(8,128)(2,1)}, bf16[512,384]{1,0:T(8,128)(2,1)}, u32[]{:S(2)}, u32[]{:S(2)}) collective-permute-start(bf16[512,384]{1,0:T(8,128)(2,1)} %get-tuple-element.128), channel_id=1, source_target_pairs={{0,3},{1,2},{2,1},{3,0},{4,7},{5,6},{6,5},{7,4},{8,11},{9,10},{10,... | collective-permute-start | bytes 1179656 | tf_op jit(solution)/shard_map/ppermute | solution.py:94
  140.2 16.4 %collective-permute-start.14 = (bf16[512,384]{1,0:T(8,128)(2,1)}, bf16[512,384]{1,0:T(8,128)(2,1)S(1)}, u32[]{:S(2)}, u32[]{:S(2)}) collective-permute-start(bf16[512,384]{1,0:T(8,128)(2,1)} %get-tuple-element.155), channel_id=1, source_target_pairs={{0,1},{1,0},{2,3},{3,2},{4,5},{5,4},{6,7},{7,6},{8,9},{9,8},{10,11... | collective-permute-start | bytes 1179656 | tf_op jit(solution)/shard_map/ppermute | solution.py:94
  140.4 16.2 %collective-permute-start.15 = (bf16[512,384]{1,0:T(8,128)(2,1)}, bf16[512,384]{1,0:T(8,128)(2,1)S(1)}, u32[]{:S(2)}, u32[]{:S(2)}) collective-permute-start(bf16[512,384]{1,0:T(8,128)(2,1)} %get-tuple-element.156), channel_id=1, source_target_pairs={{0,2},{1,3},{2,0},{3,1},{4,6},{5,7},{6,4},{7,5},{8,10},{9,11},{10,... | collective-permute-start | bytes 1179656 | tf_op jit(solution)/shard_map/ppermute | solution.py:94
  141.0 18.8 %collective-permute-start.16 = (bf16[512,384]{1,0:T(8,128)(2,1)}, bf16[512,384]{1,0:T(8,128)(2,1)S(1)}, u32[]{:S(2)}, u32[]{:S(2)}) collective-permute-start(bf16[512,384]{1,0:T(8,128)(2,1)} %get-tuple-element.157), channel_id=1, source_target_pairs={{0,3},{1,2},{2,1},{3,0},{4,7},{5,6},{6,5},{7,4},{8,11},{9,10},{10,... | collective-permute-start | bytes 1179656 | tf_op jit(solution)/shard_map/ppermute | solution.py:94
  142.1 17.7 %collective-permute-start.17 = (bf16[512,384]{1,0:T(8,128)(2,1)}, bf16[512,384]{1,0:T(8,128)(2,1)S(1)}, u32[]{:S(2)}, u32[]{:S(2)}) collective-permute-start(bf16[512,384]{1,0:T(8,128)(2,1)} %get-tuple-element.158), channel_id=1, source_target_pairs={{0,6},{1,7},{2,4},{3,5},{4,2},{5,3},{6,0},{7,1},{8,14},{9,15},{10,... | collective-permute-start | bytes 1179656 | tf_op jit(solution)/shard_map/ppermute | solution.py:94
  145.2 18.0 %collective-permute-start.18 = (bf16[512,384]{1,0:T(8,128)(2,1)}, bf16[512,384]{1,0:T(8,128)(2,1)}, u32[]{:S(2)}, u32[]{:S(2)}) collective-permute-start(bf16[512,384]{1,0:T(8,128)(2,1)} %get-tuple-element.159), channel_id=1, source_target_pairs={{0,7},{1,6},{2,5},{3,4},{4,3},{5,2},{6,1},{7,0},{8,15},{9,14},{10,... | collective-permute-start | bytes 1179656 | tf_op jit(solution)/shard_map/ppermute | solution.py:94
  156.6 34.0 %copy-start.22 = (bf16[512,384]{1,0:T(8,128)(2,1)}, bf16[512,384]{1,0:T(8,128)(2,1)S(1)}, u32[]{:S(2)}) copy-start(bf16[512,384]{1,0:T(8,128)(2,1)S(1)} %collective-permute-done.14.refs_1_) | copy-start | bytes 1179652
  156.6 34.7 %copy-start.24 = (bf16[512,384]{1,0:T(8,128)(2,1)}, bf16[512,384]{1,0:T(8,128)(2,1)S(1)}, u32[]{:S(2)}) copy-start(bf16[512,384]{1,0:T(8,128)(2,1)S(1)} %collective-permute-done.15.refs_2_) | copy-start | bytes 1179652
  159.8 30.7 %copy-start.25 = (bf16[512,384]{1,0:T(8,128)(2,1)}, bf16[512,384]{1,0:T(8,128)(2,1)S(1)}, u32[]{:S(2)}) copy-start(bf16[512,384]{1,0:T(8,128)(2,1)S(1)} %collective-permute-done.16.refs_3_) | copy-start | bytes 1179652
  159.8 30.7 %copy-start.26 = (bf16[512,384]{1,0:T(8,128)(2,1)}, bf16[512,384]{1,0:T(8,128)(2,1)S(1)}, u32[]{:S(2)}) copy-start(bf16[512,384]{1,0:T(8,128)(2,1)S(1)} %collective-permute-done.17.refs_6_) | copy-start | bytes 1179652
  163.2 40.8 %all-to-all-start.2 = ((bf16[16,256,128]{2,1,0:T(8,128)(2,1)}), bf16[16,256,128]{2,1,0:T(8,128)(2,1)S(1)}, u32[]{:S(2)}, u32[]{:S(2)}) async-start(bf16[16,256,128]{2,1,0:T(8,128)(2,1)} %bitcast.87), calls=%async_computation.2 | async-start | bytes 2097152 | tf_op jit(solution)/shard_map/all_to_all | solution.py:31
  170.1 13.8 %collective-permute-start.19 = (bf16[512,384]{1,0:T(8,128)(2,1)}, bf16[512,384]{1,0:T(8,128)(2,1)S(1)}, u32[]{:S(2)}, u32[]{:S(2)}) collective-permute-start(bf16[512,384]{1,0:T(8,128)(2,1)} %get-tuple-element.163), channel_id=1, source_target_pairs={{0,4},{1,5},{2,6},{3,7},{4,0},{5,1},{6,2},{7,3},{8,12},{9,13},{10,... | collective-permute-start | bytes 1179656 | tf_op jit(solution)/shard_map/ppermute | solution.py:94
  171.0 19.5 %collective-permute-start.20 = (bf16[512,384]{1,0:T(8,128)(2,1)}, bf16[512,384]{1,0:T(8,128)(2,1)S(1)}, u32[]{:S(2)}, u32[]{:S(2)}) collective-permute-start(bf16[512,384]{1,0:T(8,128)(2,1)} %get-tuple-element.164), channel_id=1, source_target_pairs={{0,5},{1,4},{2,7},{3,6},{4,1},{5,0},{6,3},{7,2},{8,13},{9,12},{10,... | collective-permute-start | bytes 1179656 | tf_op jit(solution)/shard_map/ppermute | solution.py:94
  190.6 13.1 %collective-permute-start.21 = (bf16[512,384]{1,0:T(8,128)(2,1)}, bf16[512,384]{1,0:T(8,128)(2,1)S(1)}, u32[]{:S(2)}, u32[]{:S(2)}) collective-permute-start(bf16[512,384]{1,0:T(8,128)(2,1)} %get-tuple-element.178), channel_id=1, source_target_pairs={{0,1},{1,0},{2,3},{3,2},{4,5},{5,4},{6,7},{7,6},{8,9},{9,8},{10,11... | collective-permute-start | bytes 1179656 | tf_op jit(solution)/shard_map/ppermute | solution.py:94
  191.3 12.4 %collective-permute-start.22 = (bf16[512,384]{1,0:T(8,128)(2,1)}, bf16[512,384]{1,0:T(8,128)(2,1)S(1)}, u32[]{:S(2)}, u32[]{:S(2)}) collective-permute-start(bf16[512,384]{1,0:T(8,128)(2,1)} %get-tuple-element.179), channel_id=1, source_target_pairs={{0,2},{1,3},{2,0},{3,1},{4,6},{5,7},{6,4},{7,5},{8,10},{9,11},{10,... | collective-permute-start | bytes 1179656 | tf_op jit(solution)/shard_map/ppermute | solution.py:94
  191.7 12.3 %collective-permute-start.23 = (bf16[512,384]{1,0:T(8,128)(2,1)}, bf16[512,384]{1,0:T(8,128)(2,1)S(1)}, u32[]{:S(2)}, u32[]{:S(2)}) collective-permute-start(bf16[512,384]{1,0:T(8,128)(2,1)} %get-tuple-element.180), channel_id=1, source_target_pairs={{0,6},{1,7},{2,4},{3,5},{4,2},{5,3},{6,0},{7,1},{8,14},{9,15},{10,... | collective-permute-start | bytes 1179656 | tf_op jit(solution)/shard_map/ppermute | solution.py:94
  203.7 31.7 %copy-start.18 = (bf16[512,384]{1,0:T(8,128)(2,1)}, bf16[512,384]{1,0:T(8,128)(2,1)S(1)}, u32[]{:S(2)}) copy-start(bf16[512,384]{1,0:T(8,128)(2,1)S(1)} %collective-permute-done.21.refs_1_) | copy-start | bytes 1179652
  204.8 21.3 %all-to-all-start.3 = ((bf16[16,24,1024]{2,1,0:T(8,128)(2,1)}), bf16[16,24,1024]{2,1,0:T(8,128)(2,1)S(1)}, u32[]{:S(2)}, u32[]{:S(2)}) async-start(bf16[16,24,1024]{2,1,0:T(8,128)(2,1)} %get-tuple-element.184), calls=%async_computation.3 | async-start | bytes 1572864 | tf_op jit(solution)/shard_map/all_to_all | solution.py:369
  211.6 11.6 %collective-permute-start.24 = (bf16[512,384]{1,0:T(8,128)(2,1)}, bf16[512,384]{1,0:T(8,128)(2,1)S(1)}, u32[]{:S(2)}, u32[]{:S(2)}) collective-permute-start(bf16[512,384]{1,0:T(8,128)(2,1)} %get-tuple-element.185), channel_id=1, source_target_pairs={{0,3},{1,2},{2,1},{3,0},{4,7},{5,6},{6,5},{7,4},{8,11},{9,10},{10,... | collective-permute-start | bytes 1179656 | tf_op jit(solution)/shard_map/ppermute | solution.py:94
  211.9 12.1 %collective-permute-start.25 = (bf16[512,384]{1,0:T(8,128)(2,1)}, bf16[512,384]{1,0:T(8,128)(2,1)}, u32[]{:S(2)}, u32[]{:S(2)}) collective-permute-start(bf16[512,384]{1,0:T(8,128)(2,1)} %get-tuple-element.186), channel_id=1, source_target_pairs={{0,7},{1,6},{2,5},{3,4},{4,3},{5,2},{6,1},{7,0},{8,15},{9,14},{10,... | collective-permute-start | bytes 1179656 | tf_op jit(solution)/shard_map/ppermute | solution.py:94
  227.0 26.1 %all-to-all-start.4 = ((bf16[16,264,128]{2,1,0:T(8,128)(2,1)}), bf16[16,264,128]{2,1,0:T(8,128)(2,1)S(1)}, u32[]{:S(2)}, u32[]{:S(2)}) async-start(bf16[16,264,128]{2,1,0:T(8,128)(2,1)} %get-tuple-element.190), calls=%async_computation.4 | async-start | bytes 2162688 | tf_op jit(solution)/shard_map/all_to_all | solution.py:31
  232.0 94.2 %all-gather.2.cloned.1.call-start = ((), (), s32[]{:S(2)}) async-start(), calls=%async_computation.8 | async-start | bytes 2263040 | tf_op jit(solution)/shard_map/all_gather | solution.py:386
  232.0 13.7 %collective-permute-start.26 = (bf16[512,384]{1,0:T(8,128)(2,1)}, bf16[512,384]{1,0:T(8,128)(2,1)S(1)}, u32[]{:S(2)}, u32[]{:S(2)}) collective-permute-start(bf16[512,384]{1,0:T(8,128)(2,1)} %get-tuple-element.191), channel_id=1, source_target_pairs={{0,4},{1,5},{2,6},{3,7},{4,0},{5,1},{6,2},{7,3},{8,12},{9,13},{10,... | collective-permute-start | bytes 1179656 | tf_op jit(solution)/shard_map/ppermute | solution.py:94
  234.7 18.3 %collective-permute-start.27 = (bf16[512,384]{1,0:T(8,128)(2,1)}, bf16[512,384]{1,0:T(8,128)(2,1)}, u32[]{:S(2)}, u32[]{:S(2)}) collective-permute-start(bf16[512,384]{1,0:T(8,128)(2,1)} %get-tuple-element.192), channel_id=1, source_target_pairs={{0,5},{1,4},{2,7},{3,6},{4,1},{5,0},{6,3},{7,2},{8,13},{9,12},{10,... | collective-permute-start | bytes 1179656 | tf_op jit(solution)/shard_map/ppermute | solution.py:94
  255.2 24.0 %all-to-all-start.5 = ((bf16[48,8,1024]{2,1,0:T(8,128)(2,1)}), bf16[48,8,1024]{2,1,0:T(8,128)(2,1)S(1)}, u32[]{:S(2)}, u32[]{:S(2)}) async-start(bf16[48,8,1024]{2,1,0:T(8,128)(2,1)} %copy.85), calls=%async_computation.5 | async-start | bytes 1572864 | tf_op jit(solution)/shard_map/all_to_all | solution.py:377
  279.3 23.9 %all-to-all-start.6 = ((bf16[16,64,512]{2,1,0:T(8,128)(2,1)}), bf16[16,64,512]{2,1,0:T(8,128)(2,1)S(1)}, u32[]{:S(2)}, u32[]{:S(2)}) async-start(bf16[16,64,512]{2,1,0:T(8,128)(2,1)} %bitcast.88), calls=%async_computation.6 | async-start | bytes 2097152 | tf_op jit(solution)/shard_map/all_to_all | solution.py:31
  287.5 1.4 collective-permute-start.28
  288.9 19.8 %collective-permute-start.29 = (f32[264,128]{1,0:T(8,128)S(1)}, f32[264,128]{1,0:T(8,128)S(1)}, u32[]{:S(2)}, u32[]{:S(2)}) collective-permute-start(f32[264,128]{1,0:T(8,128)S(1)} %bitcast_add_fusion.1), channel_id=1, source_target_pairs={{0,2},{1,3},{2,0},{3,1},{4,6},{5,7},{6,4},{7,5},{8,10},{9,11},{10,... | collective-permute-start | bytes 405512 | tf_op jit(solution)/shard_map/ppermute | solution.py:55
  290.1 18.6 %collective-permute-start.30 = (f32[264,128]{1,0:T(8,128)S(1)}, f32[264,128]{1,0:T(8,128)S(1)}, u32[]{:S(2)}, u32[]{:S(2)}) collective-permute-start(f32[264,128]{1,0:T(8,128)S(1)} %bitcast_add_fusion.1), channel_id=1, source_target_pairs={{0,4},{1,5},{2,6},{3,7},{4,0},{5,1},{6,2},{7,3},{8,12},{9,13},{10,... | collective-permute-start | bytes 405512 | tf_op jit(solution)/shard_map/ppermute | solution.py:55
  293.4 15.4 %collective-permute-start.31 = (f32[264,128]{1,0:T(8,128)S(1)}, f32[264,128]{1,0:T(8,128)S(1)}, u32[]{:S(2)}, u32[]{:S(2)}) collective-permute-start(f32[264,128]{1,0:T(8,128)S(1)} %bitcast_add_fusion.1), channel_id=1, source_target_pairs={{0,6},{1,7},{2,4},{3,5},{4,2},{5,3},{6,0},{7,1},{8,14},{9,15},{10,... | collective-permute-start | bytes 405512 | tf_op jit(solution)/shard_map/ppermute | solution.py:55
  304.5 20.0 %all-to-all-start.7 = ((bf16[16,64,512]{2,1,0:T(8,128)(2,1)}), bf16[16,64,512]{2,1,0:T(8,128)(2,1)S(1)}, u32[]{:S(2)}, u32[]{:S(2)}) async-start(bf16[16,64,512]{2,1,0:T(8,128)(2,1)} %broadcast_in_dim.16), calls=%async_computation.7 | async-start | bytes 2097152 | tf_op jit(solution)/shard_map/all_to_all | solution.py:41
  308.8 2.8 collective-permute-start.32
  (24 other events, 215.8 us)
Sparse Core Ops, SparseCore 0:
  254.0 55.6 all-gather.1
